TPU v7x, 32 devices: a whole 2x2x4 slice. The times are simulated.
32 devices in a mesh: expert: 8 (over y, x, core), tensor: 4 (over z).
Axes of the slice: x: 2, y: 2, z: 4, core: 2. Of those that a mesh axis runs over, the one named last changes fastest.
Arguments:
- tokens: bfloat16 [4096, 2560], P(('expert', 'tensor')), may hold values from -6 to 6
- expert_ids: int32 [4096, 1], P(('expert', 'tensor')), may hold values from 0 to 7; in each aligned block of 512 rows (0 to 511, 512 to 1023, ...) at most 128 rows name the same one
- gates: float32 [4096], P(('expert', 'tensor')), may hold values from 0.3 to 3
- w_gate: bfloat16 [8, 2560, 4096], P('expert', None, 'tensor'), may hold values from -0.125 to 0.125
- w_up: bfloat16 [8, 2560, 4096], P('expert', None, 'tensor'), may hold values from -0.125 to 0.125
- w_down: bfloat16 [8, 4096, 2560], P('expert', 'tensor'), may hold values from -0.09375 to 0.09375
- s_gate: bfloat16 [2560, 4096], P('expert', 'tensor'), may hold values from -0.125 to 0.125
- s_up: bfloat16 [2560, 4096], P('expert', 'tensor'), may hold values from -0.125 to 0.125
- s_down: bfloat16 [4096, 2560], P('tensor', 'expert'), may hold values from -0.09375 to 0.09375
Outputs:
- mixed: bfloat16 [4096, 2560], P(('expert', 'tensor'))
Inputs may be any that keep to these rules, and one draw needn't show every extreme that they name: `expert_ids`: in each aligned block of 512 tokens no expert is named by more than 128 tokens, and some block has an expert named by exactly 128 tokens.
All inputs are finite; a program needn't handle non-finite values.
Results may differ from a plain program's by a relative error of at most 0.013.
Values may be sent and summed in bfloat16 or wider, within the bound.
No kernel may reach another device: no remote copies, remote signals or barrier semaphores. Data moves between devices by JAX's collectives and lax.ppermute only.
A program may use at most 128 MiB of HBM per device.

v0:
```python
import functools

import jax
import jax.numpy as jnp
from jax import lax
from jax.experimental import pallas as pl
from jax.experimental.pallas import tpu as pltpu
from jax.sharding import PartitionSpec as P


F32 = jnp.float32
BF16 = jnp.bfloat16
LANES = 128
VMEM_BYTES = 56 * 1024 * 1024
VMEM_SPEC = pl.BlockSpec(memory_space=pltpu.VMEM)
ANY_SPEC = pl.BlockSpec(memory_space=pl.ANY)


def dot(a, b):
    return jnp.dot(a, b, preferred_element_type=F32)


def dot_t(a, b):
    return lax.dot_general(a, b, (((1,), (1,)), ((), ())), preferred_element_type=F32)


def add(block, *others):
    out = block.astype(F32)
    for other in others:
        out = out + other.astype(F32)
    return out.astype(BF16)


def swap(block, axis, bits):
    size = lax.axis_size(axis)
    return lax.ppermute(block, axis, [(i, i ^ bits) for i in range(size)])


def hop(block, step, sources):
    return lax.ppermute(block, "tensor", [(i, i + step) for i in sources])


def bits_of(number):
    return [1 << b for b in range(number.bit_length()) if number >> b & 1]


def far(offset):
    return len(bits_of(offset >> 1)) > 1


def line_gather(block, count, direct):
    ups, downs = [], []
    for back in range(1, count):
        if back <= direct:
            ups.append(hop(block, back, range(count - back)))
            downs.append(hop(block, -back, range(back, count)))
        else:
            ups.append(hop(ups[-1], 1, range(back - 1, count - 1)))
            downs.append(hop(downs[-1], -1, range(1, count - back + 1)))
    return ups, downs


def line_scatter(part, count):
    up = down = None
    got = []
    for back in range(count - 1, 0, -1):
        first, second = part[count - back], part[back]
        if up is not None:
            first, second = add(first, up), add(second, down)
            up = down = None
        if back < 3:
            got.append(hop(first, back, range(count - back)))
            got.append(hop(second, -back, range(back, count)))
        else:
            up = hop(first, 1, range(count - back))
            down = hop(second, -1, range(back, count))
    return add(part[0], *got)


def with_partner(held):
    return {**held, **{o + 1: swap(b, "expert", 1) for o, b in held.items()}}


def far_blocks(near, block, size):
    half = block.shape[1] // 2
    held = {0: block, **near}
    for offset in range(2, size, 2):
        if offset not in held:
            low, high = bits_of(offset)[0], bits_of(offset)[-1]
            held[offset] = jnp.concatenate(
                [
                    swap(held[offset ^ low][:, :half], "expert", low),
                    swap(held[offset ^ high][:, half:], "expert", high),
                ],
                axis=1,
            )
    return {o: b for o, b in held.items() if far(o)}


def in_order(held, me):
    rows, columns = held[0].shape
    out = jnp.zeros((rows * len(held), columns), held[0].dtype)
    for offset, block in held.items():
        out = lax.dynamic_update_slice(out, block, ((me ^ offset) * rows, 0))
    return out


def tiles_of(width):
    for tile in (512, 256, LANES):
        if width % tile == 0:
            return width // tile
    return 1


def each(count, step):
    @pl.loop(0, count)
    def _(n):
        step(n)


def cut(n, tile):
    return pl.ds(pl.multiple_of(n * tile, tile), tile)


def stack(refs, x, sem):
    copies, at = [], 0
    for k, ref in enumerate(refs):
        rows = ref.shape[0]
        copies.append(pltpu.make_async_copy(ref, x.at[pl.ds(at, rows), :], sem.at[k]))
        at += rows
    for copy in copies:
        copy.start()

    def wait():
        for copy in copies:
            copy.wait()

    return wait


def columns_in(source, target, tiles, sem):
    tile = target.shape[-1] // tiles

    def copy(n):
        at = cut(n, tile)
        return pltpu.make_async_copy(source.at[:, at], target.at[:, at], sem.at[n])

    each(tiles, lambda n: copy(n).start())
    return lambda n: copy(n).wait()


def rows_out(source, targets, tiles, sem):
    tile = source.shape[-1] // tiles

    def copies(n):
        at, start = cut(n, tile), 0
        for k, target in enumerate(targets):
            rows = target.shape[0]
            yield pltpu.make_async_copy(
                source.at[pl.ds(start, rows), at], target.at[:, at], sem.at[k, n]
            )
            start += rows

    def begin(n):
        for copy in copies(n):
            copy.start()

    def finish(n):
        for copy in copies(n):
            copy.wait()

    return begin, lambda: each(tiles, finish)


def take(refs, *counts):
    out, at = [], 0
    for count in counts:
        out.append(refs[at] if count is None else refs[at:at + count])
        at += 1 if count is None else count
    return out + list(refs[at:])


def pick_kernel(count, lengths, *refs):
    own, ups, downs, slot, outs, group, x, pick, made, sem_in, sem_out, sem_group = take(
        refs, None, count - 1, count - 1, None, len(lengths), None
    )
    place = lax.axis_index("tensor")
    rows = own.shape[0]
    width = x.shape[1]
    tiles = tiles_of(width)

    def into(ref, k):
        return pltpu.make_async_copy(ref, x.at[pl.ds(k * rows, rows), :], sem_in.at[k])

    into(own, 0).start()
    for k in range(1, count):
        @pl.when(place >= k)
        def _():
            into(ups[k - 1], k).start()

        @pl.when(place < k)
        def _():
            into(downs[count - k - 1], k).start()

    places = lax.broadcasted_iota(jnp.int32, pick.shape, 0)
    pick[...] = (places == slot[...]).astype(F32).astype(BF16)
    for k in range(count):
        into(own, k).wait()
    whole = pltpu.make_async_copy(x, group, sem_group)
    whole.start()
    begin, finish = rows_out(made, outs, tiles, sem_out)

    def step(n):
        at = cut(n, width // tiles)
        made[:, at] = dot(pick[...], x[:, at]).astype(BF16)
        begin(n)

    each(tiles, step)
    finish()
    whole.wait()


def expert_kernel(count, *refs):
    blocks, gate_w, up_w, down_w, outs, x, gate, upper, down, hidden, made, *sems = take(
        refs, count, None, None, None, count
    )
    inner, outer = down.shape
    ins, os = tiles_of(inner // 2), tiles_of(outer)
    wait_x = stack(blocks, x, sems[0])
    wait_gate = columns_in(gate_w.at[0], gate, ins, sems[1])
    wait_up = columns_in(up_w.at[0], upper, ins, sems[2])
    wait_down = columns_in(down_w.at[0], down, os, sems[3])
    wait_x()

    def one(n):
        at = cut(n, inner // ins)
        wait_gate(n)
        g = dot(x[...], gate[:, at])
        wait_up(n)
        hidden[:, at] = (jax.nn.silu(g) * dot(x[...], upper[:, at])).astype(BF16)

    each(ins, one)
    begin, finish = rows_out(made, outs, os, sems[4])

    def two(n):
        at = cut(n, outer // os)
        wait_down(n)
        made[:, at] = dot(hidden[...], down[:, at]).astype(BF16)
        begin(n)

    each(os, two)
    finish()


def load_pairs(refs, offsets, start, width, held, sem, core):
    rows = refs[0].shape[0]
    copies = []
    for k, (ref, offset) in enumerate(zip(refs, offsets)):
        at = pl.multiple_of((core ^ (offset & 1)) * rows, rows)
        copies.append(
            pltpu.make_async_copy(
                ref.at[:, pl.ds(start, width)], held.at[k // 2, pl.ds(at, rows), :], sem.at[k]
            )
        )
    for copy in copies:
        copy.start()
    return copies


def columns_of(offset, width):
    pair = lax.axis_index("expert") // 2
    return pl.ds(pl.multiple_of((pair ^ (offset // 2)) * width, LANES), width)


def near_kernel(offsets, inner, *refs):
    group, blocks, out, x, held, made, *sems = take(refs, None, len(offsets))
    core = lax.axis_index("expert") & 1
    whole = pltpu.make_async_copy(group, x, sems[0])
    whole.start()
    copies = load_pairs(blocks, offsets, 0, 2 * inner, held, sems[1], core)
    whole.wait()
    for copy in copies:
        copy.wait()
    pair = held.shape[1]
    tiles = tiles_of(2 * inner)
    begin, finish = rows_out(made, [out], tiles, sems[2])

    def step(n):
        at = cut(n, 2 * inner // tiles)
        total = None
        for k in range(len(offsets) // 2):
            term = dot(x[:, columns_of(offsets[2 * k], pair)], held[k, :, at])
            total = term if total is None else total + term
        made[:, at] = total
        begin(n)

    each(tiles, step)
    finish()


def far_kernel(offsets, late, inner, *refs):
    source, group, blocks, out, x, part, held, down, hidden, made, *sems = take(
        refs, None, None, len(offsets)
    )
    core = lax.axis_index("expert") & 1
    whole = pltpu.make_async_copy(group, x, sems[0])
    whole.start()
    copies = load_pairs(
        [blocks[offsets.index(o)] for o in late], late, 0, 2 * inner, held, sems[1], core
    )
    tiles = tiles_of(inner // 2)
    tile = inner // tiles
    wait_part = columns_in(source, part, 2 * tiles, sems[2])
    later = load_pairs(blocks, offsets, 2 * inner, inner, down, sems[3], core)
    whole.wait()
    for copy in copies:
        copy.wait()
    pair = held.shape[1]

    def step(n):
        sums = []
        for base in (0, tiles):
            at = cut(base + n, tile)
            wait_part(base + n)
            total = part[:, at]
            for k in range(len(late) // 2):
                total = total + dot(x[:, columns_of(late[2 * k], pair)], held[k, :, at])
            sums.append(total)
        hidden[:, cut(n, tile)] = (jax.nn.silu(sums[0]) * sums[1]).astype(BF16)

    each(tiles, step)
    for copy in later:
        copy.wait()
    outs = []
    for k in range(len(offsets) // 2):
        at = columns_of(offsets[2 * k], pair)
        made[:, at] = dot_t(hidden[...], down[k])
        outs.append(pltpu.make_async_copy(made.at[:, at], out.at[:, at], sems[4].at[k]))
        outs[-1].start()
    for copy in outs:
        copy.wait()


def combine_kernel(count, parts, *refs):
    blocks, notes, source, outs, x, shared, made, *sems = take(refs, count, None, None, parts)
    wait_x = stack(blocks, x, sems[0])
    total, width = x.shape
    tiles = tiles_of(width)
    wait_shared = columns_in(source, shared, tiles, sems[1])
    rows = notes.shape[0]
    places = lax.broadcasted_iota(jnp.int32, (rows, total), 1)
    pick = (places == notes[:, 0:1].astype(jnp.int32)).astype(F32).astype(BF16)
    scale = notes[:, 1:2]
    wait_x()
    begin, finish = rows_out(made, outs, tiles, sems[2])

    def step(n):
        at = cut(n, width // tiles)
        routed = dot(pick, x[:, at])
        wait_shared(n)
        made[:, at] = (shared[:, at] + scale * routed).astype(BF16)
        begin(n)

    each(tiles, step)
    finish()


def call(kernel, ins, vmem, outs, scratch, flops, moved):
    return pl.pallas_call(
        kernel,
        out_shape=[jax.ShapeDtypeStruct(shape, kind) for shape, kind in outs],
        in_specs=[VMEM_SPEC if k in vmem else ANY_SPEC for k in range(len(ins))],
        out_specs=[ANY_SPEC] * len(outs),
        scratch_shapes=scratch,
        compiler_params=pltpu.CompilerParams(vmem_limit_bytes=VMEM_BYTES),
        cost_estimate=pl.CostEstimate(flops=flops, bytes_accessed=moved, transcendentals=0),
    )(*ins)


def dma(*shape):
    return pltpu.SemaphoreType.DMA(shape)


def pick_rows(own, ups, downs, slot, lengths):
    count, (rows, width) = len(ups) + 1, own.shape
    group, total = rows * count, sum(lengths)
    tiles = tiles_of(width)
    ins = [own, *ups, *downs, slot[None, :]]
    out = call(
        functools.partial(pick_kernel, count, lengths),
        ins,
        {len(ins) - 1},
        [((length, width), BF16) for length in lengths] + [((group, width), BF16)],
        [
            pltpu.VMEM((group, width), BF16),
            pltpu.VMEM((total, group), BF16),
            pltpu.VMEM((total, width), BF16),
            dma(count),
            dma(len(lengths), tiles),
            pltpu.SemaphoreType.DMA,
        ],
        2 * total * group * width,
        2 * (2 * group + total) * width,
    )
    return out[:-1], out[-1]


def expert_rows(blocks, w_gate, w_up, w_down):
    inner, width = w_down.shape[1:]
    rows = sum(b.shape[0] for b in blocks)
    ins, outs = tiles_of(inner // 2), tiles_of(width)
    return call(
        functools.partial(expert_kernel, len(blocks)),
        [*blocks, w_gate, w_up, w_down],
        (),
        [(b.shape, BF16) for b in blocks],
        [
            pltpu.VMEM((rows, width), BF16),
            pltpu.VMEM((width, inner), BF16),
            pltpu.VMEM((width, inner), BF16),
            pltpu.VMEM((inner, width), BF16),
            pltpu.VMEM((rows, inner), BF16),
            pltpu.VMEM((rows, width), BF16),
            dma(len(blocks)),
            dma(ins),
            dma(ins),
            dma(outs),
            dma(len(blocks), outs),
        ],
        6 * rows * inner * width,
        (4 * rows + 6 * inner) * width,
    )


def shared_near(group, blocks, inner):
    offsets = sorted(blocks)
    rows, (tokens, width) = blocks[0].shape[0], group.shape
    count = len(offsets)
    return call(
        functools.partial(near_kernel, offsets, inner),
        [group, *[blocks[o] for o in offsets]],
        (),
        [((tokens, 2 * inner), F32)],
        [
            pltpu.VMEM((tokens, width), BF16),
            pltpu.VMEM((count // 2, 2 * rows, 2 * inner), BF16),
            pltpu.VMEM((tokens, 2 * inner), F32),
            pltpu.SemaphoreType.DMA,
            dma(count),
            dma(1, tiles_of(2 * inner)),
        ],
        4 * tokens * inner * rows * count,
        4 * rows * inner * count + 8 * tokens * inner,
    )[0]


def shared_far(part, group, blocks, inner):
    offsets = sorted(blocks)
    late = [o for o in offsets if far(o)]
    rows, (tokens, width) = blocks[0].shape[0], group.shape
    count = len(offsets)
    return call(
        functools.partial(far_kernel, offsets, late, inner),
        [part, group, *[blocks[o] for o in offsets]],
        (),
        [((tokens, width), F32)],
        [
            pltpu.VMEM((tokens, width), BF16),
            pltpu.VMEM((tokens, 2 * inner), F32),
            pltpu.VMEM((len(late) // 2, 2 * rows, 2 * inner), BF16),
            pltpu.VMEM((count // 2, 2 * rows, inner), BF16),
            pltpu.VMEM((tokens, inner), BF16),
            pltpu.VMEM((tokens, width), F32),
            pltpu.SemaphoreType.DMA,
            dma(len(late)),
            dma(2 * tiles_of(inner // 2)),
            dma(count),
            dma(count // 2),
        ],
        4 * tokens * inner * rows * len(late) + 2 * tokens * inner * width,
        4 * rows * inner * len(late) + 6 * tokens * width + 8 * tokens * inner,
    )[0]


def combine(blocks, notes, shared, parts):
    group, width = shared.shape
    total = sum(b.shape[0] for b in blocks)
    tiles = tiles_of(width)
    ins = [*blocks, notes, shared]
    return call(
        functools.partial(combine_kernel, len(blocks), parts),
        ins,
        {len(blocks)},
        [((group // parts, width), BF16)] * parts,
        [
            pltpu.VMEM((total, width), BF16),
            pltpu.VMEM((group, width), F32),
            pltpu.VMEM((group, width), BF16),
            dma(len(blocks)),
            dma(tiles),
            dma(parts, tiles),
        ],
        2 * group * total * width,
        (2 * total + 6 * group) * width,
    )


def body(tokens, expert_ids, gates, w_gate, w_up, w_down, s_gate, s_up, s_down):
    size = lax.axis_size("expert")
    count = lax.axis_size("tensor")
    me = lax.axis_index("expert")
    place = lax.axis_index("tensor")
    rows, _ = tokens.shape
    group = rows * count
    experts = w_gate.shape[0] * size
    cap = 2 * group // experts
    half = cap // 2
    inner = s_gate.shape[1]

    ups, downs = line_gather(tokens, count, 2)
    s_all = jnp.concatenate([s_gate, s_up, s_down.T], axis=1)
    near = {bit: swap(s_all, "expert", bit) for bit in bits_of((size - 1) & ~1)}
    notes = jnp.concatenate([expert_ids.astype(F32).T, gates[None, :]], axis=0)
    above, below = line_gather(notes, count, count)
    parts = [notes]
    for back in range(1, count):
        parts.append(jnp.where(place >= back, above[back - 1], below[count - back - 1]))
    notes = jnp.concatenate(parts, axis=1)
    ids, scale = notes[0].astype(jnp.int32), notes[1]

    index = jnp.arange(group, dtype=jnp.int32)
    back = index // rows
    index = jnp.where(back > place, place - back + count, place - back) * rows + index % rows
    same = (ids[:, None] == ids[None, :]) & (index[None, :] < index[:, None])
    spot = jnp.sum(same.astype(jnp.int32), axis=1)
    turned = spot + (place & 1) * half
    turned = jnp.where(turned >= cap, turned - cap, turned)
    base, lengths, total = [], [], 0
    for offset in range(size):
        lengths.append(half if far(offset) else cap)
        base.append(total)
        total += lengths[-1]
    slot = jnp.full((group,), -1, jnp.int32)
    for offset in range(size):
        value = base[offset] + spot
        if far(offset):
            value = jnp.where(turned < half, base[offset] + turned, -1)
        slot = jnp.where(ids ^ me == offset, value, slot)
    slot = lax.optimization_barrier(slot)
    fars = [o for o in range(size) if far(o)]
    nears = [o for o in range(2, size) if not far(o)]

    sent, tokens = pick_rows(tokens, ups, downs, slot, lengths)
    got = {0: sent[0]}
    for o in fars:
        got[o] = swap(sent[o], "expert", o)
    for o in [1] + nears:
        got[o] = swap(sent[o], "expert", o)
    blocks = with_partner({0: s_all, **near})
    part = None
    if 2 * s_all.shape[0] % LANES == 0:
        part = shared_near(tokens, blocks, inner)
    mine = jnp.concatenate([got[o] for o in fars])
    mine, *ready = lax.optimization_barrier((mine, *near.values()))
    near = dict(zip(near, ready))
    other = swap(mine, "tensor", 1)
    blocks = {**blocks, **with_partner(far_blocks(near, s_all, size))}

    home = {}
    home[0], made, mine, theirs = expert_rows([got[0], got[1], mine, other], w_gate, w_up, w_down)
    theirs = swap(theirs, "tensor", 1)
    mine = add(mine, theirs)
    home[1] = swap(made, "expert", 1)
    for k, o in enumerate(fars):
        home[o] = swap(mine[k * half:(k + 1) * half], "expert", o)
    made = expert_rows([got[o] for o in nears], w_gate, w_up, w_down)
    for k, o in enumerate(nears):
        home[o] = swap(made[k], "expert", o)

    if part is not None:
        shared = shared_far(part, tokens, blocks, inner)
    else:
        s_in = in_order({o: b[:, :2 * inner] for o, b in blocks.items()}, me)
        s_out = in_order({o: b[:, 2 * inner:] for o, b in blocks.items()}, me)
        pre = dot(tokens, s_in)
        shared = (jax.nn.silu(pre[:, :inner]) * pre[:, inner:]).astype(BF16)
        shared = dot_t(shared, s_out)

    notes = jnp.stack([slot.astype(F32), scale], axis=1)
    parts = combine([home[o] for o in range(size)], notes, shared, count)
    return line_scatter(parts, count)


def solution(mesh):
    return jax.shard_map(
        body,
        mesh=mesh,
        in_specs=(
            P(("expert", "tensor"), None),
            P(("expert", "tensor"), None),
            P(("expert", "tensor")),
            P("expert", None, "tensor"),
            P("expert", None, "tensor"),
            P("expert", "tensor", None),
            P("expert", "tensor"),
            P("expert", "tensor"),
            P("tensor", "expert"),
        ),
        out_specs=P(("expert", "tensor"), None),
        check_vma=False,
    )
```

profile of v0, /device:TPU:0, one launch (start us, length us, event | category | flops | bytes accessed | tf_op | source)
XLA Modules:
  0.0 306.7 jit_solution(3762331704162139670)
XLA Ops:
  1.3 7.0 %collective-permute-start.10 = (f32[2,128]{1,0:T(2,128)S(1)}, f32[2,128]{1,0:T(2,128)S(1)}, u32[]{:S(2)}, u32[]{:S(2)}) collective-permute-start(f32[2,128]{1,0:T(2,128)S(1)} %pad_maximum_fusion.4), channel_id=1, source_target_pairs={{0,3},{4,7},{8,11},{12,15},{16,19},{20,23},{24,27},{28,31}} | collective-permute-start | bytes 3080 | tf_op jit(solution)/shard_map/ppermute | solution.py:40
  8.3 1.3 collective-permute-start.11
  10.9 1.3 collective-permute-start.9
  12.2 4.5 %collective-permute-start.6 = (f32[2,128]{1,0:T(2,128)S(1)}, f32[2,128]{1,0:T(2,128)S(1)}, u32[]{:S(2)}, u32[]{:S(2)}) collective-permute-start(f32[2,128]{1,0:T(2,128)S(1)} %pad_maximum_fusion.4), channel_id=1, source_target_pairs={{0,1},{1,2},{2,3},{4,5},{5,6},{6,7},{8,9},{9,10},{10,11},{12,13},{... | collective-permute-start | bytes 3080 | tf_op jit(solution)/shard_map/ppermute | solution.py:40
  16.8 1.7 pad_maximum_fusion.refs_1_.refs_2_
  18.5 1.3 collective-permute-start.7
  19.8 4.9 %collective-permute-start.1 = (bf16[128,2560]{1,0:T(8,128)(2,1)S(1)}, bf16[128,2560]{1,0:T(8,128)(2,1)S(1)}, u32[]{:S(2)}, u32[]{:S(2)}) collective-permute-start(bf16[128,2560]{1,0:T(8,128)(2,1)S(1)} %copy-done.16), channel_id=1, source_target_pairs={{0,2},{1,3},{4,6},{5,7},{8,10},{9,11},{12,14},{13,15},{16,18},{17,... | collective-permute-start | bytes 1966088 | tf_op jit(solution)/shard_map/ppermute | solution.py:40
  24.7 1.3 collective-permute-start.4
  26.0 4.0 %collective-permute-start = (bf16[128,2560]{1,0:T(8,128)(2,1)S(1)}, bf16[128,2560]{1,0:T(8,128)(2,1)S(1)}, u32[]{:S(2)}, u32[]{:S(2)}) collective-permute-start(bf16[128,2560]{1,0:T(8,128)(2,1)S(1)} %copy-done.16), channel_id=1, source_target_pairs={{0,1},{1,2},{2,3},{4,5},{5,6},{6,7},{8,9},{9,10},{10,11},{12,13},{... | collective-permute-start | bytes 1966088 | tf_op jit(solution)/shard_map/ppermute | solution.py:40
  30.1 1.6 collective-permute-start.15
  31.7 1.5 collective-permute-start.16
  33.2 6.6 %collective-permute-done.1.refs_2_ = bf16[128,2560]{1,0:T(8,128)(2,1)S(1)} collective-permute-done((bf16[128,2560]{1,0:T(8,128)(2,1)S(1)}, bf16[128,2560]{1,0:T(8,128)(2,1)S(1)}, u32[]{:S(2)}, u32[]{:S(2)}) %collective-permute-start.1) | collective-permute-done | bytes 655392 | tf_op jit(solution)/shard_map/ppermute | solution.py:40
  41.1 15.6 %collective-permute-done.4.refs_5_ = bf16[128,2560]{1,0:T(8,128)(2,1)S(1)} collective-permute-done((bf16[128,2560]{1,0:T(8,128)(2,1)S(1)}, bf16[128,2560]{1,0:T(8,128)(2,1)S(1)}, u32[]{:S(2)}, u32[]{:S(2)}) %collective-permute-start.4) | collective-permute-done | bytes 655392 | tf_op jit(solution)/shard_map/ppermute | solution.py:40
  57.4 1.3 collective-permute-start.5
  59.7 11.0 %collective-permute-done.3.refs_4_ = bf16[128,2560]{1,0:T(8,128)(2,1)S(1)} collective-permute-done((bf16[128,2560]{1,0:T(8,128)(2,1)S(1)}, bf16[128,2560]{1,0:T(8,128)(2,1)S(1)}, u32[]{:S(2)}, u32[]{:S(2)}) %collective-permute-start.3) | collective-permute-done | bytes 655392 | tf_op jit(solution)/shard_map/ppermute | solution.py:40
  70.7 14.0 %collective-permute-done.5.refs_6_ = bf16[128,2560]{1,0:T(8,128)(2,1)S(1)} collective-permute-done((bf16[128,2560]{1,0:T(8,128)(2,1)S(1)}, bf16[128,2560]{1,0:T(8,128)(2,1)S(1)}, u32[]{:S(2)}, u32[]{:S(2)}) %collective-permute-start.5) | collective-permute-done | bytes 655392 | tf_op jit(solution)/shard_map/ppermute | solution.py:40
  85.6 7.0 %shard_map.91 = (bf16[128,2560]{1,0:T(8,128)(2,1)}, bf16[128,2560]{1,0:T(8,128)(2,1)}, bf16[128,2560]{1,0:T(8,128)(2,1)}, bf16[128,2560]{1,0:T(8,128)(2,1)}, bf1...) custom-call(bf16[128,2560]{1,0:T(8,128)(2,1)} %refs_0_.1, ...), custom_call_target="tpu_custom_call" | custom-call | flops 2348810240 | bytes 9830400 | tf_op jit(solution)/shard_map/pallas_call | solution.py:369
  92.5 2.5 collective-permute-start.13
  95.1 9.2 %collective-permute-done.13 = bf16[64,2560]{1,0:T(8,128)(2,1)S(1)} collective-permute-done((bf16[64,2560]{1,0:T(8,128)(2,1)}, bf16[64,2560]{1,0:T(8,128)(2,1)S(1)}, u32[]{:S(2)}, u32[]{:S(2)}) %collective-permute-start.13) | collective-permute-done | bytes 327712 | tf_op jit(solution)/shard_map/ppermute | solution.py:36
  104.3 5.3 %collective-permute-done.14 = bf16[64,2560]{1,0:T(8,128)(2,1)S(1)} collective-permute-done((bf16[64,2560]{1,0:T(8,128)(2,1)}, bf16[64,2560]{1,0:T(8,128)(2,1)S(1)}, u32[]{:S(2)}, u32[]{:S(2)}) %collective-permute-start.14) | collective-permute-done | bytes 327712 | tf_op jit(solution)/shard_map/ppermute | solution.py:36
  111.6 1.4 collective-permute-start.33
  114.5 1.5 collective-permute-start.34
  118.0 12.4 %collective-permute-done.17.refs_3_ = bf16[128,2560]{1,0:T(8,128)(2,1)} collective-permute-done((bf16[128,2560]{1,0:T(8,128)(2,1)}, bf16[128,2560]{1,0:T(8,128)(2,1)}, u32[]{:S(2)}, u32[]{:S(2)}) %collective-permute-start.17) | collective-permute-done | bytes 655392 | tf_op jit(solution)/shard_map/ppermute | solution.py:36
  130.5 1.5 collective-permute-start.21
  132.0 4.5 %collective-permute-done.33 = bf16[320,1536]{1,0:T(8,128)(2,1)S(1)} collective-permute-done((bf16[320,1536]{1,0:T(8,128)(2,1)}, bf16[320,1536]{1,0:T(8,128)(2,1)S(1)}, u32[]{:S(2)}, u32[]{:S(2)}) %collective-permute-start.33) | collective-permute-done | bytes 983072 | tf_op jit(solution)/shard_map/ppermute | solution.py:36
  137.2 13.7 %shard_map.92 = (bf16[128,2560]{1,0:T(8,128)(2,1)}, bf16[128,2560]{1,0:T(8,128)(2,1)}, bf16[128,2560]{1,0:T(8,128)(2,1)}, bf16[128,2560]{1,0:T(8,128)(2,1)}) custom-call(bf16[128,2560]{1,0:T(8,128)(2,1)} %get-tuple-element.29.refs_0_, bf16[128,2560]{1,0:T(8,128)(2,1)} %collective-permute-done.12.refs_1_, bf16[128,2560]{1,0:T(8,128)(2,1)} %pad_maximum_fusion.1.refs_2_, ...), custom_call_target="tpu_custom_call" | custom-call | flops 8053063680 | bytes 20971520 | tf_op jit(solution)/shard_map/pallas_call | solution.py:369
  152.8 2.3 constant_dynamic-update-slice_fusion.refs_8_
  155.6 8.4 %collective-permute-done.20.refs_1_ = bf16[128,2560]{1,0:T(8,128)(2,1)} collective-permute-done((bf16[128,2560]{1,0:T(8,128)(2,1)}, bf16[128,2560]{1,0:T(8,128)(2,1)}, u32[]{:S(2)}, u32[]{:S(2)}) %collective-permute-start.20) | collective-permute-done | bytes 655392 | tf_op jit(solution)/shard_map/ppermute | solution.py:36
  166.4 13.7 %shard_map.93 = (bf16[128,2560]{1,0:T(8,128)(2,1)}, bf16[128,2560]{1,0:T(8,128)(2,1)}, bf16[128,2560]{1,0:T(8,128)(2,1)}, bf16[128,2560]{1,0:T(8,128)(2,1)}) custom-call(bf16[128,2560]{1,0:T(8,128)(2,1)} %copy-done.20, bf16[128,2560]{1,0:T(8,128)(2,1)} %collective-permute-done.20.refs_1_, bf16[128,2560]{1,0:T(8,128)(2,1)} %collective-permute-done.21.refs_2_, ...), custom_call_target="tpu_custom_call" | custom-call | flops 8053063680 | bytes 20971520 | tf_op jit(solution)/shard_map/pallas_call | solution.py:369
  181.4 1.6 collective-permute-start.23
  183.2 15.9 %collective-permute-done.23.refs_2_ = bf16[128,2560]{1,0:T(8,128)(2,1)S(1)} collective-permute-done((bf16[128,2560]{1,0:T(8,128)(2,1)}, bf16[128,2560]{1,0:T(8,128)(2,1)S(1)}, u32[]{:S(2)}, u32[]{:S(2)}) %collective-permute-start.23) | collective-permute-done | bytes 655392 | tf_op jit(solution)/shard_map/ppermute | solution.py:36
  199.2 1.6 collective-permute-start.25
  201.3 10.7 %shard_map.94.refs_0_ = f32[512,2048]{1,0:T(8,128)} custom-call(bf16[512,2560]{1,0:T(8,128)(2,1)} %get-tuple-element.46.refs_0_.refs_1_, bf16[320,3072]{1,0:T(8,128)(2,1)} %copy-done, bf16[320,3072]{1,0:T(8,128)(2,1)} %collective-permute-done.30.refs_2_.refs_3_, bf16[320,3072]{1,0:T(8,128)(2,1)} %copy-done.1, ...), custom_call_target="tpu_custom_call" | custom-call | flops 4026531840 | bytes 12058624 | tf_op jit(solution)/shard_map/pallas_call | solution.py:369
  212.1 2.6 collective-permute-start.28
  214.8 10.1 %shard_map.95.refs_9_ = f32[512,2560]{1,0:T(8,128)} custom-call(f32[512,2048]{1,0:T(8,128)} %shard_map.94.refs_0_, bf16[512,2560]{1,0:T(8,128)(2,1)} %get-tuple-element.46.refs_0_.refs_1_, bf16[320,3072]{1,0:T(8,128)(2,1)} %copy-done, bf16[320,3072]{1,0:T(8,128)(2,1)} %collective-permute-done.30.refs_2_.refs_3_, bf16[320,3072]{1,0:T(8,128)(2,1)} %copy-done.1, ...), custom_call_target="tpu_custom_call" | custom-call | flops 4026531840 | bytes 14680064 | tf_op jit(solution)/shard_map/pallas_call | solution.py:369
  224.9 6.1 %collective-permute-done.25.refs_4_ = bf16[128,2560]{1,0:T(8,128)(2,1)S(1)} collective-permute-done((bf16[128,2560]{1,0:T(8,128)(2,1)}, bf16[128,2560]{1,0:T(8,128)(2,1)S(1)}, u32[]{:S(2)}, u32[]{:S(2)}) %collective-permute-start.25) | collective-permute-done | bytes 655392 | tf_op jit(solution)/shard_map/ppermute | solution.py:36
  231.0 9.1 %collective-permute-done.26.refs_5_ = bf16[128,2560]{1,0:T(8,128)(2,1)S(1)} collective-permute-done((bf16[128,2560]{1,0:T(8,128)(2,1)}, bf16[128,2560]{1,0:T(8,128)(2,1)S(1)}, u32[]{:S(2)}, u32[]{:S(2)}) %collective-permute-start.26) | collective-permute-done | bytes 655392 | tf_op jit(solution)/shard_map/ppermute | solution.py:36
  241.4 8.7 %shard_map.96 = (bf16[128,2560]{1,0:T(8,128)(2,1)}, bf16[128,2560]{1,0:T(8,128)(2,1)}, bf16[128,2560]{1,0:T(8,128)(2,1)}, bf16[128,2560]{1,0:T(8,128)(2,1)}) custom-call(bf16[128,2560]{1,0:T(8,128)(2,1)} %get-tuple-element.34.refs_0_, bf16[128,2560]{1,0:T(8,128)(2,1)} %copy-done.9, bf16[128,2560]{1,0:T(8,128)(2,1)} %copy-done.5, ...), custom_call_target="tpu_custom_call" | custom-call | flops 2348810240 | bytes 12451840 | tf_op jit(solution)/shard_map/pallas_call | solution.py:369
  250.2 4.2 %collective-permute-start.36 = (bf16[128,2560]{1,0:T(8,128)(2,1)}, bf16[128,2560]{1,0:T(8,128)(2,1)S(1)}, u32[]{:S(2)}, u32[]{:S(2)}) collective-permute-start(bf16[128,2560]{1,0:T(8,128)(2,1)} %get-tuple-element.51), channel_id=1, source_target_pairs={{0,1},{4,5},{8,9},{12,13},{16,17},{20,21},{24,25},{28,29}} | collective-permute-start | bytes 1966088 | tf_op jit(solution)/shard_map/ppermute | solution.py:40
  255.1 1.3 collective-permute-start.40
  256.4 1.3 collective-permute-start.41
  257.7 12.0 %collective-permute-done.36 = bf16[128,2560]{1,0:T(8,128)(2,1)S(1)} collective-permute-done((bf16[128,2560]{1,0:T(8,128)(2,1)}, bf16[128,2560]{1,0:T(8,128)(2,1)S(1)}, u32[]{:S(2)}, u32[]{:S(2)}) %collective-permute-start.36) | collective-permute-done | bytes 655392 | tf_op jit(solution)/shard_map/ppermute | solution.py:40
  269.8 1.3 fusion
  271.1 1.3 collective-permute-start.37
  272.4 1.3 collective-permute-start.39
  273.7 10.1 %collective-permute-done.40 = bf16[128,2560]{1,0:T(8,128)(2,1)S(1)} collective-permute-done((bf16[128,2560]{1,0:T(8,128)(2,1)}, bf16[128,2560]{1,0:T(8,128)(2,1)S(1)}, u32[]{:S(2)}, u32[]{:S(2)}) %collective-permute-start.40) | collective-permute-done | bytes 655392 | tf_op jit(solution)/shard_map/ppermute | solution.py:40
  283.8 13.7 %collective-permute-done.37 = bf16[128,2560]{1,0:T(8,128)(2,1)S(1)} collective-permute-done((bf16[128,2560]{1,0:T(8,128)(2,1)S(1)}, bf16[128,2560]{1,0:T(8,128)(2,1)S(1)}, u32[]{:S(2)}, u32[]{:S(2)}) %collective-permute-start.37) | collective-permute-done | bytes 655392 | tf_op jit(solution)/shard_map/ppermute | solution.py:40
  297.5 8.0 %collective-permute-done.39 = bf16[128,2560]{1,0:T(8,128)(2,1)S(1)} collective-permute-done((bf16[128,2560]{1,0:T(8,128)(2,1)S(1)}, bf16[128,2560]{1,0:T(8,128)(2,1)S(1)}, u32[]{:S(2)}, u32[]{:S(2)}) %collective-permute-start.39) | collective-permute-done | bytes 655392 | tf_op jit(solution)/shard_map/ppermute | solution.py:40
  (113 shorter events, 22.7 us)
Async XLA Ops:
  1.3 17.2 %collective-permute-start.10 = (f32[2,128]{1,0:T(2,128)S(1)}, f32[2,128]{1,0:T(2,128)S(1)}, u32[]{:S(2)}, u32[]{:S(2)}) collective-permute-start(f32[2,128]{1,0:T(2,128)S(1)} %pad_maximum_fusion.4), channel_id=1, source_target_pairs={{0,3},{4,7},{8,11},{12,15},{16,19},{20,23},{24,27},{28,31}} | collective-permute-start | bytes 3080 | tf_op jit(solution)/shard_map/ppermute | solution.py:40
  8.3 11.5 %collective-permute-start.11 = (f32[2,128]{1,0:T(2,128)S(1)}, f32[2,128]{1,0:T(2,128)S(1)}, u32[]{:S(2)}, u32[]{:S(2)}) collective-permute-start(f32[2,128]{1,0:T(2,128)S(1)} %pad_maximum_fusion.4), channel_id=1, source_target_pairs={{1,0},{2,1},{3,2},{5,4},{6,5},{7,6},{9,8},{10,9},{11,10},{13,12},{... | collective-permute-start | bytes 3080 | tf_op jit(solution)/shard_map/ppermute | solution.py:40
  9.6 15.1 %collective-permute-start.8 = (f32[2,128]{1,0:T(2,128)S(1)}, f32[2,128]{1,0:T(2,128)S(1)}, u32[]{:S(2)}, u32[]{:S(2)}) collective-permute-start(f32[2,128]{1,0:T(2,128)S(1)} %pad_maximum_fusion.4), channel_id=1, source_target_pairs={{0,2},{1,3},{4,6},{5,7},{8,10},{9,11},{12,14},{13,15},{16,18},{17,... | collective-permute-start | bytes 3080 | tf_op jit(solution)/shard_map/ppermute | solution.py:40
  10.9 15.1 %collective-permute-start.9 = (f32[2,128]{1,0:T(2,128)S(1)}, f32[2,128]{1,0:T(2,128)S(1)}, u32[]{:S(2)}, u32[]{:S(2)}) collective-permute-start(f32[2,128]{1,0:T(2,128)S(1)} %pad_maximum_fusion.4), channel_id=1, source_target_pairs={{2,0},{3,1},{6,4},{7,5},{10,8},{11,9},{14,12},{15,13},{18,16},{19,... | collective-permute-start | bytes 3080 | tf_op jit(solution)/shard_map/ppermute | solution.py:40
  12.2 17.9 %collective-permute-start.6 = (f32[2,128]{1,0:T(2,128)S(1)}, f32[2,128]{1,0:T(2,128)S(1)}, u32[]{:S(2)}, u32[]{:S(2)}) collective-permute-start(f32[2,128]{1,0:T(2,128)S(1)} %pad_maximum_fusion.4), channel_id=1, source_target_pairs={{0,1},{1,2},{2,3},{4,5},{5,6},{6,7},{8,9},{9,10},{10,11},{12,13},{... | collective-permute-start | bytes 3080 | tf_op jit(solution)/shard_map/ppermute | solution.py:40
  16.8 42.0 %copy-start.15 = (f32[128]{0:T(128)S(1)}, f32[128]{0:T(128)}, u32[]{:S(2)}) copy-start(f32[128]{0:T(128)} %param.11) | copy-start | bytes 1540
  18.5 132.5 %copy-start = (bf16[320,3072]{1,0:T(8,128)(2,1)}, bf16[320,3072]{1,0:T(8,128)(2,1)S(1)}, u32[]{:S(2)}) copy-start(bf16[320,3072]{1,0:T(8,128)(2,1)S(1)} %pad_maximum_fusion.refs_1_.refs_2_) | copy-start | bytes 5898244
  18.5 13.1 %collective-permute-start.7 = (f32[2,128]{1,0:T(2,128)S(1)}, f32[2,128]{1,0:T(2,128)S(1)}, u32[]{:S(2)}, u32[]{:S(2)}) collective-permute-start(f32[2,128]{1,0:T(2,128)S(1)} %pad_maximum_fusion.4), channel_id=1, source_target_pairs={{3,0},{7,4},{11,8},{15,12},{19,16},{23,20},{27,24},{31,28}} | collective-permute-start | bytes 3080 | tf_op jit(solution)/shard_map/ppermute | solution.py:40
  19.8 20.0 %collective-permute-start.1 = (bf16[128,2560]{1,0:T(8,128)(2,1)S(1)}, bf16[128,2560]{1,0:T(8,128)(2,1)S(1)}, u32[]{:S(2)}, u32[]{:S(2)}) collective-permute-start(bf16[128,2560]{1,0:T(8,128)(2,1)S(1)} %copy-done.16), channel_id=1, source_target_pairs={{0,2},{1,3},{4,6},{5,7},{8,10},{9,11},{12,14},{13,15},{16,18},{17,... | collective-permute-start | bytes 1966088 | tf_op jit(solution)/shard_map/ppermute | solution.py:40
  24.7 32.0 %collective-permute-start.4 = (bf16[128,2560]{1,0:T(8,128)(2,1)S(1)}, bf16[128,2560]{1,0:T(8,128)(2,1)S(1)}, u32[]{:S(2)}, u32[]{:S(2)}) collective-permute-start(bf16[128,2560]{1,0:T(8,128)(2,1)S(1)} %copy-done.16), channel_id=1, source_target_pairs={{2,0},{3,1},{6,4},{7,5},{10,8},{11,9},{14,12},{15,13},{18,16},{19,... | collective-permute-start | bytes 1966088 | tf_op jit(solution)/shard_map/ppermute | solution.py:40
  26.0 31.4 %collective-permute-start = (bf16[128,2560]{1,0:T(8,128)(2,1)S(1)}, bf16[128,2560]{1,0:T(8,128)(2,1)S(1)}, u32[]{:S(2)}, u32[]{:S(2)}) collective-permute-start(bf16[128,2560]{1,0:T(8,128)(2,1)S(1)} %copy-done.16), channel_id=1, source_target_pairs={{0,1},{1,2},{2,3},{4,5},{5,6},{6,7},{8,9},{9,10},{10,11},{12,13},{... | collective-permute-start | bytes 1966088 | tf_op jit(solution)/shard_map/ppermute | solution.py:40
  30.1 80.4 %collective-permute-start.15 = (bf16[320,3072]{1,0:T(8,128)(2,1)S(1)}, bf16[320,3072]{1,0:T(8,128)(2,1)S(1)}, u32[]{:S(2)}, u32[]{:S(2)}) collective-permute-start(bf16[320,3072]{1,0:T(8,128)(2,1)S(1)} %pad_maximum_fusion.refs_1_.refs_2_), channel_id=1, source_target_pairs={{0,8},{4,12},{8,0},{12,4},{16,24},{20,28},{24,16},{28,20},{1,9},{5... | collective-permute-start | bytes 5898248 | tf_op jit(solution)/shard_map/ppermute | solution.py:36
  31.7 78.8 %collective-permute-start.16 = (bf16[320,3072]{1,0:T(8,128)(2,1)S(1)}, bf16[320,3072]{1,0:T(8,128)(2,1)S(1)}, u32[]{:S(2)}, u32[]{:S(2)}) collective-permute-start(bf16[320,3072]{1,0:T(8,128)(2,1)S(1)} %pad_maximum_fusion.refs_1_.refs_2_), channel_id=1, source_target_pairs={{0,16},{4,20},{8,24},{12,28},{16,0},{20,4},{24,8},{28,12},{1,17},{... | collective-permute-start | bytes 5898248 | tf_op jit(solution)/shard_map/ppermute | solution.py:36
  39.8 45.8 %copy-start.17 = (bf16[128,2560]{1,0:T(8,128)(2,1)}, bf16[128,2560]{1,0:T(8,128)(2,1)S(1)}, u32[]{:S(2)}) copy-start(bf16[128,2560]{1,0:T(8,128)(2,1)S(1)} %collective-permute-done.1.refs_2_) | copy-start | bytes 1966084
  39.8 30.9 %collective-permute-start.3 = (bf16[128,2560]{1,0:T(8,128)(2,1)S(1)}, bf16[128,2560]{1,0:T(8,128)(2,1)S(1)}, u32[]{:S(2)}, u32[]{:S(2)}) collective-permute-start(bf16[128,2560]{1,0:T(8,128)(2,1)S(1)} %copy-done.16), channel_id=1, source_target_pairs={{1,0},{2,1},{3,2},{5,4},{6,5},{7,6},{9,8},{10,9},{11,10},{13,12},{... | collective-permute-start | bytes 1966088 | tf_op jit(solution)/shard_map/ppermute | solution.py:40
  56.7 28.9 %copy-start.18 = (bf16[128,2560]{1,0:T(8,128)(2,1)}, bf16[128,2560]{1,0:T(8,128)(2,1)S(1)}, u32[]{:S(2)}) copy-start(bf16[128,2560]{1,0:T(8,128)(2,1)S(1)} %collective-permute-done.4.refs_5_) | copy-start | bytes 1966084
  56.7 14.0 %collective-permute-start.2 = (bf16[128,2560]{1,0:T(8,128)(2,1)S(1)}, bf16[128,2560]{1,0:T(8,128)(2,1)S(1)}, u32[]{:S(2)}, u32[]{:S(2)}) collective-permute-start(bf16[128,2560]{1,0:T(8,128)(2,1)S(1)} %collective-permute-done.1.refs_2_), channel_id=1, source_target_pairs={{2,3},{6,7},{10,11},{14,15},{18,19},{22,23},{26,27},{30,31}} | collective-permute-start | bytes 1966088 | tf_op jit(solution)/shard_map/ppermute | solution.py:40
  57.4 27.3 %collective-permute-start.5 = (bf16[128,2560]{1,0:T(8,128)(2,1)S(1)}, bf16[128,2560]{1,0:T(8,128)(2,1)S(1)}, u32[]{:S(2)}, u32[]{:S(2)}) collective-permute-start(bf16[128,2560]{1,0:T(8,128)(2,1)S(1)} %collective-permute-done.4.refs_5_), channel_id=1, source_target_pairs={{1,0},{5,4},{9,8},{13,12},{17,16},{21,20},{25,24},{29,28}} | collective-permute-start | bytes 1966088 | tf_op jit(solution)/shard_map/ppermute | solution.py:40
  92.5 11.8 %collective-permute-start.13 = (bf16[64,2560]{1,0:T(8,128)(2,1)}, bf16[64,2560]{1,0:T(8,128)(2,1)S(1)}, u32[]{:S(2)}, u32[]{:S(2)}) collective-permute-start(bf16[64,2560]{1,0:T(8,128)(2,1)} %get-tuple-element.31), channel_id=1, source_target_pairs={{0,24},{4,28},{8,16},{12,20},{16,8},{20,12},{24,0},{28,4},{1,25},{... | collective-permute-start | bytes 983048 | tf_op jit(solution)/shard_map/ppermute | solution.py:36
  95.1 14.5 %collective-permute-start.14 = (bf16[64,2560]{1,0:T(8,128)(2,1)}, bf16[64,2560]{1,0:T(8,128)(2,1)S(1)}, u32[]{:S(2)}, u32[]{:S(2)}) collective-permute-start(bf16[64,2560]{1,0:T(8,128)(2,1)} %get-tuple-element.32), channel_id=1, source_target_pairs={{0,28},{4,24},{8,20},{12,16},{16,12},{20,8},{24,4},{28,0},{1,29},{... | collective-permute-start | bytes 983048 | tf_op jit(solution)/shard_map/ppermute | solution.py:36
  111.6 24.8 %collective-permute-start.33 = (bf16[320,1536]{1,0:T(8,128)(2,1)}, bf16[320,1536]{1,0:T(8,128)(2,1)S(1)}, u32[]{:S(2)}, u32[]{:S(2)}) collective-permute-start(bf16[320,1536]{1,0:T(8,128)(2,1)} %slice.22), channel_id=1, source_target_pairs={{0,8},{4,12},{8,0},{12,4},{16,24},{20,28},{24,16},{28,20},{1,9},{5... | collective-permute-start | bytes 2949128 | tf_op jit(solution)/shard_map/ppermute | solution.py:36
  113.0 4.4 %collective-permute-start.12 = (bf16[128,2560]{1,0:T(8,128)(2,1)}, bf16[128,2560]{1,0:T(8,128)(2,1)}, u32[]{:S(2)}, u32[]{:S(2)}) collective-permute-start(bf16[128,2560]{1,0:T(8,128)(2,1)} %get-tuple-element.30), channel_id=1, source_target_pairs={{0,4},{4,0},{8,12},{12,8},{16,20},{20,16},{24,28},{28,24},{1,5},{5... | collective-permute-start | bytes 1966088 | tf_op jit(solution)/shard_map/ppermute | solution.py:36
  113.5 17.0 %collective-permute-start.17 = (bf16[128,2560]{1,0:T(8,128)(2,1)}, bf16[128,2560]{1,0:T(8,128)(2,1)}, u32[]{:S(2)}, u32[]{:S(2)}) collective-permute-start(bf16[128,2560]{1,0:T(8,128)(2,1)} %pad_maximum_fusion.1.refs_2_), channel_id=1, source_target_pairs={{0,1},{1,0},{2,3},{3,2},{4,5},{5,4},{6,7},{7,6},{8,9},{9,8},{10,11... | collective-permute-start | bytes 1966088 | tf_op jit(solution)/shard_map/ppermute | solution.py:36
  114.5 36.5 %collective-permute-start.34 = (bf16[320,1536]{1,0:T(8,128)(2,1)}, bf16[320,1536]{1,0:T(8,128)(2,1)}, u32[]{:S(2)}, u32[]{:S(2)}) collective-permute-start(bf16[320,1536]{1,0:T(8,128)(2,1)} %slice.23), channel_id=1, source_target_pairs={{0,16},{4,20},{8,24},{12,28},{16,0},{20,4},{24,8},{28,12},{1,17},{... | collective-permute-start | bytes 2949128 | tf_op jit(solution)/shard_map/ppermute | solution.py:36
  116.9 38.2 %collective-permute-start.19 = (bf16[128,2560]{1,0:T(8,128)(2,1)}, bf16[128,2560]{1,0:T(8,128)(2,1)S(1)}, u32[]{:S(2)}, u32[]{:S(2)}) collective-permute-start(bf16[128,2560]{1,0:T(8,128)(2,1)} %get-tuple-element.36), channel_id=1, source_target_pairs={{0,8},{4,12},{8,0},{12,4},{16,24},{20,28},{24,16},{28,20},{1,9},{5... | collective-permute-start | bytes 1966088 | tf_op jit(solution)/shard_map/ppermute | solution.py:36
  117.4 46.5 %collective-permute-start.20 = (bf16[128,2560]{1,0:T(8,128)(2,1)}, bf16[128,2560]{1,0:T(8,128)(2,1)}, u32[]{:S(2)}, u32[]{:S(2)}) collective-permute-start(bf16[128,2560]{1,0:T(8,128)(2,1)} %get-tuple-element.37), channel_id=1, source_target_pairs={{0,12},{4,8},{8,4},{12,0},{16,28},{20,24},{24,20},{28,16},{1,13},{... | collective-permute-start | bytes 1966088 | tf_op jit(solution)/shard_map/ppermute | solution.py:36
  130.5 34.0 %collective-permute-start.21 = (bf16[128,2560]{1,0:T(8,128)(2,1)}, bf16[128,2560]{1,0:T(8,128)(2,1)}, u32[]{:S(2)}, u32[]{:S(2)}) collective-permute-start(bf16[128,2560]{1,0:T(8,128)(2,1)} %get-tuple-element.38), channel_id=1, source_target_pairs={{0,16},{4,20},{8,24},{12,28},{16,0},{20,4},{24,8},{28,12},{1,17},{... | collective-permute-start | bytes 1966088 | tf_op jit(solution)/shard_map/ppermute | solution.py:36
  136.4 29.2 %collective-permute-start.22 = (bf16[128,2560]{1,0:T(8,128)(2,1)}, bf16[128,2560]{1,0:T(8,128)(2,1)}, u32[]{:S(2)}, u32[]{:S(2)}) collective-permute-start(bf16[128,2560]{1,0:T(8,128)(2,1)} %get-tuple-element.39), channel_id=1, source_target_pairs={{0,20},{4,16},{8,28},{12,24},{16,4},{20,0},{24,12},{28,8},{1,21},{... | collective-permute-start | bytes 1966088 | tf_op jit(solution)/shard_map/ppermute | solution.py:36
  151.0 32.1 %collective-permute-start.30 = (bf16[320,3072]{1,0:T(8,128)(2,1)S(1)}, bf16[320,3072]{1,0:T(8,128)(2,1)}, u32[]{:S(2)}, u32[]{:S(2)}) collective-permute-start(bf16[320,3072]{1,0:T(8,128)(2,1)S(1)} %pad_maximum_fusion.refs_1_.refs_2_), channel_id=1, source_target_pairs={{0,4},{4,0},{8,12},{12,8},{16,20},{20,16},{24,28},{28,24},{1,5},{5... | collective-permute-start | bytes 5898248 | tf_op jit(solution)/shard_map/ppermute | solution.py:36
  155.1 45.7 %collective-permute-start.31 = (bf16[320,3072]{1,0:T(8,128)(2,1)S(1)}, bf16[320,3072]{1,0:T(8,128)(2,1)}, u32[]{:S(2)}, u32[]{:S(2)}) collective-permute-start(bf16[320,3072]{1,0:T(8,128)(2,1)S(1)} %copy-done.2), channel_id=1, source_target_pairs={{0,4},{4,0},{8,12},{12,8},{16,20},{20,16},{24,28},{28,24},{1,5},{5... | collective-permute-start | bytes 5898248 | tf_op jit(solution)/shard_map/ppermute | solution.py:36
  164.0 36.8 %collective-permute-start.32 = (bf16[320,3072]{1,0:T(8,128)(2,1)S(1)}, bf16[320,3072]{1,0:T(8,128)(2,1)}, u32[]{:S(2)}, u32[]{:S(2)}) collective-permute-start(bf16[320,3072]{1,0:T(8,128)(2,1)S(1)} %copy-done.4), channel_id=1, source_target_pairs={{0,4},{4,0},{8,12},{12,8},{16,20},{20,16},{24,28},{28,24},{1,5},{5... | collective-permute-start | bytes 5898248 | tf_op jit(solution)/shard_map/ppermute | solution.py:36
  164.4 18.5 %copy-start.10 = (bf16[128,2560]{1,0:T(8,128)(2,1)S(1)}, bf16[128,2560]{1,0:T(8,128)(2,1)}, u32[]{:S(2)}) copy-start(bf16[128,2560]{1,0:T(8,128)(2,1)} %get-tuple-element.44) | copy-start | bytes 1966084
  164.4 16.9 %collective-permute-start.27 = (bf16[128,2560]{1,0:T(8,128)(2,1)}, bf16[128,2560]{1,0:T(8,128)(2,1)S(1)}, u32[]{:S(2)}, u32[]{:S(2)}) collective-permute-start(bf16[128,2560]{1,0:T(8,128)(2,1)} %get-tuple-element.45), channel_id=1, source_target_pairs={{0,1},{1,0},{2,3},{3,2},{4,5},{5,4},{6,7},{7,6},{8,9},{9,8},{10,11... | collective-permute-start | bytes 1966088 | tf_op jit(solution)/shard_map/ppermute | solution.py:36
  165.7 49.1 %collective-permute-start.35 = (bf16[320,3072]{1,0:T(8,128)(2,1)}, bf16[320,3072]{1,0:T(8,128)(2,1)}, u32[]{:S(2)}, u32[]{:S(2)}) collective-permute-start(bf16[320,3072]{1,0:T(8,128)(2,1)} %constant_dynamic-update-slice_fusion.refs_8_), channel_id=1, source_target_pairs={{0,4},{4,0},{8,12},{12,8},{16,20},{20,16},{24,28},{28,24},{1,5},{5... | collective-permute-start | bytes 5898248 | tf_op jit(solution)/shard_map/ppermute | solution.py:36
  181.4 17.8 %collective-permute-start.23 = (bf16[128,2560]{1,0:T(8,128)(2,1)}, bf16[128,2560]{1,0:T(8,128)(2,1)S(1)}, u32[]{:S(2)}, u32[]{:S(2)}) collective-permute-start(bf16[128,2560]{1,0:T(8,128)(2,1)} %get-tuple-element.40), channel_id=1, source_target_pairs={{0,8},{4,12},{8,0},{12,4},{16,24},{20,28},{24,16},{28,20},{1,9},{5... | collective-permute-start | bytes 1966088 | tf_op jit(solution)/shard_map/ppermute | solution.py:36
  183.1 29.0 %collective-permute-start.24 = (bf16[128,2560]{1,0:T(8,128)(2,1)}, bf16[128,2560]{1,0:T(8,128)(2,1)S(1)}, u32[]{:S(2)}, u32[]{:S(2)}) collective-permute-start(bf16[128,2560]{1,0:T(8,128)(2,1)} %get-tuple-element.41), channel_id=1, source_target_pairs={{0,12},{4,8},{8,4},{12,0},{16,28},{20,24},{24,20},{28,16},{1,13},{... | collective-permute-start | bytes 1966088 | tf_op jit(solution)/shard_map/ppermute | solution.py:36
  199.2 31.9 %collective-permute-start.25 = (bf16[128,2560]{1,0:T(8,128)(2,1)}, bf16[128,2560]{1,0:T(8,128)(2,1)S(1)}, u32[]{:S(2)}, u32[]{:S(2)}) collective-permute-start(bf16[128,2560]{1,0:T(8,128)(2,1)} %get-tuple-element.42), channel_id=1, source_target_pairs={{0,16},{4,20},{8,24},{12,28},{16,0},{20,4},{24,8},{28,12},{1,17},{... | collective-permute-start | bytes 1966088 | tf_op jit(solution)/shard_map/ppermute | solution.py:36
  200.8 39.4 %collective-permute-start.26 = (bf16[128,2560]{1,0:T(8,128)(2,1)}, bf16[128,2560]{1,0:T(8,128)(2,1)S(1)}, u32[]{:S(2)}, u32[]{:S(2)}) collective-permute-start(bf16[128,2560]{1,0:T(8,128)(2,1)} %get-tuple-element.43), channel_id=1, source_target_pairs={{0,20},{4,16},{8,28},{12,24},{16,4},{20,0},{24,12},{28,8},{1,21},{... | collective-permute-start | bytes 1966088 | tf_op jit(solution)/shard_map/ppermute | solution.py:36
  200.8 39.4 %collective-permute-start.18 = (bf16[128,2560]{1,0:T(8,128)(2,1)}, bf16[128,2560]{1,0:T(8,128)(2,1)S(1)}, u32[]{:S(2)}, u32[]{:S(2)}) collective-permute-start(bf16[128,2560]{1,0:T(8,128)(2,1)} %get-tuple-element.35), channel_id=1, source_target_pairs={{0,4},{4,0},{8,12},{12,8},{16,20},{20,16},{24,28},{28,24},{1,5},{5... | collective-permute-start | bytes 1966088 | tf_op jit(solution)/shard_map/ppermute | solution.py:36
  212.1 28.1 %collective-permute-start.28 = (bf16[64,2560]{1,0:T(8,128)(2,1)S(1)}, bf16[64,2560]{1,0:T(8,128)(2,1)S(1)}, u32[]{:S(2)}, u32[]{:S(2)}) collective-permute-start(bf16[64,2560]{1,0:T(8,128)(2,1)S(1)} %get-tuple-element.56), channel_id=1, source_target_pairs={{0,24},{4,28},{8,16},{12,20},{16,8},{20,12},{24,0},{28,4},{1,25},{... | collective-permute-start | bytes 983048 | tf_op jit(solution)/shard_map/ppermute | solution.py:36
  214.8 25.4 %collective-permute-start.29 = (bf16[64,2560]{1,0:T(8,128)(2,1)S(1)}, bf16[64,2560]{1,0:T(8,128)(2,1)S(1)}, u32[]{:S(2)}, u32[]{:S(2)}) collective-permute-start(bf16[64,2560]{1,0:T(8,128)(2,1)S(1)} %get-tuple-element.55), channel_id=1, source_target_pairs={{0,28},{4,24},{8,20},{12,16},{16,12},{20,8},{24,4},{28,0},{1,29},{... | collective-permute-start | bytes 983048 | tf_op jit(solution)/shard_map/ppermute | solution.py:36
  250.2 55.3 %copy-start.11 = (bf16[128,2560]{1,0:T(8,128)(2,1)S(1)}, bf16[128,2560]{1,0:T(8,128)(2,1)}, u32[]{:S(2)}) copy-start(bf16[128,2560]{1,0:T(8,128)(2,1)} %get-tuple-element.49) | copy-start | bytes 1966084
  250.2 19.6 %collective-permute-start.36 = (bf16[128,2560]{1,0:T(8,128)(2,1)}, bf16[128,2560]{1,0:T(8,128)(2,1)S(1)}, u32[]{:S(2)}, u32[]{:S(2)}) collective-permute-start(bf16[128,2560]{1,0:T(8,128)(2,1)} %get-tuple-element.51), channel_id=1, source_target_pairs={{0,1},{4,5},{8,9},{12,13},{16,17},{20,21},{24,25},{28,29}} | collective-permute-start | bytes 1966088 | tf_op jit(solution)/shard_map/ppermute | solution.py:40
  254.4 15.4 %collective-permute-start.38 = (bf16[128,2560]{1,0:T(8,128)(2,1)}, bf16[128,2560]{1,0:T(8,128)(2,1)S(1)}, u32[]{:S(2)}, u32[]{:S(2)}) collective-permute-start(bf16[128,2560]{1,0:T(8,128)(2,1)} %get-tuple-element.52), channel_id=1, source_target_pairs={{3,2},{7,6},{11,10},{15,14},{19,18},{23,22},{27,26},{31,30}} | collective-permute-start | bytes 1966088 | tf_op jit(solution)/shard_map/ppermute | solution.py:40
  255.1 28.7 %collective-permute-start.40 = (bf16[128,2560]{1,0:T(8,128)(2,1)}, bf16[128,2560]{1,0:T(8,128)(2,1)S(1)}, u32[]{:S(2)}, u32[]{:S(2)}) collective-permute-start(bf16[128,2560]{1,0:T(8,128)(2,1)} %get-tuple-element.52), channel_id=1, source_target_pairs={{0,1},{1,2},{2,3},{4,5},{5,6},{6,7},{8,9},{9,10},{10,11},{12,13},{... | collective-permute-start | bytes 1966088 | tf_op jit(solution)/shard_map/ppermute | solution.py:40
  256.4 27.4 %collective-permute-start.41 = (bf16[128,2560]{1,0:T(8,128)(2,1)}, bf16[128,2560]{1,0:T(8,128)(2,1)S(1)}, u32[]{:S(2)}, u32[]{:S(2)}) collective-permute-start(bf16[128,2560]{1,0:T(8,128)(2,1)} %get-tuple-element.51), channel_id=1, source_target_pairs={{1,0},{2,1},{3,2},{5,4},{6,5},{7,6},{9,8},{10,9},{11,10},{13,12},{... | collective-permute-start | bytes 1966088 | tf_op jit(solution)/shard_map/ppermute | solution.py:40
  271.1 26.4 %collective-permute-start.37 = (bf16[128,2560]{1,0:T(8,128)(2,1)S(1)}, bf16[128,2560]{1,0:T(8,128)(2,1)S(1)}, u32[]{:S(2)}, u32[]{:S(2)}) collective-permute-start(bf16[128,2560]{1,0:T(8,128)(2,1)S(1)} %get-tuple-element.53), channel_id=1, source_target_pairs={{0,2},{1,3},{4,6},{5,7},{8,10},{9,11},{12,14},{13,15},{16,18},{17,... | collective-permute-start | bytes 1966088 | tf_op jit(solution)/shard_map/ppermute | solution.py:40
  272.4 33.0 %collective-permute-start.39 = (bf16[128,2560]{1,0:T(8,128)(2,1)S(1)}, bf16[128,2560]{1,0:T(8,128)(2,1)S(1)}, u32[]{:S(2)}, u32[]{:S(2)}) collective-permute-start(bf16[128,2560]{1,0:T(8,128)(2,1)S(1)} %get-tuple-element.54), channel_id=1, source_target_pairs={{2,0},{3,1},{6,4},{7,5},{10,8},{11,9},{14,12},{15,13},{18,16},{19,... | collective-permute-start | bytes 1966088 | tf_op jit(solution)/shard_map/ppermute | solution.py:40
  (18 other events, 114.5 us)
where the time goes:
time: 307 us
  waiting for transfers between devices  164 us (53%)
  Pallas kernels  64 us (21%)
  starting transfers between devices  61.6 us (20%)
  local copies, waits for them, and re-layouts  8.5 us (3%)
  other arithmetic  7.61 us (2%)
    ppermute x18, waiting for transfers between devices, hop(): return lax.ppermute(block, 'tensor', [(i, i + step) for i in sources])  91 us
    ppermute x24, waiting for transfers between devices, swap(): return lax.ppermute(block, axis, [(i, i ^ bits) for i in range(size)])  73.5 us
    pallas_call x6, Pallas kernels, call(): pl.pallas_call(kernel, out_shape=[jax.ShapeDtypeStruct(shape, kind) for s...  64 us
    ppermute x18, starting transfers between devices, hop(): return lax.ppermute(block, 'tensor', [(i, i + step) for i in sources])  40.3 us
    ppermute x24, starting transfers between devices, swap(): return lax.ppermute(block, axis, [(i, i ^ bits) for i in range(size)])  21.3 us
  transfers between devices with their start and end apart: 42, of which 18 were waited for; matrix products, arithmetic and copies ran while one was open for 3% of the time, Pallas kernels for 18%

commit v1 on v0

--- a/solution.py
+++ b/solution.py
@@ -11,6 +11,7 @@
 F32 = jnp.float32
 BF16 = jnp.bfloat16
 LANES = 128
+PARTS = 2
 VMEM_BYTES = 56 * 1024 * 1024
 VMEM_SPEC = pl.BlockSpec(memory_space=pltpu.VMEM)
 ANY_SPEC = pl.BlockSpec(memory_space=pl.ANY)
@@ -48,32 +49,45 @@
     return len(bits_of(offset >> 1)) > 1
 
 
-def line_gather(block, count, direct):
-    ups, downs = [], []
+def line_all(block, count):
+    parts = [block] + [0] * (count - 1)
     for back in range(1, count):
-        if back <= direct:
-            ups.append(hop(block, back, range(count - back)))
-            downs.append(hop(block, -back, range(back, count)))
-        else:
-            ups.append(hop(ups[-1], 1, range(back - 1, count - 1)))
-            downs.append(hop(downs[-1], -1, range(1, count - back + 1)))
-    return ups, downs
+        parts[back] += hop(block, back, range(count - back))
+        parts[count - back] += hop(block, -back, range(back, count))
+    return parts
+
+
+def line_gather(block, count):
+    if count < 4:
+        return {
+            k: [(part, range(count))] for k, part in enumerate(line_all(block, count)) if k
+        }
+    got = {k: [] for k in range(1, count)}
+    middle = (count // 2 - 1, count // 2)
+    up = hop(block, 2, range(count - 2))
+    down = hop(block, -2, range(2, count))
+    got[2].append((up, list(range(2, count))))
+    got[count - 2].append((down, list(range(count - 2))))
+    outer = [i for i in range(count - 1) if i != middle[0]]
+    got[1].append((hop(block, 1, outer), [i + 1 for i in outer]))
+    outer = [i + 1 for i in outer]
+    got[count - 1].append((hop(block, -1, outer), [i - 1 for i in outer]))
+    block, up, down = lax.optimization_barrier((block, up, down))
+    for back in range(3, count):
+        up = hop(up, 1, range(back - 1, count - 1))
+        down = hop(down, -1, range(1, count - back + 1))
+        got[back].append((up, list(range(back, count))))
+        got[count - back].append((down, list(range(count - back))))
+    got[1].append((hop(block, 1, middle[:1]), [middle[1]]))
+    got[count - 1].append((hop(block, -1, middle[1:]), [middle[0]]))
+    return got
 
 
 def line_scatter(part, count):
-    up = down = None
     got = []
     for back in range(count - 1, 0, -1):
-        first, second = part[count - back], part[back]
-        if up is not None:
-            first, second = add(first, up), add(second, down)
-            up = down = None
-        if back < 3:
-            got.append(hop(first, back, range(count - back)))
-            got.append(hop(second, -back, range(back, count)))
-        else:
-            up = hop(first, 1, range(count - back))
-            down = hop(second, -1, range(back, count))
+        got.append(hop(part[count - back], back, range(count - back)))
+        got.append(hop(part[back], -back, range(back, count)))
     return add(part[0], *got)
 
 
@@ -87,13 +101,11 @@
     for offset in range(2, size, 2):
         if offset not in held:
             low, high = bits_of(offset)[0], bits_of(offset)[-1]
-            held[offset] = jnp.concatenate(
-                [
-                    swap(held[offset ^ low][:, :half], "expert", low),
-                    swap(held[offset ^ high][:, half:], "expert", high),
-                ],
-                axis=1,
-            )
+            pieces = [
+                swap(held[offset ^ low][:, :half], "expert", low),
+                swap(held[offset ^ high][:, half:], "expert", high),
+            ]
+            held[offset] = jnp.concatenate(pieces, axis=1)
     return {o: b for o, b in held.items() if far(o)}
 
 
@@ -138,26 +150,26 @@
     return wait
 
 
-def columns_in(source, target, tiles, sem):
+def columns_in(source, target, tiles, sem, base=0):
     tile = target.shape[-1] // tiles
 
     def copy(n):
-        at = cut(n, tile)
-        return pltpu.make_async_copy(source.at[:, at], target.at[:, at], sem.at[n])
+        from_at = pl.ds(pl.multiple_of(base + n * tile, LANES), tile)
+        return pltpu.make_async_copy(source.at[:, from_at], target.at[:, cut(n, tile)], sem.at[n])
 
     each(tiles, lambda n: copy(n).start())
     return lambda n: copy(n).wait()
 
 
-def rows_out(source, targets, tiles, sem):
-    tile = source.shape[-1] // tiles
+def rows_out(source, targets, tiles, sem, base=0):
+    tile = targets[0].shape[-1] // tiles
 
     def copies(n):
-        at, start = cut(n, tile), 0
+        at, start = pl.ds(pl.multiple_of(base + n * tile, LANES), tile), 0
         for k, target in enumerate(targets):
             rows = target.shape[0]
             yield pltpu.make_async_copy(
-                source.at[pl.ds(start, rows), at], target.at[:, at], sem.at[k, n]
+                source.at[pl.ds(start, rows), at], target.at[:, cut(n, tile)], sem.at[k, n]
             )
             start += rows
 
@@ -180,9 +192,9 @@
     return out + list(refs[at:])
 
 
-def pick_kernel(count, lengths, *refs):
-    own, ups, downs, slot, outs, group, x, pick, made, sem_in, sem_out, sem_group = take(
-        refs, None, count - 1, count - 1, None, len(lengths), None
+def pick_kernel(count, sources, lengths, *refs):
+    own, parts, slot, outs, group, x, pick, made, sem_in, sem_out, sem_group = take(
+        refs, None, len(sources), None, len(lengths), None
     )
     place = lax.axis_index("tensor")
     rows = own.shape[0]
@@ -193,14 +205,12 @@
         return pltpu.make_async_copy(ref, x.at[pl.ds(k * rows, rows), :], sem_in.at[k])
 
     into(own, 0).start()
-    for k in range(1, count):
-        @pl.when(place >= k)
+    for part, (k, places) in zip(parts, sources):
+        here = functools.reduce(jnp.logical_or, [place == p for p in places])
+
+        @pl.when(here)
         def _():
-            into(ups[k - 1], k).start()
-
-        @pl.when(place < k)
-        def _():
-            into(downs[count - k - 1], k).start()
+            into(part, k).start()
 
     places = lax.broadcasted_iota(jnp.int32, pick.shape, 0)
     pick[...] = (places == slot[...]).astype(F32).astype(BF16)
@@ -222,14 +232,15 @@
 
 def expert_kernel(count, *refs):
     blocks, gate_w, up_w, down_w, outs, x, gate, upper, down, hidden, made, *sems = take(
-        refs, count, None, None, None, count
+        refs, count, None, None, None, PARTS * count
     )
     inner, outer = down.shape
-    ins, os = tiles_of(inner // 2), tiles_of(outer)
+    ins, os = tiles_of(inner // 2), tiles_of(outer // PARTS)
+    tile = outer // PARTS // os
     wait_x = stack(blocks, x, sems[0])
     wait_gate = columns_in(gate_w.at[0], gate, ins, sems[1])
     wait_up = columns_in(up_w.at[0], upper, ins, sems[2])
-    wait_down = columns_in(down_w.at[0], down, os, sems[3])
+    wait_down = columns_in(down_w.at[0], down, PARTS * os, sems[3])
     wait_x()
 
     def one(n):
@@ -240,16 +251,22 @@
         hidden[:, at] = (jax.nn.silu(g) * dot(x[...], upper[:, at])).astype(BF16)
 
     each(ins, one)
-    begin, finish = rows_out(made, outs, os, sems[4])
-
-    def two(n):
-        at = cut(n, outer // os)
-        wait_down(n)
-        made[:, at] = dot(hidden[...], down[:, at]).astype(BF16)
-        begin(n)
-
-    each(os, two)
-    finish()
+    finishes = []
+    for c in range(PARTS):
+        begin, finish = rows_out(
+            made, outs[c * count:(c + 1) * count], os, sems[4].at[c], c * outer // PARTS
+        )
+        finishes.append(finish)
+
+        def two(n):
+            wait_down(c * os + n)
+            at = pl.ds(pl.multiple_of((c * os + n) * tile, LANES), tile)
+            made[:, at] = dot(hidden[...], down[:, at]).astype(BF16)
+            begin(n)
+
+        each(os, two)
+    for finish in finishes:
+        finish()
 
 
 def load_pairs(refs, offsets, start, width, held, sem, core):
@@ -341,12 +358,12 @@
         copy.wait()
 
 
-def combine_kernel(count, parts, *refs):
+def combine_kernel(count, parts, base, *refs):
     blocks, notes, source, outs, x, shared, made, *sems = take(refs, count, None, None, parts)
     wait_x = stack(blocks, x, sems[0])
     total, width = x.shape
     tiles = tiles_of(width)
-    wait_shared = columns_in(source, shared, tiles, sems[1])
+    wait_shared = columns_in(source, shared, tiles, sems[1], base)
     rows = notes.shape[0]
     places = lax.broadcasted_iota(jnp.int32, (rows, total), 1)
     pick = (places == notes[:, 0:1].astype(jnp.int32)).astype(F32).astype(BF16)
@@ -381,13 +398,14 @@
     return pltpu.SemaphoreType.DMA(shape)
 
 
-def pick_rows(own, ups, downs, slot, lengths):
-    count, (rows, width) = len(ups) + 1, own.shape
+def pick_rows(own, got, slot, lengths):
+    sources = [(k, places) for k in got for _, places in got[k]]
+    count, (rows, width) = len(got) + 1, own.shape
     group, total = rows * count, sum(lengths)
     tiles = tiles_of(width)
-    ins = [own, *ups, *downs, slot[None, :]]
+    ins = [own, *[block for k in got for block, _ in got[k]], slot[None, :]]
     out = call(
-        functools.partial(pick_kernel, count, lengths),
+        functools.partial(pick_kernel, count, sources, lengths),
         ins,
         {len(ins) - 1},
         [((length, width), BF16) for length in lengths] + [((group, width), BF16)],
@@ -407,13 +425,13 @@
 
 def expert_rows(blocks, w_gate, w_up, w_down):
     inner, width = w_down.shape[1:]
-    rows = sum(b.shape[0] for b in blocks)
-    ins, outs = tiles_of(inner // 2), tiles_of(width)
-    return call(
-        functools.partial(expert_kernel, len(blocks)),
+    rows, count = sum(b.shape[0] for b in blocks), len(blocks)
+    ins, outs = tiles_of(inner // 2), tiles_of(width // PARTS)
+    made = call(
+        functools.partial(expert_kernel, count),
         [*blocks, w_gate, w_up, w_down],
         (),
-        [(b.shape, BF16) for b in blocks],
+        [((b.shape[0], width // PARTS), BF16) for b in blocks] * PARTS,
         [
             pltpu.VMEM((rows, width), BF16),
             pltpu.VMEM((width, inner), BF16),
@@ -421,15 +439,16 @@
             pltpu.VMEM((inner, width), BF16),
             pltpu.VMEM((rows, inner), BF16),
             pltpu.VMEM((rows, width), BF16),
-            dma(len(blocks)),
+            dma(count),
             dma(ins),
             dma(ins),
-            dma(outs),
-            dma(len(blocks), outs),
+            dma(PARTS * outs),
+            dma(PARTS, count, outs),
         ],
         6 * rows * inner * width,
         (4 * rows + 6 * inner) * width,
     )
+    return [made[c * count:(c + 1) * count] for c in range(PARTS)]
 
 
 def shared_near(group, blocks, inner):
@@ -482,13 +501,13 @@
     )[0]
 
 
-def combine(blocks, notes, shared, parts):
-    group, width = shared.shape
+def combine(blocks, notes, shared, parts, base):
+    group, width = shared.shape[0], blocks[0].shape[1]
     total = sum(b.shape[0] for b in blocks)
     tiles = tiles_of(width)
     ins = [*blocks, notes, shared]
     return call(
-        functools.partial(combine_kernel, len(blocks), parts),
+        functools.partial(combine_kernel, len(blocks), parts, base),
         ins,
         {len(blocks)},
         [((group // parts, width), BF16)] * parts,
@@ -510,22 +529,18 @@
     count = lax.axis_size("tensor")
     me = lax.axis_index("expert")
     place = lax.axis_index("tensor")
-    rows, _ = tokens.shape
+    rows, width = tokens.shape
     group = rows * count
     experts = w_gate.shape[0] * size
     cap = 2 * group // experts
     half = cap // 2
     inner = s_gate.shape[1]
 
-    ups, downs = line_gather(tokens, count, 2)
+    gathered = line_gather(tokens, count)
     s_all = jnp.concatenate([s_gate, s_up, s_down.T], axis=1)
     near = {bit: swap(s_all, "expert", bit) for bit in bits_of((size - 1) & ~1)}
     notes = jnp.concatenate([expert_ids.astype(F32).T, gates[None, :]], axis=0)
-    above, below = line_gather(notes, count, count)
-    parts = [notes]
-    for back in range(1, count):
-        parts.append(jnp.where(place >= back, above[back - 1], below[count - back - 1]))
-    notes = jnp.concatenate(parts, axis=1)
+    notes = jnp.concatenate(line_all(notes, count), axis=1)
     ids, scale = notes[0].astype(jnp.int32), notes[1]
 
     index = jnp.arange(group, dtype=jnp.int32)
@@ -550,32 +565,38 @@
     fars = [o for o in range(size) if far(o)]
     nears = [o for o in range(2, size) if not far(o)]
 
-    sent, tokens = pick_rows(tokens, ups, downs, slot, lengths)
+    sent, tokens = pick_rows(tokens, gathered, slot, lengths)
     got = {0: sent[0]}
     for o in fars:
         got[o] = swap(sent[o], "expert", o)
-    for o in [1] + nears:
+    for o in nears:
         got[o] = swap(sent[o], "expert", o)
+    got[1] = swap(sent[1], "expert", 1)
     blocks = with_partner({0: s_all, **near})
     part = None
     if 2 * s_all.shape[0] % LANES == 0:
         part = shared_near(tokens, blocks, inner)
+    own = expert_rows([got[0], got[1]], w_gate, w_up, w_down)
+    home = [{0: own[c][0]} for c in range(PARTS)]
+    for c in range(PARTS):
+        home[c][1] = swap(own[c][1], "expert", 1)
     mine = jnp.concatenate([got[o] for o in fars])
     mine, *ready = lax.optimization_barrier((mine, *near.values()))
     near = dict(zip(near, ready))
     other = swap(mine, "tensor", 1)
-    blocks = {**blocks, **with_partner(far_blocks(near, s_all, size))}
-
-    home = {}
-    home[0], made, mine, theirs = expert_rows([got[0], got[1], mine, other], w_gate, w_up, w_down)
-    theirs = swap(theirs, "tensor", 1)
-    mine = add(mine, theirs)
-    home[1] = swap(made, "expert", 1)
-    for k, o in enumerate(fars):
-        home[o] = swap(mine[k * half:(k + 1) * half], "expert", o)
+    late = far_blocks(near, s_all, size)
+    made = expert_rows([mine, other], w_gate, w_up, w_down)
+    pair = []
+    for c in range(PARTS):
+        pair.append((made[c][0], swap(made[c][1], "tensor", 1)))
     made = expert_rows([got[o] for o in nears], w_gate, w_up, w_down)
-    for k, o in enumerate(nears):
-        home[o] = swap(made[k], "expert", o)
+    for c in range(PARTS):
+        mine = add(*pair[c])
+        for k, o in enumerate(fars):
+            home[c][o] = swap(mine[k * half:(k + 1) * half], "expert", o)
+        for k, o in enumerate(nears):
+            home[c][o] = swap(made[c][k], "expert", o)
+    blocks = {**blocks, **with_partner(late)}
 
     if part is not None:
         shared = shared_far(part, tokens, blocks, inner)
@@ -587,8 +608,11 @@
         shared = dot_t(shared, s_out)
 
     notes = jnp.stack([slot.astype(F32), scale], axis=1)
-    parts = combine([home[o] for o in range(size)], notes, shared, count)
-    return line_scatter(parts, count)
+    outs = []
+    for c in range(PARTS):
+        parts = combine([home[c][o] for o in range(size)], notes, shared, count, c * width // PARTS)
+        outs.append(line_scatter(parts, count))
+    return jnp.concatenate(outs, axis=1)
 
 
 def solution(mesh):

time: 307 us -> 342 us (1.11); the launches traced: 307 us -> 337 us
  starting transfers between devices: 61.6 us -> 92.5 us
  waiting for transfers between devices: 164 us -> 152 us
  Pallas kernels: 64 us -> 75.8 us
    ppermute x18 -> x26, starting transfers between devices: 40.3 us -> 64.4 us  [hop(): return lax.ppermute(block, 'tensor', [(i, i + step) for i in sources])]
    ppermute x18 -> x26, waiting for transfers between devices: 91 us -> 71.5 us  [hop(): return lax.ppermute(block, 'tensor', [(i, i + step) for i in sources])]
    pallas_call x6 -> x8, Pallas kernels: 64 us -> 75.8 us  [call(): pl.pallas_call(kernel, out_shape=[jax.ShapeDtypeStruct(shape, kind) for s...]
    ppermute x24 -> x32, waiting for transfers between devices: 73.5 us -> 80.5 us  [swap(): return lax.ppermute(block, axis, [(i, i ^ bits) for i in range(size)])]
    ppermute x24 -> x32, starting transfers between devices: 21.3 us -> 28.1 us  [swap(): return lax.ppermute(block, axis, [(i, i ^ bits) for i in range(size)])]
  transfers between devices with their start and end apart: 42 -> 58, of which waited for: 18 -> 18; matrix products, arithmetic and copies ran while one was open for 3% -> 4% of each run, Pallas kernels for 18% -> 23%
where the time goes in v1:
time: 342 us; the launch traced here: 337 us
  waiting for transfers between devices  152 us (44%)
  starting transfers between devices  92.5 us (27%)
  Pallas kernels  75.8 us (22%)
  local copies, waits for them, and re-layouts  11 us (3%)
  other arithmetic  4.36 us (1%)
    ppermute x32, waiting for transfers between devices, swap(): return lax.ppermute(block, axis, [(i, i ^ bits) for i in range(size)])  80.5 us
    pallas_call x8, Pallas kernels, call(): pl.pallas_call(kernel, out_shape=[jax.ShapeDtypeStruct(shape, kind) for s...  75.8 us
    ppermute x26, waiting for transfers between devices, hop(): return lax.ppermute(block, 'tensor', [(i, i + step) for i in sources])  71.5 us
    ppermute x26, starting transfers between devices, hop(): return lax.ppermute(block, 'tensor', [(i, i + step) for i in sources])  64.4 us
    ppermute x32, starting transfers between devices, swap(): return lax.ppermute(block, axis, [(i, i ^ bits) for i in range(size)])  28.1 us
  transfers between devices with their start and end apart: 58, of which 18 were waited for; matrix products, arithmetic and copies ran while one was open for 4% of the time, Pallas kernels for 23%

profile of v1, /device:TPU:0, one launch (start us, length us, event | category | flops | bytes accessed | tf_op | source)
XLA Modules:
  0.0 336.7 jit_solution(11206228236321105699)
XLA Ops:
  1.3 6.1 %collective-permute-start.1 = (bf16[128,2560]{1,0:T(8,128)(2,1)}, bf16[128,2560]{1,0:T(8,128)(2,1)S(1)}, u32[]{:S(2)}, u32[]{:S(2)}) collective-permute-start(bf16[128,2560]{1,0:T(8,128)(2,1)} %refs_0_.1), channel_id=1, source_target_pairs={{0,2},{1,3},{4,6},{5,7},{8,10},{9,11},{12,14},{13,15},{16,18},{17,... | collective-permute-start | bytes 1966088 | tf_op jit(solution)/shard_map/ppermute | solution.py:41
  7.4 1.7 pad_maximum_fusion.refs_1_.refs_2_
  9.1 2.5 collective-permute-start.27
  11.6 4.3 %collective-permute-start = (bf16[128,2560]{1,0:T(8,128)(2,1)S(1)}, bf16[128,2560]{1,0:T(8,128)(2,1)}, u32[]{:S(2)}, u32[]{:S(2)}) collective-permute-start(bf16[128,2560]{1,0:T(8,128)(2,1)S(1)} %copy-done.24), channel_id=1, source_target_pairs={{0,1},{2,3},{4,5},{6,7},{8,9},{10,11},{12,13},{14,15},{16,17},{18,... | collective-permute-start | bytes 1966088 | tf_op jit(solution)/shard_map/ppermute | solution.py:41
  17.2 17.2 %collective-permute-done.2.refs_5_ = bf16[128,2560]{1,0:T(8,128)(2,1)S(1)} collective-permute-done((bf16[128,2560]{1,0:T(8,128)(2,1)}, bf16[128,2560]{1,0:T(8,128)(2,1)S(1)}, u32[]{:S(2)}, u32[]{:S(2)}) %collective-permute-start.2) | collective-permute-done | bytes 655392 | tf_op jit(solution)/shard_map/ppermute | solution.py:41
  35.8 7.6 %collective-permute-start.13 = (f32[2,128]{1,0:T(2,128)S(1)}, f32[2,128]{1,0:T(2,128)S(1)}, u32[]{:S(2)}, u32[]{:S(2)}) collective-permute-start(f32[2,128]{1,0:T(2,128)S(1)} %pad_maximum_fusion.5), channel_id=1, source_target_pairs={{0,3},{4,7},{8,11},{12,15},{16,19},{20,23},{24,27},{28,31}} | collective-permute-start | bytes 3080 | tf_op jit(solution)/shard_map/ppermute | solution.py:41
  45.9 13.7 %collective-permute-done.12 = f32[2,128]{1,0:T(2,128)S(1)} collective-permute-done((f32[2,128]{1,0:T(2,128)S(1)}, f32[2,128]{1,0:T(2,128)S(1)}, u32[]{:S(2)}, u32[]{:S(2)}) %collective-permute-start.12) | collective-permute-done | bytes 1056 | tf_op jit(solution)/shard_map/ppermute | solution.py:41
  60.9 5.1 %collective-permute-done.11 = f32[2,128]{1,0:T(2,128)S(1)} collective-permute-done((f32[2,128]{1,0:T(2,128)S(1)}, f32[2,128]{1,0:T(2,128)S(1)}, u32[]{:S(2)}, u32[]{:S(2)}) %collective-permute-start.11) | collective-permute-done | bytes 1056 | tf_op jit(solution)/shard_map/ppermute | solution.py:41
  65.9 1.6 collective-permute-start.10
  70.2 6.0 %collective-permute-done.9 = f32[2,128]{1,0:T(2,128)S(1)} collective-permute-done((f32[2,128]{1,0:T(2,128)S(1)}, f32[2,128]{1,0:T(2,128)S(1)}, u32[]{:S(2)}, u32[]{:S(2)}) %collective-permute-start.9) | collective-permute-done | bytes 1056 | tf_op jit(solution)/shard_map/ppermute | solution.py:41
  78.7 2.2 collective-permute-start.26
  85.3 7.1 %shard_map.91 = (bf16[128,2560]{1,0:T(8,128)(2,1)}, bf16[128,2560]{1,0:T(8,128)(2,1)}, bf16[128,2560]{1,0:T(8,128)(2,1)}, bf16[128,2560]{1,0:T(8,128)(2,1)}, bf1...) custom-call(bf16[128,2560]{1,0:T(8,128)(2,1)} %refs_0_.1, ...), custom_call_target="tpu_custom_call" | custom-call | flops 2348810240 | bytes 9830400 | tf_op jit(solution)/shard_map/pallas_call | solution.py:386
  94.5 37.6 %collective-permute-done.24 = bf16[64,2560]{1,0:T(8,128)(2,1)S(1)} collective-permute-done((bf16[64,2560]{1,0:T(8,128)(2,1)}, bf16[64,2560]{1,0:T(8,128)(2,1)S(1)}, u32[]{:S(2)}, u32[]{:S(2)}) %collective-permute-start.24) | collective-permute-done | bytes 327712 | tf_op jit(solution)/shard_map/ppermute | solution.py:37
  132.0 6.2 %collective-permute-done.25 = bf16[64,2560]{1,0:T(8,128)(2,1)S(1)} collective-permute-done((bf16[64,2560]{1,0:T(8,128)(2,1)}, bf16[64,2560]{1,0:T(8,128)(2,1)S(1)}, u32[]{:S(2)}, u32[]{:S(2)}) %collective-permute-start.25) | collective-permute-done | bytes 327712 | tf_op jit(solution)/shard_map/ppermute | solution.py:37
  141.4 2.4 slice.28
  145.1 7.6 %collective-permute-done.16.refs_0_ = bf16[128,2560]{1,0:T(8,128)(2,1)} collective-permute-done((bf16[128,2560]{1,0:T(8,128)(2,1)}, bf16[128,2560]{1,0:T(8,128)(2,1)}, u32[]{:S(2)}, u32[]{:S(2)}) %collective-permute-start.16) | collective-permute-done | bytes 655392 | tf_op jit(solution)/shard_map/ppermute | solution.py:37
  152.7 7.2 %collective-permute-done.17.refs_1_ = bf16[128,2560]{1,0:T(8,128)(2,1)} collective-permute-done((bf16[128,2560]{1,0:T(8,128)(2,1)}, bf16[128,2560]{1,0:T(8,128)(2,1)}, u32[]{:S(2)}, u32[]{:S(2)}) %collective-permute-start.17) | collective-permute-done | bytes 655392 | tf_op jit(solution)/shard_map/ppermute | solution.py:37
  160.0 2.0 collective-permute-start.28
  162.3 7.3 %collective-permute-done.19.refs_3_ = bf16[128,2560]{1,0:T(8,128)(2,1)} collective-permute-done((bf16[128,2560]{1,0:T(8,128)(2,1)}, bf16[128,2560]{1,0:T(8,128)(2,1)}, u32[]{:S(2)}, u32[]{:S(2)}) %collective-permute-start.19) | collective-permute-done | bytes 655392 | tf_op jit(solution)/shard_map/ppermute | solution.py:37
  169.6 1.8 collective-permute-start.35
  171.4 14.7 %shard_map.93 = (bf16[128,1280]{1,0:T(8,128)(2,1)}, bf16[128,1280]{1,0:T(8,128)(2,1)}, bf16[128,1280]{1,0:T(8,128)(2,1)}, bf16[128,1280]{1,0:T(8,128)(2,1)}, bf1...) custom-call(bf16[128,2560]{1,0:T(8,128)(2,1)} %collective-permute-don, ...), custom_call_target="tpu_custom_call" | custom-call | flops 8053063680 | bytes 20971520 | tf_op jit(solution)/shard_map/pallas_call | solution.py:386
  186.2 10.0 %shard_map.94 = (bf16[128,1280]{1,0:T(8,128)(2,1)}, bf16[128,1280]{1,0:T(8,128)(2,1)}, bf16[128,1280]{1,0:T(8,128)(2,1)}, bf16[128,1280]{1,0:T(8,128)(2,1)}) custom-call(bf16[128,2560]{1,0:T(8,128)(2,1)} %copy-done.3, bf16[128,2560]{1,0:T(8,128)(2,1)} %collective-permute-done.28.refs_1_, bf16[1,2560,1024]{2,1,0:T(8,128)(2,1)} %refs_2_.3, ...), custom_call_target="tpu_custom_call" | custom-call | flops 4026531840 | bytes 18350080 | tf_op jit(solution)/shard_map/pallas_call | solution.py:386
  196.8 2.2 constant_dynamic-update-slice_fusion.1
  199.0 2.3 collective-permute-start.49
  201.3 2.2 constant_dynamic-update-slice_fusion.refs_8_
  203.5 10.1 %shard_map.92 = (bf16[128,1280]{1,0:T(8,128)(2,1)}, bf16[128,1280]{1,0:T(8,128)(2,1)}, bf16[128,1280]{1,0:T(8,128)(2,1)}, bf16[128,1280]{1,0:T(8,128)(2,1)}) custom-call(bf16[128,2560]{1,0:T(8,128)(2,1)} %get-tuple-element.47.refs_0_, bf16[128,2560]{1,0:T(8,128)(2,1)} %collective-permute-done.14.refs_1_, bf16[1,2560,1024]{2,1,0:T(8,128)(2,1)} %refs_2_.3, ...), custom_call_target="tpu_custom_call" | custom-call | flops 4026531840 | bytes 18350080 | tf_op jit(solution)/shard_map/pallas_call | solution.py:386
  213.8 10.0 %collective-permute-done.29 = bf16[128,1280]{1,0:T(8,128)(2,1)S(1)} collective-permute-done((bf16[128,1280]{1,0:T(8,128)(2,1)S(1)}, bf16[128,1280]{1,0:T(8,128)(2,1)S(1)}, u32[]{:S(2)}, u32[]{:S(2)}) %collective-permute-start.29) | collective-permute-done | bytes 327712 | tf_op jit(solution)/shard_map/ppermute | solution.py:37
  224.2 1.7 collective-permute-start.46
  225.9 1.5 collective-permute-start.47
  227.5 10.8 %shard_map.95.refs_0_ = f32[512,2048]{1,0:T(8,128)} custom-call(bf16[512,2560]{1,0:T(8,128)(2,1)} %get-tuple-element.64.refs_0_.refs_1_, bf16[320,3072]{1,0:T(8,128)(2,1)} %copy-done, bf16[320,3072]{1,0:T(8,128)(2,1)} %copy-done.1, bf16[320,3072]{1,0:T(8,128)(2,1)} %collective-permute-done.26.refs_3_.refs_4_, ...), custom_call_target="tpu_custom_call" | custom-call | flops 4026531840 | bytes 12058624 | tf_op jit(solution)/shard_map/pallas_call | solution.py:386
  238.8 2.1 collective-permute-done.46.refs_3_
  240.9 1.9 collective-permute-start.48
  242.8 2.3 collective-permute-start.50
  245.1 10.1 %shard_map.96.refs_9_ = f32[512,2560]{1,0:T(8,128)} custom-call(f32[512,2048]{1,0:T(8,128)} %shard_map.95.refs_0_, bf16[512,2560]{1,0:T(8,128)(2,1)} %get-tuple-element.64.refs_0_.refs_1_, bf16[320,3072]{1,0:T(8,128)(2,1)} %copy-done, bf16[320,3072]{1,0:T(8,128)(2,1)} %copy-done.1, bf16[320,3072]{1,0:T(8,128)(2,1)} %collective-permute-done.26.refs_3_.refs_4_, ...), custom_call_target="tpu_custom_call" | custom-call | flops 4026531840 | bytes 14680064 | tf_op jit(solution)/shard_map/pallas_call | solution.py:386
  255.2 2.5 collective-permute-done.48.refs_5_
  257.8 1.8 collective-permute-start.22
  260.2 6.5 %shard_map.98 = (bf16[128,1280]{1,0:T(8,128)(2,1)}, bf16[128,1280]{1,0:T(8,128)(2,1)}, bf16[128,1280]{1,0:T(8,128)(2,1)}, bf16[128,1280]{1,0:T(8,128)(2,1)}) custom-call(bf16[128,1280]{1,0:T(8,128)(2,1)} %get-tuple-element.71.refs_0_, bf16[128,1280]{1,0:T(8,128)(2,1)} %copy-done.10, bf16[128,1280]{1,0:T(8,128)(2,1)} %copy-done.12, ...), custom_call_target="tpu_custom_call" | custom-call | flops 1174405120 | bytes 6225920 | tf_op jit(solution)/shard_map/pallas_call | solution.py:386
  268.0 4.9 %collective-permute-start.52 = (bf16[128,1280]{1,0:T(8,128)(2,1)}, bf16[128,1280]{1,0:T(8,128)(2,1)S(1)}, u32[]{:S(2)}, u32[]{:S(2)}) collective-permute-start(bf16[128,1280]{1,0:T(8,128)(2,1)} %get-tuple-element.80), channel_id=1, source_target_pairs={{0,3},{4,7},{8,11},{12,15},{16,19},{20,23},{24,27},{28,31}} | collective-permute-start | bytes 983048 | tf_op jit(solution)/shard_map/ppermute | solution.py:41
  273.0 1.6 collective-permute-start.31
  275.1 8.2 %collective-permute-start.56 = (bf16[128,1280]{1,0:T(8,128)(2,1)}, bf16[128,1280]{1,0:T(8,128)(2,1)S(1)}, u32[]{:S(2)}, u32[]{:S(2)}) collective-permute-start(bf16[128,1280]{1,0:T(8,128)(2,1)} %get-tuple-element.81), channel_id=1, source_target_pairs={{0,1},{1,2},{2,3},{4,5},{5,6},{6,7},{8,9},{9,10},{10,11},{12,13},{... | collective-permute-start | bytes 983048 | tf_op jit(solution)/shard_map/ppermute | solution.py:41
  286.0 6.6 %shard_map.97 = (bf16[128,1280]{1,0:T(8,128)(2,1)}, bf16[128,1280]{1,0:T(8,128)(2,1)}, bf16[128,1280]{1,0:T(8,128)(2,1)}, bf16[128,1280]{1,0:T(8,128)(2,1)}) custom-call(bf16[128,1280]{1,0:T(8,128)(2,1)} %get-tuple-element.49.refs_0_, bf16[128,1280]{1,0:T(8,128)(2,1)} %copy-done.8, bf16[128,1280]{1,0:T(8,128)(2,1)} %copy-done.9, ...), custom_call_target="tpu_custom_call" | custom-call | flops 1174405120 | bytes 6225920 | tf_op jit(solution)/shard_map/pallas_call | solution.py:386
  292.6 5.6 %collective-permute-start.54 = (bf16[128,1280]{1,0:T(8,128)(2,1)S(1)}, bf16[128,1280]{1,0:T(8,128)(2,1)S(1)}, u32[]{:S(2)}, u32[]{:S(2)}) collective-permute-start(bf16[128,1280]{1,0:T(8,128)(2,1)S(1)} %copy-done.39), channel_id=1, source_target_pairs={{0,2},{1,3},{4,6},{5,7},{8,10},{9,11},{12,14},{13,15},{16,18},{17,... | collective-permute-start | bytes 983048 | tf_op jit(solution)/shard_map/ppermute | solution.py:41
  299.5 3.4 %collective-permute-start.38 = (bf16[128,1280]{1,0:T(8,128)(2,1)}, bf16[128,1280]{1,0:T(8,128)(2,1)S(1)}, u32[]{:S(2)}, u32[]{:S(2)}) collective-permute-start(bf16[128,1280]{1,0:T(8,128)(2,1)} %get-tuple-element.68), channel_id=1, source_target_pairs={{0,3},{4,7},{8,11},{12,15},{16,19},{20,23},{24,27},{28,31}} | collective-permute-start | bytes 983048 | tf_op jit(solution)/shard_map/ppermute | solution.py:41
  302.9 1.9 collective-permute-start.42
  304.8 3.4 %collective-permute-done.55 = bf16[128,1280]{1,0:T(8,128)(2,1)S(1)} collective-permute-done((bf16[128,1280]{1,0:T(8,128)(2,1)}, bf16[128,1280]{1,0:T(8,128)(2,1)S(1)}, u32[]{:S(2)}, u32[]{:S(2)}) %collective-permute-start.55) | collective-permute-done | bytes 327712 | tf_op jit(solution)/shard_map/ppermute | solution.py:41
  310.8 11.0 %collective-permute-done.43 = bf16[128,1280]{1,0:T(8,128)(2,1)S(1)} collective-permute-done((bf16[128,1280]{1,0:T(8,128)(2,1)}, bf16[128,1280]{1,0:T(8,128)(2,1)S(1)}, u32[]{:S(2)}, u32[]{:S(2)}) %collective-permute-start.43) | collective-permute-done | bytes 327712 | tf_op jit(solution)/shard_map/ppermute | solution.py:41
  321.8 2.0 collective-permute-start.40
  324.1 11.4 %collective-permute-done.41 = bf16[128,1280]{1,0:T(8,128)(2,1)S(1)} collective-permute-done((bf16[128,1280]{1,0:T(8,128)(2,1)}, bf16[128,1280]{1,0:T(8,128)(2,1)S(1)}, u32[]{:S(2)}, u32[]{:S(2)}) %collective-permute-start.41) | collective-permute-done | bytes 327712 | tf_op jit(solution)/shard_map/ppermute | solution.py:41
  (188 shorter events, 36.1 us)
Async XLA Ops:
  0.0 34.4 %collective-permute-start.2 = (bf16[128,2560]{1,0:T(8,128)(2,1)}, bf16[128,2560]{1,0:T(8,128)(2,1)S(1)}, u32[]{:S(2)}, u32[]{:S(2)}) collective-permute-start(bf16[128,2560]{1,0:T(8,128)(2,1)} %refs_0_.1), channel_id=1, source_target_pairs={{2,0},{3,1},{6,4},{7,5},{10,8},{11,9},{14,12},{15,13},{18,16},{19,... | collective-permute-start | bytes 1966088 | tf_op jit(solution)/shard_map/ppermute | solution.py:41
  1.3 33.1 %collective-permute-start.1 = (bf16[128,2560]{1,0:T(8,128)(2,1)}, bf16[128,2560]{1,0:T(8,128)(2,1)S(1)}, u32[]{:S(2)}, u32[]{:S(2)}) collective-permute-start(bf16[128,2560]{1,0:T(8,128)(2,1)} %refs_0_.1), channel_id=1, source_target_pairs={{0,2},{1,3},{4,6},{5,7},{8,10},{9,11},{12,14},{13,15},{16,18},{17,... | collective-permute-start | bytes 1966088 | tf_op jit(solution)/shard_map/ppermute | solution.py:41
  9.1 129.7 %collective-permute-start.27 = (bf16[320,3072]{1,0:T(8,128)(2,1)S(1)}, bf16[320,3072]{1,0:T(8,128)(2,1)}, u32[]{:S(2)}, u32[]{:S(2)}) collective-permute-start(bf16[320,3072]{1,0:T(8,128)(2,1)S(1)} %pad_maximum_fusion.refs_1_.refs_2_), channel_id=1, source_target_pairs={{0,16},{4,20},{8,24},{12,28},{16,0},{20,4},{24,8},{28,12},{1,17},{... | collective-permute-start | bytes 5898248 | tf_op jit(solution)/shard_map/ppermute | solution.py:37
  11.6 69.3 %collective-permute-start = (bf16[128,2560]{1,0:T(8,128)(2,1)S(1)}, bf16[128,2560]{1,0:T(8,128)(2,1)}, u32[]{:S(2)}, u32[]{:S(2)}) collective-permute-start(bf16[128,2560]{1,0:T(8,128)(2,1)S(1)} %copy-done.24), channel_id=1, source_target_pairs={{0,1},{2,3},{4,5},{6,7},{8,9},{10,11},{12,13},{14,15},{16,17},{18,... | collective-permute-start | bytes 1966088 | tf_op jit(solution)/shard_map/ppermute | solution.py:41
  15.9 65.7 %collective-permute-start.5 = (bf16[128,2560]{1,0:T(8,128)(2,1)S(1)}, bf16[128,2560]{1,0:T(8,128)(2,1)}, u32[]{:S(2)}, u32[]{:S(2)}) collective-permute-start(bf16[128,2560]{1,0:T(8,128)(2,1)S(1)} %copy-done.24), channel_id=1, source_target_pairs={{1,0},{3,2},{5,4},{7,6},{9,8},{11,10},{13,12},{15,14},{17,16},{19,... | collective-permute-start | bytes 1966088 | tf_op jit(solution)/shard_map/ppermute | solution.py:41
  34.4 47.9 %collective-permute-start.3 = (bf16[128,2560]{1,0:T(8,128)(2,1)S(1)}, bf16[128,2560]{1,0:T(8,128)(2,1)}, u32[]{:S(2)}, u32[]{:S(2)}) collective-permute-start(bf16[128,2560]{1,0:T(8,128)(2,1)S(1)} %collective-permute-done.2.refs_5_), channel_id=1, source_target_pairs={{1,0},{5,4},{9,8},{13,12},{17,16},{21,20},{25,24},{29,28}} | collective-permute-start | bytes 1966088 | tf_op jit(solution)/shard_map/ppermute | solution.py:41
  44.6 15.0 %collective-permute-start.12 = (f32[2,128]{1,0:T(2,128)S(1)}, f32[2,128]{1,0:T(2,128)S(1)}, u32[]{:S(2)}, u32[]{:S(2)}) collective-permute-start(f32[2,128]{1,0:T(2,128)S(1)} %pad_maximum_fusion.5), channel_id=1, source_target_pairs={{1,0},{2,1},{3,2},{5,4},{6,5},{7,6},{9,8},{10,9},{11,10},{13,12},{... | collective-permute-start | bytes 3080 | tf_op jit(solution)/shard_map/ppermute | solution.py:41
  78.7 62.5 %collective-permute-start.26 = (bf16[320,3072]{1,0:T(8,128)(2,1)S(1)}, bf16[320,3072]{1,0:T(8,128)(2,1)}, u32[]{:S(2)}, u32[]{:S(2)}) collective-permute-start(bf16[320,3072]{1,0:T(8,128)(2,1)S(1)} %pad_maximum_fusion.refs_1_.refs_2_), channel_id=1, source_target_pairs={{0,8},{4,12},{8,0},{12,4},{16,24},{20,28},{24,16},{28,20},{1,9},{5... | collective-permute-start | bytes 5898248 | tf_op jit(solution)/shard_map/ppermute | solution.py:37
  92.4 39.6 %collective-permute-start.24 = (bf16[64,2560]{1,0:T(8,128)(2,1)}, bf16[64,2560]{1,0:T(8,128)(2,1)S(1)}, u32[]{:S(2)}, u32[]{:S(2)}) collective-permute-start(bf16[64,2560]{1,0:T(8,128)(2,1)} %get-tuple-element.59), channel_id=1, source_target_pairs={{0,24},{4,28},{8,16},{12,20},{16,8},{20,12},{24,0},{28,4},{1,25},{... | collective-permute-start | bytes 983048 | tf_op jit(solution)/shard_map/ppermute | solution.py:37
  93.0 45.3 %collective-permute-start.25 = (bf16[64,2560]{1,0:T(8,128)(2,1)}, bf16[64,2560]{1,0:T(8,128)(2,1)S(1)}, u32[]{:S(2)}, u32[]{:S(2)}) collective-permute-start(bf16[64,2560]{1,0:T(8,128)(2,1)} %get-tuple-element.60), channel_id=1, source_target_pairs={{0,28},{4,24},{8,20},{12,16},{16,12},{20,8},{24,4},{28,0},{1,29},{... | collective-permute-start | bytes 983048 | tf_op jit(solution)/shard_map/ppermute | solution.py:37
  93.0 59.8 %collective-permute-start.16 = (bf16[128,2560]{1,0:T(8,128)(2,1)}, bf16[128,2560]{1,0:T(8,128)(2,1)}, u32[]{:S(2)}, u32[]{:S(2)}) collective-permute-start(bf16[128,2560]{1,0:T(8,128)(2,1)} %get-tuple-element.51), channel_id=1, source_target_pairs={{0,8},{4,12},{8,0},{12,4},{16,24},{20,28},{24,16},{28,20},{1,9},{5... | collective-permute-start | bytes 1966088 | tf_op jit(solution)/shard_map/ppermute | solution.py:37
  132.0 27.9 %collective-permute-start.17 = (bf16[128,2560]{1,0:T(8,128)(2,1)}, bf16[128,2560]{1,0:T(8,128)(2,1)}, u32[]{:S(2)}, u32[]{:S(2)}) collective-permute-start(bf16[128,2560]{1,0:T(8,128)(2,1)} %get-tuple-element.52), channel_id=1, source_target_pairs={{0,12},{4,8},{8,4},{12,0},{16,28},{20,24},{24,20},{28,16},{1,13},{... | collective-permute-start | bytes 1966088 | tf_op jit(solution)/shard_map/ppermute | solution.py:37
  138.2 23.7 %collective-permute-start.18 = (bf16[128,2560]{1,0:T(8,128)(2,1)}, bf16[128,2560]{1,0:T(8,128)(2,1)}, u32[]{:S(2)}, u32[]{:S(2)}) collective-permute-start(bf16[128,2560]{1,0:T(8,128)(2,1)} %get-tuple-element.53), channel_id=1, source_target_pairs={{0,16},{4,20},{8,24},{12,28},{16,0},{20,4},{24,8},{28,12},{1,17},{... | collective-permute-start | bytes 1966088 | tf_op jit(solution)/shard_map/ppermute | solution.py:37
  138.7 30.8 %collective-permute-start.19 = (bf16[128,2560]{1,0:T(8,128)(2,1)}, bf16[128,2560]{1,0:T(8,128)(2,1)}, u32[]{:S(2)}, u32[]{:S(2)}) collective-permute-start(bf16[128,2560]{1,0:T(8,128)(2,1)} %get-tuple-element.54), channel_id=1, source_target_pairs={{0,20},{4,16},{8,28},{12,24},{16,4},{20,0},{24,12},{28,8},{1,21},{... | collective-permute-start | bytes 1966088 | tf_op jit(solution)/shard_map/ppermute | solution.py:37
  141.2 82.7 %collective-permute-start.32 = (bf16[320,3072]{1,0:T(8,128)(2,1)S(1)}, bf16[320,3072]{1,0:T(8,128)(2,1)S(1)}, u32[]{:S(2)}, u32[]{:S(2)}) collective-permute-start(bf16[320,3072]{1,0:T(8,128)(2,1)S(1)} %pad_maximum_fusion.refs_1_.refs_2_), channel_id=1, source_target_pairs={{0,4},{4,0},{8,12},{12,8},{16,20},{20,16},{24,28},{28,24},{1,5},{5... | collective-permute-start | bytes 5898248 | tf_op jit(solution)/shard_map/ppermute | solution.py:37
  152.7 50.8 %collective-permute-start.14 = (bf16[128,2560]{1,0:T(8,128)(2,1)S(1)}, bf16[128,2560]{1,0:T(8,128)(2,1)}, u32[]{:S(2)}, u32[]{:S(2)}) collective-permute-start(bf16[128,2560]{1,0:T(8,128)(2,1)S(1)} %copy-done.27), channel_id=1, source_target_pairs={{0,4},{4,0},{8,12},{12,8},{16,20},{20,16},{24,28},{28,24},{1,5},{5... | collective-permute-start | bytes 1966088 | tf_op jit(solution)/shard_map/ppermute | solution.py:37
  160.0 26.1 %collective-permute-start.28 = (bf16[128,2560]{1,0:T(8,128)(2,1)S(1)}, bf16[128,2560]{1,0:T(8,128)(2,1)}, u32[]{:S(2)}, u32[]{:S(2)}) collective-permute-start(bf16[128,2560]{1,0:T(8,128)(2,1)S(1)} %pad_maximum_fusion.1.refs_0_), channel_id=1, source_target_pairs={{0,1},{1,0},{2,3},{3,2},{4,5},{5,4},{6,7},{7,6},{8,9},{9,8},{10,11... | collective-permute-start | bytes 1966088 | tf_op jit(solution)/shard_map/ppermute | solution.py:37
  162.0 37.0 %collective-permute-start.36 = (bf16[320,1536]{1,0:T(8,128)(2,1)S(1)}, bf16[320,1536]{1,0:T(8,128)(2,1)}, u32[]{:S(2)}, u32[]{:S(2)}) collective-permute-start(bf16[320,1536]{1,0:T(8,128)(2,1)S(1)} %slice.29), channel_id=1, source_target_pairs={{0,16},{4,20},{8,24},{12,28},{16,0},{20,4},{24,8},{28,12},{1,17},{... | collective-permute-start | bytes 2949128 | tf_op jit(solution)/shard_map/ppermute | solution.py:37
  169.6 26.7 %collective-permute-start.35 = (bf16[320,1536]{1,0:T(8,128)(2,1)}, bf16[320,1536]{1,0:T(8,128)(2,1)}, u32[]{:S(2)}, u32[]{:S(2)}) collective-permute-start(bf16[320,1536]{1,0:T(8,128)(2,1)} %slice.28), channel_id=1, source_target_pairs={{0,8},{4,12},{8,0},{12,4},{16,24},{20,28},{24,16},{28,20},{1,9},{5... | collective-permute-start | bytes 2949128 | tf_op jit(solution)/shard_map/ppermute | solution.py:37
  186.1 38.1 %collective-permute-start.34 = (bf16[320,3072]{1,0:T(8,128)(2,1)}, bf16[320,3072]{1,0:T(8,128)(2,1)S(1)}, u32[]{:S(2)}, u32[]{:S(2)}) collective-permute-start(bf16[320,3072]{1,0:T(8,128)(2,1)} %collective-permute-done.27.refs_5_.refs_6_), channel_id=1, source_target_pairs={{0,4},{4,0},{8,12},{12,8},{16,20},{20,16},{24,28},{28,24},{1,5},{5... | collective-permute-start | bytes 5898248 | tf_op jit(solution)/shard_map/ppermute | solution.py:37
  196.2 29.7 %collective-permute-start.33 = (bf16[320,3072]{1,0:T(8,128)(2,1)}, bf16[320,3072]{1,0:T(8,128)(2,1)}, u32[]{:S(2)}, u32[]{:S(2)}) collective-permute-start(bf16[320,3072]{1,0:T(8,128)(2,1)} %collective-permute-done.26.refs_3_.refs_4_), channel_id=1, source_target_pairs={{0,4},{4,0},{8,12},{12,8},{16,20},{20,16},{24,28},{28,24},{1,5},{5... | collective-permute-start | bytes 5898248 | tf_op jit(solution)/shard_map/ppermute | solution.py:37
  199.0 14.6 %collective-permute-start.49 = (bf16[128,1280]{1,0:T(8,128)(2,1)S(1)}, bf16[128,1280]{1,0:T(8,128)(2,1)S(1)}, u32[]{:S(2)}, u32[]{:S(2)}) collective-permute-start(bf16[128,1280]{1,0:T(8,128)(2,1)S(1)} %copy-done.41), channel_id=1, source_target_pairs={{0,1},{1,0},{2,3},{3,2},{4,5},{5,4},{6,7},{7,6},{8,9},{9,8},{10,11... | collective-permute-start | bytes 983048 | tf_op jit(solution)/shard_map/ppermute | solution.py:37
  203.5 39.3 %collective-permute-start.37 = (bf16[320,3072]{1,0:T(8,128)(2,1)}, bf16[320,3072]{1,0:T(8,128)(2,1)}, u32[]{:S(2)}, u32[]{:S(2)}) collective-permute-start(bf16[320,3072]{1,0:T(8,128)(2,1)} %constant_dynamic-update-slice_fusion.refs_8_), channel_id=1, source_target_pairs={{0,4},{4,0},{8,12},{12,8},{16,20},{20,16},{24,28},{28,24},{1,5},{5... | collective-permute-start | bytes 5898248 | tf_op jit(solution)/shard_map/ppermute | solution.py:37
  223.8 14.5 %collective-permute-start.44 = (bf16[128,1280]{1,0:T(8,128)(2,1)}, bf16[128,1280]{1,0:T(8,128)(2,1)S(1)}, u32[]{:S(2)}, u32[]{:S(2)}) collective-permute-start(bf16[128,1280]{1,0:T(8,128)(2,1)} %get-tuple-element.72), channel_id=1, source_target_pairs={{0,4},{4,0},{8,12},{12,8},{16,20},{20,16},{24,28},{28,24},{1,5},{5... | collective-permute-start | bytes 983048 | tf_op jit(solution)/shard_map/ppermute | solution.py:37
  223.9 14.4 %collective-permute-start.45 = (bf16[128,1280]{1,0:T(8,128)(2,1)}, bf16[128,1280]{1,0:T(8,128)(2,1)S(1)}, u32[]{:S(2)}, u32[]{:S(2)}) collective-permute-start(bf16[128,1280]{1,0:T(8,128)(2,1)} %get-tuple-element.73), channel_id=1, source_target_pairs={{0,8},{4,12},{8,0},{12,4},{16,24},{20,28},{24,16},{28,20},{1,9},{5... | collective-permute-start | bytes 983048 | tf_op jit(solution)/shard_map/ppermute | solution.py:37
  224.2 16.7 %collective-permute-start.46 = (bf16[128,1280]{1,0:T(8,128)(2,1)S(1)}, bf16[128,1280]{1,0:T(8,128)(2,1)S(1)}, u32[]{:S(2)}, u32[]{:S(2)}) collective-permute-start(bf16[128,1280]{1,0:T(8,128)(2,1)S(1)} %copy-done.38), channel_id=1, source_target_pairs={{0,12},{4,8},{8,4},{12,0},{16,28},{20,24},{24,20},{28,16},{1,13},{... | collective-permute-start | bytes 983048 | tf_op jit(solution)/shard_map/ppermute | solution.py:37
  225.9 16.8 %collective-permute-start.47 = (bf16[128,1280]{1,0:T(8,128)(2,1)S(1)}, bf16[128,1280]{1,0:T(8,128)(2,1)S(1)}, u32[]{:S(2)}, u32[]{:S(2)}) collective-permute-start(bf16[128,1280]{1,0:T(8,128)(2,1)S(1)} %copy-done.37), channel_id=1, source_target_pairs={{0,16},{4,20},{8,24},{12,28},{16,0},{20,4},{24,8},{28,12},{1,17},{... | collective-permute-start | bytes 983048 | tf_op jit(solution)/shard_map/ppermute | solution.py:37
  238.3 28.4 %collective-permute-start.15 = (bf16[128,1280]{1,0:T(8,128)(2,1)S(1)}, bf16[128,1280]{1,0:T(8,128)(2,1)S(1)}, u32[]{:S(2)}, u32[]{:S(2)}) collective-permute-start(bf16[128,1280]{1,0:T(8,128)(2,1)S(1)} %copy-done.36), channel_id=1, source_target_pairs={{0,4},{4,0},{8,12},{12,8},{16,20},{20,16},{24,28},{28,24},{1,5},{5... | collective-permute-start | bytes 983048 | tf_op jit(solution)/shard_map/ppermute | solution.py:37
  238.4 29.6 %collective-permute-start.20 = (bf16[128,1280]{1,0:T(8,128)(2,1)S(1)}, bf16[128,1280]{1,0:T(8,128)(2,1)S(1)}, u32[]{:S(2)}, u32[]{:S(2)}) collective-permute-start(bf16[128,1280]{1,0:T(8,128)(2,1)S(1)} %copy-done.34), channel_id=1, source_target_pairs={{0,8},{4,12},{8,0},{12,4},{16,24},{20,28},{24,16},{28,20},{1,9},{5... | collective-permute-start | bytes 983048 | tf_op jit(solution)/shard_map/ppermute | solution.py:37
  240.9 16.8 %collective-permute-start.48 = (bf16[128,1280]{1,0:T(8,128)(2,1)S(1)}, bf16[128,1280]{1,0:T(8,128)(2,1)S(1)}, u32[]{:S(2)}, u32[]{:S(2)}) collective-permute-start(bf16[128,1280]{1,0:T(8,128)(2,1)S(1)} %copy-done.35), channel_id=1, source_target_pairs={{0,20},{4,16},{8,28},{12,24},{16,4},{20,0},{24,12},{28,8},{1,21},{... | collective-permute-start | bytes 983048 | tf_op jit(solution)/shard_map/ppermute | solution.py:37
  242.8 15.0 %collective-permute-start.51 = (bf16[64,1280]{1,0:T(8,128)(2,1)S(1)}, bf16[64,1280]{1,0:T(8,128)(2,1)S(1)}, u32[]{:S(2)}, u32[]{:S(2)}) collective-permute-start(bf16[64,1280]{1,0:T(8,128)(2,1)S(1)} %get-tuple-element.85), channel_id=1, source_target_pairs={{0,28},{4,24},{8,20},{12,16},{16,12},{20,8},{24,4},{28,0},{1,29},{... | collective-permute-start | bytes 491528 | tf_op jit(solution)/shard_map/ppermute | solution.py:37
  242.8 16.7 %collective-permute-start.50 = (bf16[64,1280]{1,0:T(8,128)(2,1)S(1)}, bf16[64,1280]{1,0:T(8,128)(2,1)S(1)}, u32[]{:S(2)}, u32[]{:S(2)}) collective-permute-start(bf16[64,1280]{1,0:T(8,128)(2,1)S(1)} %get-tuple-element.86), channel_id=1, source_target_pairs={{0,24},{4,28},{8,16},{12,20},{16,8},{20,12},{24,0},{28,4},{1,25},{... | collective-permute-start | bytes 491528 | tf_op jit(solution)/shard_map/ppermute | solution.py:37
  257.7 15.2 %collective-permute-start.21 = (bf16[128,1280]{1,0:T(8,128)(2,1)S(1)}, bf16[128,1280]{1,0:T(8,128)(2,1)S(1)}, u32[]{:S(2)}, u32[]{:S(2)}) collective-permute-start(bf16[128,1280]{1,0:T(8,128)(2,1)S(1)} %copy-done.33), channel_id=1, source_target_pairs={{0,12},{4,8},{8,4},{12,0},{16,28},{20,24},{24,20},{28,16},{1,13},{... | collective-permute-start | bytes 983048 | tf_op jit(solution)/shard_map/ppermute | solution.py:37
  257.8 16.8 %collective-permute-start.22 = (bf16[128,1280]{1,0:T(8,128)(2,1)S(1)}, bf16[128,1280]{1,0:T(8,128)(2,1)S(1)}, u32[]{:S(2)}, u32[]{:S(2)}) collective-permute-start(bf16[128,1280]{1,0:T(8,128)(2,1)S(1)} %copy-done.32), channel_id=1, source_target_pairs={{0,16},{4,20},{8,24},{12,28},{16,0},{20,4},{24,8},{28,12},{1,17},{... | collective-permute-start | bytes 983048 | tf_op jit(solution)/shard_map/ppermute | solution.py:37
  259.5 15.5 %collective-permute-start.23 = (bf16[128,1280]{1,0:T(8,128)(2,1)S(1)}, bf16[128,1280]{1,0:T(8,128)(2,1)S(1)}, u32[]{:S(2)}, u32[]{:S(2)}) collective-permute-start(bf16[128,1280]{1,0:T(8,128)(2,1)S(1)} %copy-done.31), channel_id=1, source_target_pairs={{0,20},{4,16},{8,28},{12,24},{16,4},{20,0},{24,12},{28,8},{1,21},{... | collective-permute-start | bytes 983048 | tf_op jit(solution)/shard_map/ppermute | solution.py:37
  266.7 25.9 %collective-permute-start.57 = (bf16[128,1280]{1,0:T(8,128)(2,1)}, bf16[128,1280]{1,0:T(8,128)(2,1)S(1)}, u32[]{:S(2)}, u32[]{:S(2)}) collective-permute-start(bf16[128,1280]{1,0:T(8,128)(2,1)} %get-tuple-element.80), channel_id=1, source_target_pairs={{1,0},{2,1},{3,2},{5,4},{6,5},{7,6},{9,8},{10,9},{11,10},{13,12},{... | collective-permute-start | bytes 983048 | tf_op jit(solution)/shard_map/ppermute | solution.py:41
  268.0 30.2 %collective-permute-start.52 = (bf16[128,1280]{1,0:T(8,128)(2,1)}, bf16[128,1280]{1,0:T(8,128)(2,1)S(1)}, u32[]{:S(2)}, u32[]{:S(2)}) collective-permute-start(bf16[128,1280]{1,0:T(8,128)(2,1)} %get-tuple-element.80), channel_id=1, source_target_pairs={{0,3},{4,7},{8,11},{12,15},{16,19},{20,23},{24,27},{28,31}} | collective-permute-start | bytes 983048 | tf_op jit(solution)/shard_map/ppermute | solution.py:41
  273.0 10.3 %collective-permute-start.31 = (bf16[64,1280]{1,0:T(8,128)(2,1)S(1)}, bf16[64,1280]{1,0:T(8,128)(2,1)S(1)}, u32[]{:S(2)}, u32[]{:S(2)}) collective-permute-start(bf16[64,1280]{1,0:T(8,128)(2,1)S(1)} %get-tuple-element.83), channel_id=1, source_target_pairs={{0,28},{4,24},{8,20},{12,16},{16,12},{20,8},{24,4},{28,0},{1,29},{... | collective-permute-start | bytes 491528 | tf_op jit(solution)/shard_map/ppermute | solution.py:37
  275.1 24.5 %collective-permute-start.56 = (bf16[128,1280]{1,0:T(8,128)(2,1)}, bf16[128,1280]{1,0:T(8,128)(2,1)S(1)}, u32[]{:S(2)}, u32[]{:S(2)}) collective-permute-start(bf16[128,1280]{1,0:T(8,128)(2,1)} %get-tuple-element.81), channel_id=1, source_target_pairs={{0,1},{1,2},{2,3},{4,5},{5,6},{6,7},{8,9},{9,10},{10,11},{12,13},{... | collective-permute-start | bytes 983048 | tf_op jit(solution)/shard_map/ppermute | solution.py:41
  283.3 19.7 %collective-permute-start.53 = (bf16[128,1280]{1,0:T(8,128)(2,1)}, bf16[128,1280]{1,0:T(8,128)(2,1)S(1)}, u32[]{:S(2)}, u32[]{:S(2)}) collective-permute-start(bf16[128,1280]{1,0:T(8,128)(2,1)} %get-tuple-element.81), channel_id=1, source_target_pairs={{3,0},{7,4},{11,8},{15,12},{19,16},{23,20},{27,24},{31,28}} | collective-permute-start | bytes 983048 | tf_op jit(solution)/shard_map/ppermute | solution.py:41
  284.6 23.6 %collective-permute-start.55 = (bf16[128,1280]{1,0:T(8,128)(2,1)}, bf16[128,1280]{1,0:T(8,128)(2,1)S(1)}, u32[]{:S(2)}, u32[]{:S(2)}) collective-permute-start(bf16[128,1280]{1,0:T(8,128)(2,1)} %get-tuple-element.82), channel_id=1, source_target_pairs={{2,0},{3,1},{6,4},{7,5},{10,8},{11,9},{14,12},{15,13},{18,16},{19,... | collective-permute-start | bytes 983048 | tf_op jit(solution)/shard_map/ppermute | solution.py:41
  292.6 16.9 %collective-permute-start.54 = (bf16[128,1280]{1,0:T(8,128)(2,1)S(1)}, bf16[128,1280]{1,0:T(8,128)(2,1)S(1)}, u32[]{:S(2)}, u32[]{:S(2)}) collective-permute-start(bf16[128,1280]{1,0:T(8,128)(2,1)S(1)} %copy-done.39), channel_id=1, source_target_pairs={{0,2},{1,3},{4,6},{5,7},{8,10},{9,11},{12,14},{13,15},{16,18},{17,... | collective-permute-start | bytes 983048 | tf_op jit(solution)/shard_map/ppermute | solution.py:41
  298.2 23.5 %collective-permute-start.43 = (bf16[128,1280]{1,0:T(8,128)(2,1)}, bf16[128,1280]{1,0:T(8,128)(2,1)S(1)}, u32[]{:S(2)}, u32[]{:S(2)}) collective-permute-start(bf16[128,1280]{1,0:T(8,128)(2,1)} %get-tuple-element.68), channel_id=1, source_target_pairs={{1,0},{2,1},{3,2},{5,4},{6,5},{7,6},{9,8},{10,9},{11,10},{13,12},{... | collective-permute-start | bytes 983048 | tf_op jit(solution)/shard_map/ppermute | solution.py:41
  299.5 24.6 %collective-permute-start.38 = (bf16[128,1280]{1,0:T(8,128)(2,1)}, bf16[128,1280]{1,0:T(8,128)(2,1)S(1)}, u32[]{:S(2)}, u32[]{:S(2)}) collective-permute-start(bf16[128,1280]{1,0:T(8,128)(2,1)} %get-tuple-element.68), channel_id=1, source_target_pairs={{0,3},{4,7},{8,11},{12,15},{16,19},{20,23},{24,27},{28,31}} | collective-permute-start | bytes 983048 | tf_op jit(solution)/shard_map/ppermute | solution.py:41
  302.9 21.2 %collective-permute-start.42 = (bf16[128,1280]{1,0:T(8,128)(2,1)}, bf16[128,1280]{1,0:T(8,128)(2,1)S(1)}, u32[]{:S(2)}, u32[]{:S(2)}) collective-permute-start(bf16[128,1280]{1,0:T(8,128)(2,1)} %get-tuple-element.69), channel_id=1, source_target_pairs={{0,1},{1,2},{2,3},{4,5},{5,6},{6,7},{8,9},{9,10},{10,11},{12,13},{... | collective-permute-start | bytes 983048 | tf_op jit(solution)/shard_map/ppermute | solution.py:41
  308.2 15.9 %collective-permute-start.39 = (bf16[128,1280]{1,0:T(8,128)(2,1)}, bf16[128,1280]{1,0:T(8,128)(2,1)S(1)}, u32[]{:S(2)}, u32[]{:S(2)}) collective-permute-start(bf16[128,1280]{1,0:T(8,128)(2,1)} %get-tuple-element.69), channel_id=1, source_target_pairs={{3,0},{7,4},{11,8},{15,12},{19,16},{23,20},{27,24},{31,28}} | collective-permute-start | bytes 983048 | tf_op jit(solution)/shard_map/ppermute | solution.py:41
  309.5 26.1 %collective-permute-start.41 = (bf16[128,1280]{1,0:T(8,128)(2,1)}, bf16[128,1280]{1,0:T(8,128)(2,1)S(1)}, u32[]{:S(2)}, u32[]{:S(2)}) collective-permute-start(bf16[128,1280]{1,0:T(8,128)(2,1)} %get-tuple-element.70), channel_id=1, source_target_pairs={{2,0},{3,1},{6,4},{7,5},{10,8},{11,9},{14,12},{15,13},{18,16},{19,... | collective-permute-start | bytes 983048 | tf_op jit(solution)/shard_map/ppermute | solution.py:41
  321.8 13.8 %collective-permute-start.40 = (bf16[128,1280]{1,0:T(8,128)(2,1)}, bf16[128,1280]{1,0:T(8,128)(2,1)S(1)}, u32[]{:S(2)}, u32[]{:S(2)}) collective-permute-start(bf16[128,1280]{1,0:T(8,128)(2,1)} %get-tuple-element.70), channel_id=1, source_target_pairs={{0,2},{1,3},{4,6},{5,7},{8,10},{9,11},{12,14},{13,15},{16,18},{17,... | collective-permute-start | bytes 983048 | tf_op jit(solution)/shard_map/ppermute | solution.py:41
  (53 other events, 813.5 us)

commit v2 on v1

--- a/solution.py
+++ b/solution.py
@@ -37,8 +37,9 @@
     return lax.ppermute(block, axis, [(i, i ^ bits) for i in range(size)])
 
 
-def hop(block, step, sources):
-    return lax.ppermute(block, "tensor", [(i, i + step) for i in sources])
+def ring(block, step):
+    count = lax.axis_size("tensor")
+    return lax.ppermute(block, "tensor", [(i, (i + step) % count) for i in range(count)])
 
 
 def bits_of(number):
@@ -49,46 +50,24 @@
     return len(bits_of(offset >> 1)) > 1
 
 
-def line_all(block, count):
-    parts = [block] + [0] * (count - 1)
-    for back in range(1, count):
-        parts[back] += hop(block, back, range(count - back))
-        parts[count - back] += hop(block, -back, range(back, count))
-    return parts
-
-
 def line_gather(block, count):
-    if count < 4:
-        return {
-            k: [(part, range(count))] for k, part in enumerate(line_all(block, count)) if k
-        }
-    got = {k: [] for k in range(1, count)}
-    middle = (count // 2 - 1, count // 2)
-    up = hop(block, 2, range(count - 2))
-    down = hop(block, -2, range(2, count))
-    got[2].append((up, list(range(2, count))))
-    got[count - 2].append((down, list(range(count - 2))))
-    outer = [i for i in range(count - 1) if i != middle[0]]
-    got[1].append((hop(block, 1, outer), [i + 1 for i in outer]))
-    outer = [i + 1 for i in outer]
-    got[count - 1].append((hop(block, -1, outer), [i - 1 for i in outer]))
-    block, up, down = lax.optimization_barrier((block, up, down))
-    for back in range(3, count):
-        up = hop(up, 1, range(back - 1, count - 1))
-        down = hop(down, -1, range(1, count - back + 1))
-        got[back].append((up, list(range(back, count))))
-        got[count - back].append((down, list(range(count - back))))
-    got[1].append((hop(block, 1, middle[:1]), [middle[1]]))
-    got[count - 1].append((hop(block, -1, middle[1:]), [middle[0]]))
-    return got
+    if count != 4:
+        return [(ring(block, back), [(back, range(count))]) for back in range(1, count)]
+    direct = ring(block, 2)
+    outer = swap(block, "tensor", 1)
+    block, direct = lax.optimization_barrier((block, direct))
+    ahead = lax.ppermute(direct, "tensor", [(2, 3), (1, 0)])
+    middle = lax.ppermute(block, "tensor", [(1, 2), (2, 1)])
+    return [
+        (direct, [(2, range(4))]),
+        (outer, [(1, (1, 3)), (3, (0, 2))]),
+        (ahead, [(1, (0,)), (3, (3,))]),
+        (middle, [(1, (2,)), (3, (1,))]),
+    ]
 
 
 def line_scatter(part, count):
-    got = []
-    for back in range(count - 1, 0, -1):
-        got.append(hop(part[count - back], back, range(count - back)))
-        got.append(hop(part[back], -back, range(back, count)))
-    return add(part[0], *got)
+    return add(part[0], *[ring(part[k], -k) for k in range(1, count)])
 
 
 def with_partner(held):
@@ -205,12 +184,13 @@
         return pltpu.make_async_copy(ref, x.at[pl.ds(k * rows, rows), :], sem_in.at[k])
 
     into(own, 0).start()
-    for part, (k, places) in zip(parts, sources):
-        here = functools.reduce(jnp.logical_or, [place == p for p in places])
-
-        @pl.when(here)
-        def _():
-            into(part, k).start()
+    for part, uses in zip(parts, sources):
+        for k, places in uses:
+            here = functools.reduce(jnp.logical_or, [place == p for p in places])
+
+            @pl.when(here)
+            def _():
+                into(part, k).start()
 
     places = lax.broadcasted_iota(jnp.int32, pick.shape, 0)
     pick[...] = (places == slot[...]).astype(F32).astype(BF16)
@@ -399,11 +379,11 @@
 
 
 def pick_rows(own, got, slot, lengths):
-    sources = [(k, places) for k in got for _, places in got[k]]
-    count, (rows, width) = len(got) + 1, own.shape
+    sources = [uses for _, uses in got]
+    count, (rows, width) = lax.axis_size("tensor"), own.shape
     group, total = rows * count, sum(lengths)
     tiles = tiles_of(width)
-    ins = [own, *[block for k in got for block, _ in got[k]], slot[None, :]]
+    ins = [own, *[block for block, _ in got], slot[None, :]]
     out = call(
         functools.partial(pick_kernel, count, sources, lengths),
         ins,
@@ -540,7 +520,8 @@
     s_all = jnp.concatenate([s_gate, s_up, s_down.T], axis=1)
     near = {bit: swap(s_all, "expert", bit) for bit in bits_of((size - 1) & ~1)}
     notes = jnp.concatenate([expert_ids.astype(F32).T, gates[None, :]], axis=0)
-    notes = jnp.concatenate(line_all(notes, count), axis=1)
+    others = [ring(notes, back) for back in range(1, count)]
+    notes = jnp.concatenate([notes, *others], axis=1)
     ids, scale = notes[0].astype(jnp.int32), notes[1]
 
     index = jnp.arange(group, dtype=jnp.int32)

time: 342 us -> 290 us (0.85); the launches traced: 337 us -> 289 us
  starting transfers between devices: 92.5 us -> 49.6 us
  waiting for transfers between devices: 152 us -> 148 us
    ppermute x26 -> x12, starting transfers between devices: 64.4 us -> 19.6 us  [the longest x10 17.6 us: ring(): lax.ppermute(block, 'tensor', [(i, (i + step) % count) for i in range(cou...]
    ppermute x26 -> x12, waiting for transfers between devices: 71.5 us -> 66.7 us  [the longest x10 54.9 us: ring(): lax.ppermute(block, 'tensor', [(i, (i + step) % count) for i in range(cou...]
    ppermute x32 -> x33, starting transfers between devices: 28.1 us -> 30 us  [swap(): return lax.ppermute(block, axis, [(i, i ^ bits) for i in range(size)])]
    ppermute x32 -> x33, waiting for transfers between devices: 80.5 us -> 81 us  [swap(): return lax.ppermute(block, axis, [(i, i ^ bits) for i in range(size)])]
  transfers between devices with their start and end apart: 58 -> 45, of which waited for: 18 -> 19; matrix products, arithmetic and copies ran while one was open for 4% -> 4% of each run, Pallas kernels for 23% -> 26%
where the time goes in v2:
time: 290 us; the launch traced here: 289 us
  waiting for transfers between devices  148 us (51%)
  Pallas kernels  75.7 us (26%)
  starting transfers between devices  49.6 us (17%)
  local copies, waits for them, and re-layouts  10.7 us (4%)
  other arithmetic  5.06 us (2%)
    ppermute x33, waiting for transfers between devices, swap(): return lax.ppermute(block, axis, [(i, i ^ bits) for i in range(size)])  81 us
    pallas_call x8, Pallas kernels, call(): pl.pallas_call(kernel, out_shape=[jax.ShapeDtypeStruct(shape, kind) for s...  75.7 us
    ppermute x10, waiting for transfers between devices, ring(): lax.ppermute(block, 'tensor', [(i, (i + step) % count) for i in range(cou...  54.9 us
    ppermute x33, starting transfers between devices, swap(): return lax.ppermute(block, axis, [(i, i ^ bits) for i in range(size)])  30 us
    ppermute x10, starting transfers between devices, ring(): lax.ppermute(block, 'tensor', [(i, (i + step) % count) for i in range(cou...  17.6 us
    ppermute x1, waiting for transfers between devices, line_gather(): ahead = lax.ppermute(direct, 'tensor', [(2, 3), (1, 0)])  11.8 us
  transfers between devices with their start and end apart: 45, of which 19 were waited for; matrix products, arithmetic and copies ran while one was open for 4% of the time, Pallas kernels for 26%

profile of v2, /device:TPU:0, one launch (start us, length us, event | category | flops | bytes accessed | tf_op | source)
XLA Modules:
  0.0 289.2 jit_solution(12762740681682220874)
XLA Ops:
  0.0 4.1 %collective-permute-start = (bf16[128,2560]{1,0:T(8,128)(2,1)}, bf16[128,2560]{1,0:T(8,128)(2,1)S(1)}, u32[]{:S(2)}, u32[]{:S(2)}) collective-permute-start(bf16[128,2560]{1,0:T(8,128)(2,1)} %refs_0_.1), channel_id=1, source_target_pairs={{0,2},{1,3},{2,0},{3,1},{4,6},{5,7},{6,4},{7,5},{8,10},{9,11},{10,... | collective-permute-start | bytes 1966088 | tf_op jit(solution)/shard_map/ppermute | solution.py:42
  4.1 1.7 pad_maximum_fusion.refs_1_.refs_2_
  5.8 1.6 collective-permute-start.20
  8.8 1.7 collective-permute-start.5
  10.5 22.6 %collective-permute-done.refs_1_ = bf16[128,2560]{1,0:T(8,128)(2,1)S(1)} collective-permute-done((bf16[128,2560]{1,0:T(8,128)(2,1)}, bf16[128,2560]{1,0:T(8,128)(2,1)S(1)}, u32[]{:S(2)}, u32[]{:S(2)}) %collective-permute-start) | collective-permute-done | bytes 655392 | tf_op jit(solution)/shard_map/ppermute | solution.py:42
  33.1 1.5 collective-permute-start.19
  38.5 13.9 %collective-permute-done.1.refs_2_ = bf16[128,2560]{1,0:T(8,128)(2,1)S(1)} collective-permute-done((bf16[128,2560]{1,0:T(8,128)(2,1)S(1)}, bf16[128,2560]{1,0:T(8,128)(2,1)S(1)}, u32[]{:S(2)}, u32[]{:S(2)}) %collective-permute-start.1) | collective-permute-done | bytes 655392 | tf_op jit(solution)/shard_map/ppermute | solution.py:37
  52.4 11.8 %collective-permute-done.2.refs_3_ = bf16[128,2560]{1,0:T(8,128)(2,1)S(1)} collective-permute-done((bf16[128,2560]{1,0:T(8,128)(2,1)S(1)}, bf16[128,2560]{1,0:T(8,128)(2,1)S(1)}, u32[]{:S(2)}, u32[]{:S(2)}) %collective-permute-start.2) | collective-permute-done | bytes 655392 | tf_op jit(solution)/shard_map/ppermute | solution.py:59
  65.0 7.0 %shard_map.91 = (bf16[128,2560]{1,0:T(8,128)(2,1)}, bf16[128,2560]{1,0:T(8,128)(2,1)}, bf16[128,2560]{1,0:T(8,128)(2,1)}, bf16[128,2560]{1,0:T(8,128)(2,1)}, bf1...) custom-call(bf16[128,2560]{1,0:T(8,128)(2,1)} %refs_0_.1, ...), custom_call_target="tpu_custom_call" | custom-call | flops 2348810240 | bytes 9830400 | tf_op jit(solution)/shard_map/pallas_call | solution.py:366
  72.1 1.6 collective-permute-start.17
  73.6 1.5 collective-permute-start.9
  75.1 11.7 %collective-permute-done.17 = bf16[64,2560]{1,0:T(8,128)(2,1)S(1)} collective-permute-done((bf16[64,2560]{1,0:T(8,128)(2,1)}, bf16[64,2560]{1,0:T(8,128)(2,1)S(1)}, u32[]{:S(2)}, u32[]{:S(2)}) %collective-permute-start.17) | collective-permute-done | bytes 327712 | tf_op jit(solution)/shard_map/ppermute | solution.py:37
  86.8 5.2 %collective-permute-done.18 = bf16[64,2560]{1,0:T(8,128)(2,1)S(1)} collective-permute-done((bf16[64,2560]{1,0:T(8,128)(2,1)}, bf16[64,2560]{1,0:T(8,128)(2,1)S(1)}, u32[]{:S(2)}, u32[]{:S(2)}) %collective-permute-start.18) | collective-permute-done | bytes 327712 | tf_op jit(solution)/shard_map/ppermute | solution.py:37
  92.0 1.5 collective-permute-start.11
  93.5 1.5 collective-permute-start.12
  96.1 2.4 slice.28
  99.7 7.3 %collective-permute-done.9.refs_0_ = bf16[128,2560]{1,0:T(8,128)(2,1)} collective-permute-done((bf16[128,2560]{1,0:T(8,128)(2,1)}, bf16[128,2560]{1,0:T(8,128)(2,1)}, u32[]{:S(2)}, u32[]{:S(2)}) %collective-permute-start.9) | collective-permute-done | bytes 655392 | tf_op jit(solution)/shard_map/ppermute | solution.py:37
  107.0 11.1 %collective-permute-done.10.refs_1_ = bf16[128,2560]{1,0:T(8,128)(2,1)} collective-permute-done((bf16[128,2560]{1,0:T(8,128)(2,1)}, bf16[128,2560]{1,0:T(8,128)(2,1)}, u32[]{:S(2)}, u32[]{:S(2)}) %collective-permute-start.10) | collective-permute-done | bytes 655392 | tf_op jit(solution)/shard_map/ppermute | solution.py:37
  118.1 1.8 collective-permute-start.21
  119.9 1.5 collective-permute-start.29
  121.5 2.9 %collective-permute-done.12.refs_3_ = bf16[128,2560]{1,0:T(8,128)(2,1)} collective-permute-done((bf16[128,2560]{1,0:T(8,128)(2,1)}, bf16[128,2560]{1,0:T(8,128)(2,1)}, u32[]{:S(2)}, u32[]{:S(2)}) %collective-permute-start.12) | collective-permute-done | bytes 655392 | tf_op jit(solution)/shard_map/ppermute | solution.py:37
  124.5 14.7 %shard_map.93 = (bf16[128,1280]{1,0:T(8,128)(2,1)}, bf16[128,1280]{1,0:T(8,128)(2,1)}, bf16[128,1280]{1,0:T(8,128)(2,1)}, bf16[128,1280]{1,0:T(8,128)(2,1)}, bf1...) custom-call(bf16[128,2560]{1,0:T(8,128)(2,1)} %collective-permute-don, ...), custom_call_target="tpu_custom_call" | custom-call | flops 8053063680 | bytes 20971520 | tf_op jit(solution)/shard_map/pallas_call | solution.py:366
  139.3 10.0 %shard_map.94 = (bf16[128,1280]{1,0:T(8,128)(2,1)}, bf16[128,1280]{1,0:T(8,128)(2,1)}, bf16[128,1280]{1,0:T(8,128)(2,1)}, bf16[128,1280]{1,0:T(8,128)(2,1)}) custom-call(bf16[128,2560]{1,0:T(8,128)(2,1)} %copy-done.3, bf16[128,2560]{1,0:T(8,128)(2,1)} %collective-permute-done.21.refs_1_, bf16[1,2560,1024]{2,1,0:T(8,128)(2,1)} %refs_2_.3, ...), custom_call_target="tpu_custom_call" | custom-call | flops 4026531840 | bytes 18350080 | tf_op jit(solution)/shard_map/pallas_call | solution.py:366
  149.9 2.3 constant_dynamic-update-slice_fusion.1
  152.2 2.5 collective-permute-start.22
  154.6 2.2 constant_dynamic-update-slice_fusion.refs_8_
  156.9 10.1 %shard_map.92 = (bf16[128,1280]{1,0:T(8,128)(2,1)}, bf16[128,1280]{1,0:T(8,128)(2,1)}, bf16[128,1280]{1,0:T(8,128)(2,1)}, bf16[128,1280]{1,0:T(8,128)(2,1)}) custom-call(bf16[128,2560]{1,0:T(8,128)(2,1)} %get-tuple-element.45.refs_0_, bf16[128,2560]{1,0:T(8,128)(2,1)} %collective-permute-done.7.refs_1_, bf16[1,2560,1024]{2,1,0:T(8,128)(2,1)} %refs_2_.3, ...), custom_call_target="tpu_custom_call" | custom-call | flops 4026531840 | bytes 18350080 | tf_op jit(solution)/shard_map/pallas_call | solution.py:366
  167.2 10.2 %collective-permute-done.39 = bf16[128,1280]{1,0:T(8,128)(2,1)S(1)} collective-permute-done((bf16[128,1280]{1,0:T(8,128)(2,1)}, bf16[128,1280]{1,0:T(8,128)(2,1)S(1)}, u32[]{:S(2)}, u32[]{:S(2)}) %collective-permute-start.39) | collective-permute-done | bytes 327712 | tf_op jit(solution)/shard_map/ppermute | solution.py:37
  179.8 1.5 collective-permute-start.38
  181.4 10.8 %shard_map.95.refs_0_ = f32[512,2048]{1,0:T(8,128)} custom-call(bf16[512,2560]{1,0:T(8,128)(2,1)} %get-tuple-element.62.refs_0_.refs_1_, bf16[320,3072]{1,0:T(8,128)(2,1)} %copy-done, bf16[320,3072]{1,0:T(8,128)(2,1)} %copy-done.1, bf16[320,3072]{1,0:T(8,128)(2,1)} %collective-permute-done.19.refs_3_.refs_4_, ...), custom_call_target="tpu_custom_call" | custom-call | flops 4026531840 | bytes 12058624 | tf_op jit(solution)/shard_map/pallas_call | solution.py:366
  192.7 1.8 collective-permute-done.36.refs_3_
  197.2 2.0 collective-permute-start.40
  199.3 10.0 %shard_map.96.refs_9_ = f32[512,2560]{1,0:T(8,128)} custom-call(f32[512,2048]{1,0:T(8,128)} %shard_map.95.refs_0_, bf16[512,2560]{1,0:T(8,128)(2,1)} %get-tuple-element.62.refs_0_.refs_1_, bf16[320,3072]{1,0:T(8,128)(2,1)} %copy-done, bf16[320,3072]{1,0:T(8,128)(2,1)} %copy-done.1, bf16[320,3072]{1,0:T(8,128)(2,1)} %collective-permute-done.19.refs_3_.refs_4_, ...), custom_call_target="tpu_custom_call" | custom-call | flops 4026531840 | bytes 14680064 | tf_op jit(solution)/shard_map/pallas_call | solution.py:366
  209.4 4.9 %collective-permute-done.41.refs_7_ = bf16[64,1280]{1,0:T(8,128)(2,1)S(1)} collective-permute-done((bf16[64,1280]{1,0:T(8,128)(2,1)S(1)}, bf16[64,1280]{1,0:T(8,128)(2,1)S(1)}, u32[]{:S(2)}, u32[]{:S(2)}) %collective-permute-start.41) | collective-permute-done | bytes 163872 | tf_op jit(solution)/shard_map/ppermute | solution.py:37
  214.3 2.0 collective-permute-start.15
  216.3 1.9 collective-permute-done.40.refs_6_
  219.6 6.5 %shard_map.98 = (bf16[128,1280]{1,0:T(8,128)(2,1)}, bf16[128,1280]{1,0:T(8,128)(2,1)}, bf16[128,1280]{1,0:T(8,128)(2,1)}, bf16[128,1280]{1,0:T(8,128)(2,1)}) custom-call(bf16[128,1280]{1,0:T(8,128)(2,1)} %get-tuple-element.69.refs_0_, bf16[128,1280]{1,0:T(8,128)(2,1)} %copy-done.10, bf16[128,1280]{1,0:T(8,128)(2,1)} %copy-done.11, ...), custom_call_target="tpu_custom_call" | custom-call | flops 1174405120 | bytes 6225920 | tf_op jit(solution)/shard_map/pallas_call | solution.py:366
  226.1 3.0 %collective-permute-start.42 = (bf16[128,1280]{1,0:T(8,128)(2,1)}, bf16[128,1280]{1,0:T(8,128)(2,1)S(1)}, u32[]{:S(2)}, u32[]{:S(2)}) collective-permute-start(bf16[128,1280]{1,0:T(8,128)(2,1)} %get-tuple-element.78), channel_id=1, source_target_pairs={{0,3},{1,0},{2,1},{3,2},{4,7},{5,4},{6,5},{7,6},{8,11},{9,8},{10,9... | collective-permute-start | bytes 983048 | tf_op jit(solution)/shard_map/ppermute | solution.py:42
  229.5 1.9 collective-permute-start.44
  232.2 2.0 collective-permute-start.23
  234.2 4.5 %collective-permute-done.24.refs_7_ = bf16[64,1280]{1,0:T(8,128)(2,1)S(1)} collective-permute-done((bf16[64,1280]{1,0:T(8,128)(2,1)S(1)}, bf16[64,1280]{1,0:T(8,128)(2,1)S(1)}, u32[]{:S(2)}, u32[]{:S(2)}) %collective-permute-start.24) | collective-permute-done | bytes 163872 | tf_op jit(solution)/shard_map/ppermute | solution.py:37
  238.8 3.7 %collective-permute-done.23.refs_6_ = bf16[64,1280]{1,0:T(8,128)(2,1)S(1)} collective-permute-done((bf16[64,1280]{1,0:T(8,128)(2,1)S(1)}, bf16[64,1280]{1,0:T(8,128)(2,1)S(1)}, u32[]{:S(2)}, u32[]{:S(2)}) %collective-permute-start.23) | collective-permute-done | bytes 163872 | tf_op jit(solution)/shard_map/ppermute | solution.py:37
  243.1 6.5 %shard_map.97 = (bf16[128,1280]{1,0:T(8,128)(2,1)}, bf16[128,1280]{1,0:T(8,128)(2,1)}, bf16[128,1280]{1,0:T(8,128)(2,1)}, bf16[128,1280]{1,0:T(8,128)(2,1)}) custom-call(bf16[128,1280]{1,0:T(8,128)(2,1)} %get-tuple-element.47.refs_0_, bf16[128,1280]{1,0:T(8,128)(2,1)} %copy-done.7, bf16[128,1280]{1,0:T(8,128)(2,1)} %copy-done.8, ...), custom_call_target="tpu_custom_call" | custom-call | flops 1174405120 | bytes 6225920 | tf_op jit(solution)/shard_map/pallas_call | solution.py:366
  249.7 1.9 collective-permute-start.31
  252.8 1.9 collective-permute-start.33
  254.8 4.4 %collective-permute-done.43 = bf16[128,1280]{1,0:T(8,128)(2,1)S(1)} collective-permute-done((bf16[128,1280]{1,0:T(8,128)(2,1)}, bf16[128,1280]{1,0:T(8,128)(2,1)S(1)}, u32[]{:S(2)}, u32[]{:S(2)}) %collective-permute-start.43) | collective-permute-done | bytes 327712 | tf_op jit(solution)/shard_map/ppermute | solution.py:42
  259.4 6.9 %collective-permute-done.31 = bf16[128,1280]{1,0:T(8,128)(2,1)S(1)} collective-permute-done((bf16[128,1280]{1,0:T(8,128)(2,1)}, bf16[128,1280]{1,0:T(8,128)(2,1)S(1)}, u32[]{:S(2)}, u32[]{:S(2)}) %collective-permute-start.31) | collective-permute-done | bytes 327712 | tf_op jit(solution)/shard_map/ppermute | solution.py:42
  266.3 20.9 %collective-permute-done.32 = bf16[128,1280]{1,0:T(8,128)(2,1)S(1)} collective-permute-done((bf16[128,1280]{1,0:T(8,128)(2,1)}, bf16[128,1280]{1,0:T(8,128)(2,1)S(1)}, u32[]{:S(2)}, u32[]{:S(2)}) %collective-permute-start.32) | collective-permute-done | bytes 327712 | tf_op jit(solution)/shard_map/ppermute | solution.py:42
  (147 shorter events, 21.3 us)
Async XLA Ops:
  0.0 33.1 %collective-permute-start = (bf16[128,2560]{1,0:T(8,128)(2,1)}, bf16[128,2560]{1,0:T(8,128)(2,1)S(1)}, u32[]{:S(2)}, u32[]{:S(2)}) collective-permute-start(bf16[128,2560]{1,0:T(8,128)(2,1)} %refs_0_.1), channel_id=1, source_target_pairs={{0,2},{1,3},{2,0},{3,1},{4,6},{5,7},{6,4},{7,5},{8,10},{9,11},{10,... | collective-permute-start | bytes 1966088 | tf_op jit(solution)/shard_map/ppermute | solution.py:42
  4.1 30.6 %copy-start.23 = (bf16[128,2560]{1,0:T(8,128)(2,1)S(1)}, bf16[128,2560]{1,0:T(8,128)(2,1)}, u32[]{:S(2)}) copy-start(bf16[128,2560]{1,0:T(8,128)(2,1)} %refs_0_.1) | copy-start | bytes 1966084
  5.8 90.2 %copy-start = (bf16[320,3072]{1,0:T(8,128)(2,1)}, bf16[320,3072]{1,0:T(8,128)(2,1)S(1)}, u32[]{:S(2)}) copy-start(bf16[320,3072]{1,0:T(8,128)(2,1)S(1)} %pad_maximum_fusion.refs_1_.refs_2_) | copy-start | bytes 5898244
  5.8 87.8 %collective-permute-start.20 = (bf16[320,3072]{1,0:T(8,128)(2,1)S(1)}, bf16[320,3072]{1,0:T(8,128)(2,1)}, u32[]{:S(2)}, u32[]{:S(2)}) collective-permute-start(bf16[320,3072]{1,0:T(8,128)(2,1)S(1)} %pad_maximum_fusion.refs_1_.refs_2_), channel_id=1, source_target_pairs={{0,16},{4,20},{8,24},{12,28},{16,0},{20,4},{24,8},{28,12},{1,17},{... | collective-permute-start | bytes 5898248 | tf_op jit(solution)/shard_map/ppermute | solution.py:37
  7.4 27.3 %collective-permute-start.6 = (f32[2,128]{1,0:T(2,128)S(1)}, f32[2,128]{1,0:T(2,128)S(1)}, u32[]{:S(2)}, u32[]{:S(2)}) collective-permute-start(f32[2,128]{1,0:T(2,128)S(1)} %pad_maximum_fusion.5), channel_id=1, source_target_pairs={{0,3},{1,0},{2,1},{3,2},{4,7},{5,4},{6,5},{7,6},{8,11},{9,8},{10,9... | collective-permute-start | bytes 3080 | tf_op jit(solution)/shard_map/ppermute | solution.py:42
  8.8 26.7 %collective-permute-start.5 = (f32[2,128]{1,0:T(2,128)S(1)}, f32[2,128]{1,0:T(2,128)S(1)}, u32[]{:S(2)}, u32[]{:S(2)}) collective-permute-start(f32[2,128]{1,0:T(2,128)S(1)} %pad_maximum_fusion.5), channel_id=1, source_target_pairs={{0,2},{1,3},{2,0},{3,1},{4,6},{5,7},{6,4},{7,5},{8,10},{9,11},{10,... | collective-permute-start | bytes 3080 | tf_op jit(solution)/shard_map/ppermute | solution.py:42
  10.5 25.8 %collective-permute-start.4 = (f32[2,128]{1,0:T(2,128)S(1)}, f32[2,128]{1,0:T(2,128)S(1)}, u32[]{:S(2)}, u32[]{:S(2)}) collective-permute-start(f32[2,128]{1,0:T(2,128)S(1)} %pad_maximum_fusion.5), channel_id=1, source_target_pairs={{0,1},{1,2},{2,3},{3,0},{4,5},{5,6},{6,7},{7,4},{8,9},{9,10},{10,1... | collective-permute-start | bytes 3080 | tf_op jit(solution)/shard_map/ppermute | solution.py:42
  33.1 31.1 %copy-start.24 = (bf16[128,2560]{1,0:T(8,128)(2,1)}, bf16[128,2560]{1,0:T(8,128)(2,1)S(1)}, u32[]{:S(2)}) copy-start(bf16[128,2560]{1,0:T(8,128)(2,1)S(1)} %collective-permute-done.refs_1_) | copy-start | bytes 1966084
  33.1 62.9 %collective-permute-start.19 = (bf16[320,3072]{1,0:T(8,128)(2,1)S(1)}, bf16[320,3072]{1,0:T(8,128)(2,1)}, u32[]{:S(2)}, u32[]{:S(2)}) collective-permute-start(bf16[320,3072]{1,0:T(8,128)(2,1)S(1)} %pad_maximum_fusion.refs_1_.refs_2_), channel_id=1, source_target_pairs={{0,8},{4,12},{8,0},{12,4},{16,24},{20,28},{24,16},{28,20},{1,9},{5... | collective-permute-start | bytes 5898248 | tf_op jit(solution)/shard_map/ppermute | solution.py:37
  34.7 17.7 %collective-permute-start.1 = (bf16[128,2560]{1,0:T(8,128)(2,1)S(1)}, bf16[128,2560]{1,0:T(8,128)(2,1)S(1)}, u32[]{:S(2)}, u32[]{:S(2)}) collective-permute-start(bf16[128,2560]{1,0:T(8,128)(2,1)S(1)} %copy-done.23), channel_id=1, source_target_pairs={{0,1},{1,0},{2,3},{3,2},{4,5},{5,4},{6,7},{7,6},{8,9},{9,8},{10,11... | collective-permute-start | bytes 1966088 | tf_op jit(solution)/shard_map/ppermute | solution.py:37
  35.5 16.8 %collective-permute-start.3 = (bf16[128,2560]{1,0:T(8,128)(2,1)S(1)}, bf16[128,2560]{1,0:T(8,128)(2,1)S(1)}, u32[]{:S(2)}, u32[]{:S(2)}) collective-permute-start(bf16[128,2560]{1,0:T(8,128)(2,1)S(1)} %copy-done.23), channel_id=1, source_target_pairs={{1,2},{2,1},{5,6},{6,5},{9,10},{10,9},{13,14},{14,13},{17,18},{18,... | collective-permute-start | bytes 1966088 | tf_op jit(solution)/shard_map/ppermute | solution.py:60
  36.2 27.9 %collective-permute-start.2 = (bf16[128,2560]{1,0:T(8,128)(2,1)S(1)}, bf16[128,2560]{1,0:T(8,128)(2,1)S(1)}, u32[]{:S(2)}, u32[]{:S(2)}) collective-permute-start(bf16[128,2560]{1,0:T(8,128)(2,1)S(1)} %collective-permute-done.refs_1_), channel_id=1, source_target_pairs={{2,3},{1,0},{6,7},{5,4},{10,11},{9,8},{14,15},{13,12},{18,19},{17,... | collective-permute-start | bytes 1966088 | tf_op jit(solution)/shard_map/ppermute | solution.py:59
  72.1 14.8 %collective-permute-start.17 = (bf16[64,2560]{1,0:T(8,128)(2,1)}, bf16[64,2560]{1,0:T(8,128)(2,1)S(1)}, u32[]{:S(2)}, u32[]{:S(2)}) collective-permute-start(bf16[64,2560]{1,0:T(8,128)(2,1)} %get-tuple-element.57), channel_id=1, source_target_pairs={{0,24},{4,28},{8,16},{12,20},{16,8},{20,12},{24,0},{28,4},{1,25},{... | collective-permute-start | bytes 983048 | tf_op jit(solution)/shard_map/ppermute | solution.py:37
  73.6 18.4 %collective-permute-start.18 = (bf16[64,2560]{1,0:T(8,128)(2,1)}, bf16[64,2560]{1,0:T(8,128)(2,1)S(1)}, u32[]{:S(2)}, u32[]{:S(2)}) collective-permute-start(bf16[64,2560]{1,0:T(8,128)(2,1)} %get-tuple-element.58), channel_id=1, source_target_pairs={{0,28},{4,24},{8,20},{12,16},{16,12},{20,8},{24,4},{28,0},{1,29},{... | collective-permute-start | bytes 983048 | tf_op jit(solution)/shard_map/ppermute | solution.py:37
  73.6 33.4 %collective-permute-start.9 = (bf16[128,2560]{1,0:T(8,128)(2,1)}, bf16[128,2560]{1,0:T(8,128)(2,1)}, u32[]{:S(2)}, u32[]{:S(2)}) collective-permute-start(bf16[128,2560]{1,0:T(8,128)(2,1)} %get-tuple-element.49), channel_id=1, source_target_pairs={{0,8},{4,12},{8,0},{12,4},{16,24},{20,28},{24,16},{28,20},{1,9},{5... | collective-permute-start | bytes 1966088 | tf_op jit(solution)/shard_map/ppermute | solution.py:37
  86.8 31.3 %collective-permute-start.10 = (bf16[128,2560]{1,0:T(8,128)(2,1)}, bf16[128,2560]{1,0:T(8,128)(2,1)}, u32[]{:S(2)}, u32[]{:S(2)}) collective-permute-start(bf16[128,2560]{1,0:T(8,128)(2,1)} %get-tuple-element.50), channel_id=1, source_target_pairs={{0,12},{4,8},{8,4},{12,0},{16,28},{20,24},{24,20},{28,16},{1,13},{... | collective-permute-start | bytes 1966088 | tf_op jit(solution)/shard_map/ppermute | solution.py:37
  92.0 27.9 %collective-permute-start.11 = (bf16[128,2560]{1,0:T(8,128)(2,1)}, bf16[128,2560]{1,0:T(8,128)(2,1)}, u32[]{:S(2)}, u32[]{:S(2)}) collective-permute-start(bf16[128,2560]{1,0:T(8,128)(2,1)} %get-tuple-element.51), channel_id=1, source_target_pairs={{0,16},{4,20},{8,24},{12,28},{16,0},{20,4},{24,8},{28,12},{1,17},{... | collective-permute-start | bytes 1966088 | tf_op jit(solution)/shard_map/ppermute | solution.py:37
  93.5 30.8 %collective-permute-start.12 = (bf16[128,2560]{1,0:T(8,128)(2,1)}, bf16[128,2560]{1,0:T(8,128)(2,1)}, u32[]{:S(2)}, u32[]{:S(2)}) collective-permute-start(bf16[128,2560]{1,0:T(8,128)(2,1)} %get-tuple-element.52), channel_id=1, source_target_pairs={{0,20},{4,16},{8,28},{12,24},{16,4},{20,0},{24,12},{28,8},{1,21},{... | collective-permute-start | bytes 1966088 | tf_op jit(solution)/shard_map/ppermute | solution.py:37
  96.0 81.5 %collective-permute-start.25 = (bf16[320,3072]{1,0:T(8,128)(2,1)S(1)}, bf16[320,3072]{1,0:T(8,128)(2,1)S(1)}, u32[]{:S(2)}, u32[]{:S(2)}) collective-permute-start(bf16[320,3072]{1,0:T(8,128)(2,1)S(1)} %pad_maximum_fusion.refs_1_.refs_2_), channel_id=1, source_target_pairs={{0,4},{4,0},{8,12},{12,8},{16,20},{20,16},{24,28},{28,24},{1,5},{5... | collective-permute-start | bytes 5898248 | tf_op jit(solution)/shard_map/ppermute | solution.py:37
  107.0 49.9 %collective-permute-start.7 = (bf16[128,2560]{1,0:T(8,128)(2,1)}, bf16[128,2560]{1,0:T(8,128)(2,1)}, u32[]{:S(2)}, u32[]{:S(2)}) collective-permute-start(bf16[128,2560]{1,0:T(8,128)(2,1)} %get-tuple-element.46), channel_id=1, source_target_pairs={{0,4},{4,0},{8,12},{12,8},{16,20},{20,16},{24,28},{28,24},{1,5},{5... | collective-permute-start | bytes 1966088 | tf_op jit(solution)/shard_map/ppermute | solution.py:37
  118.1 21.0 %collective-permute-start.21 = (bf16[128,2560]{1,0:T(8,128)(2,1)S(1)}, bf16[128,2560]{1,0:T(8,128)(2,1)}, u32[]{:S(2)}, u32[]{:S(2)}) collective-permute-start(bf16[128,2560]{1,0:T(8,128)(2,1)S(1)} %pad_maximum_fusion.1.refs_0_), channel_id=1, source_target_pairs={{0,1},{1,0},{2,3},{3,2},{4,5},{5,4},{6,7},{7,6},{8,9},{9,8},{10,11... | collective-permute-start | bytes 1966088 | tf_op jit(solution)/shard_map/ppermute | solution.py:37
  119.9 32.2 %collective-permute-start.29 = (bf16[320,1536]{1,0:T(8,128)(2,1)S(1)}, bf16[320,1536]{1,0:T(8,128)(2,1)}, u32[]{:S(2)}, u32[]{:S(2)}) collective-permute-start(bf16[320,1536]{1,0:T(8,128)(2,1)S(1)} %slice.29), channel_id=1, source_target_pairs={{0,16},{4,20},{8,24},{12,28},{16,0},{20,4},{24,8},{28,12},{1,17},{... | collective-permute-start | bytes 2949128 | tf_op jit(solution)/shard_map/ppermute | solution.py:37
  124.4 24.9 %collective-permute-start.28 = (bf16[320,1536]{1,0:T(8,128)(2,1)}, bf16[320,1536]{1,0:T(8,128)(2,1)}, u32[]{:S(2)}, u32[]{:S(2)}) collective-permute-start(bf16[320,1536]{1,0:T(8,128)(2,1)} %slice.28), channel_id=1, source_target_pairs={{0,8},{4,12},{8,0},{12,4},{16,24},{20,28},{24,16},{28,20},{1,9},{5... | collective-permute-start | bytes 2949128 | tf_op jit(solution)/shard_map/ppermute | solution.py:37
  139.2 40.4 %collective-permute-start.27 = (bf16[320,3072]{1,0:T(8,128)(2,1)}, bf16[320,3072]{1,0:T(8,128)(2,1)S(1)}, u32[]{:S(2)}, u32[]{:S(2)}) collective-permute-start(bf16[320,3072]{1,0:T(8,128)(2,1)} %collective-permute-done.20.refs_5_.refs_6_), channel_id=1, source_target_pairs={{0,4},{4,0},{8,12},{12,8},{16,20},{20,16},{24,28},{28,24},{1,5},{5... | collective-permute-start | bytes 5898248 | tf_op jit(solution)/shard_map/ppermute | solution.py:37
  149.3 30.5 %collective-permute-start.26 = (bf16[320,3072]{1,0:T(8,128)(2,1)}, bf16[320,3072]{1,0:T(8,128)(2,1)}, u32[]{:S(2)}, u32[]{:S(2)}) collective-permute-start(bf16[320,3072]{1,0:T(8,128)(2,1)} %collective-permute-done.19.refs_3_.refs_4_), channel_id=1, source_target_pairs={{0,4},{4,0},{8,12},{12,8},{16,20},{20,16},{24,28},{28,24},{1,5},{5... | collective-permute-start | bytes 5898248 | tf_op jit(solution)/shard_map/ppermute | solution.py:37
  152.2 14.9 %collective-permute-start.22 = (bf16[128,1280]{1,0:T(8,128)(2,1)S(1)}, bf16[128,1280]{1,0:T(8,128)(2,1)S(1)}, u32[]{:S(2)}, u32[]{:S(2)}) collective-permute-start(bf16[128,1280]{1,0:T(8,128)(2,1)S(1)} %copy-done.35), channel_id=1, source_target_pairs={{0,1},{1,0},{2,3},{3,2},{4,5},{5,4},{6,7},{7,6},{8,9},{9,8},{10,11... | collective-permute-start | bytes 983048 | tf_op jit(solution)/shard_map/ppermute | solution.py:37
  156.9 40.4 %collective-permute-start.30 = (bf16[320,3072]{1,0:T(8,128)(2,1)}, bf16[320,3072]{1,0:T(8,128)(2,1)}, u32[]{:S(2)}, u32[]{:S(2)}) collective-permute-start(bf16[320,3072]{1,0:T(8,128)(2,1)} %constant_dynamic-update-slice_fusion.refs_8_), channel_id=1, source_target_pairs={{0,4},{4,0},{8,12},{12,8},{16,20},{20,16},{24,28},{28,24},{1,5},{5... | collective-permute-start | bytes 5898248 | tf_op jit(solution)/shard_map/ppermute | solution.py:37
  167.0 10.4 %collective-permute-start.39 = (bf16[128,1280]{1,0:T(8,128)(2,1)}, bf16[128,1280]{1,0:T(8,128)(2,1)S(1)}, u32[]{:S(2)}, u32[]{:S(2)}) collective-permute-start(bf16[128,1280]{1,0:T(8,128)(2,1)} %get-tuple-element.76), channel_id=1, source_target_pairs={{0,1},{1,0},{2,3},{3,2},{4,5},{5,4},{6,7},{7,6},{8,9},{9,8},{10,11... | collective-permute-start | bytes 983048 | tf_op jit(solution)/shard_map/ppermute | solution.py:37
  177.4 1.8 collective-permute-start.34
  177.6 14.6 %collective-permute-start.35 = (bf16[128,1280]{1,0:T(8,128)(2,1)}, bf16[128,1280]{1,0:T(8,128)(2,1)S(1)}, u32[]{:S(2)}, u32[]{:S(2)}) collective-permute-start(bf16[128,1280]{1,0:T(8,128)(2,1)} %get-tuple-element.71), channel_id=1, source_target_pairs={{0,8},{4,12},{8,0},{12,4},{16,24},{20,28},{24,16},{28,20},{1,9},{5... | collective-permute-start | bytes 983048 | tf_op jit(solution)/shard_map/ppermute | solution.py:37
  179.2 15.3 %collective-permute-start.36 = (bf16[128,1280]{1,0:T(8,128)(2,1)}, bf16[128,1280]{1,0:T(8,128)(2,1)S(1)}, u32[]{:S(2)}, u32[]{:S(2)}) collective-permute-start(bf16[128,1280]{1,0:T(8,128)(2,1)} %get-tuple-element.72), channel_id=1, source_target_pairs={{0,12},{4,8},{8,4},{12,0},{16,28},{20,24},{24,20},{28,16},{1,13},{... | collective-permute-start | bytes 983048 | tf_op jit(solution)/shard_map/ppermute | solution.py:37
  179.5 15.5 %collective-permute-start.37 = (bf16[128,1280]{1,0:T(8,128)(2,1)S(1)}, bf16[128,1280]{1,0:T(8,128)(2,1)S(1)}, u32[]{:S(2)}, u32[]{:S(2)}) collective-permute-start(bf16[128,1280]{1,0:T(8,128)(2,1)S(1)} %copy-done.34), channel_id=1, source_target_pairs={{0,16},{4,20},{8,24},{12,28},{16,0},{20,4},{24,8},{28,12},{1,17},{... | collective-permute-start | bytes 983048 | tf_op jit(solution)/shard_map/ppermute | solution.py:37
  179.8 16.7 %collective-permute-start.38 = (bf16[128,1280]{1,0:T(8,128)(2,1)S(1)}, bf16[128,1280]{1,0:T(8,128)(2,1)S(1)}, u32[]{:S(2)}, u32[]{:S(2)}) collective-permute-start(bf16[128,1280]{1,0:T(8,128)(2,1)S(1)} %copy-done.33), channel_id=1, source_target_pairs={{0,20},{4,16},{8,28},{12,24},{16,4},{20,0},{24,12},{28,8},{1,21},{... | collective-permute-start | bytes 983048 | tf_op jit(solution)/shard_map/ppermute | solution.py:37
  192.2 33.9 %collective-permute-start.8 = (bf16[128,1280]{1,0:T(8,128)(2,1)S(1)}, bf16[128,1280]{1,0:T(8,128)(2,1)S(1)}, u32[]{:S(2)}, u32[]{:S(2)}) collective-permute-start(bf16[128,1280]{1,0:T(8,128)(2,1)S(1)} %copy-done.32), channel_id=1, source_target_pairs={{0,4},{4,0},{8,12},{12,8},{16,20},{20,16},{24,28},{28,24},{1,5},{5... | collective-permute-start | bytes 983048 | tf_op jit(solution)/shard_map/ppermute | solution.py:37
  194.5 34.6 %collective-permute-start.13 = (bf16[128,1280]{1,0:T(8,128)(2,1)S(1)}, bf16[128,1280]{1,0:T(8,128)(2,1)S(1)}, u32[]{:S(2)}, u32[]{:S(2)}) collective-permute-start(bf16[128,1280]{1,0:T(8,128)(2,1)S(1)} %copy-done.31), channel_id=1, source_target_pairs={{0,8},{4,12},{8,0},{12,4},{16,24},{20,28},{24,16},{28,20},{1,9},{5... | collective-permute-start | bytes 983048 | tf_op jit(solution)/shard_map/ppermute | solution.py:37
  195.1 34.4 %collective-permute-start.14 = (bf16[128,1280]{1,0:T(8,128)(2,1)S(1)}, bf16[128,1280]{1,0:T(8,128)(2,1)S(1)}, u32[]{:S(2)}, u32[]{:S(2)}) collective-permute-start(bf16[128,1280]{1,0:T(8,128)(2,1)S(1)} %copy-done.30), channel_id=1, source_target_pairs={{0,12},{4,8},{8,4},{12,0},{16,28},{20,24},{24,20},{28,16},{1,13},{... | collective-permute-start | bytes 983048 | tf_op jit(solution)/shard_map/ppermute | solution.py:37
  196.5 17.8 %collective-permute-start.41 = (bf16[64,1280]{1,0:T(8,128)(2,1)S(1)}, bf16[64,1280]{1,0:T(8,128)(2,1)S(1)}, u32[]{:S(2)}, u32[]{:S(2)}) collective-permute-start(bf16[64,1280]{1,0:T(8,128)(2,1)S(1)} %get-tuple-element.83), channel_id=1, source_target_pairs={{0,28},{4,24},{8,20},{12,16},{16,12},{20,8},{24,4},{28,0},{1,29},{... | collective-permute-start | bytes 491528 | tf_op jit(solution)/shard_map/ppermute | solution.py:37
  197.2 21.0 %collective-permute-start.40 = (bf16[64,1280]{1,0:T(8,128)(2,1)S(1)}, bf16[64,1280]{1,0:T(8,128)(2,1)S(1)}, u32[]{:S(2)}, u32[]{:S(2)}) collective-permute-start(bf16[64,1280]{1,0:T(8,128)(2,1)S(1)} %get-tuple-element.84), channel_id=1, source_target_pairs={{0,24},{4,28},{8,16},{12,20},{16,8},{20,12},{24,0},{28,4},{1,25},{... | collective-permute-start | bytes 491528 | tf_op jit(solution)/shard_map/ppermute | solution.py:37
  214.3 17.2 %collective-permute-start.15 = (bf16[128,1280]{1,0:T(8,128)(2,1)S(1)}, bf16[128,1280]{1,0:T(8,128)(2,1)S(1)}, u32[]{:S(2)}, u32[]{:S(2)}) collective-permute-start(bf16[128,1280]{1,0:T(8,128)(2,1)S(1)} %copy-done.29), channel_id=1, source_target_pairs={{0,16},{4,20},{8,24},{12,28},{16,0},{20,4},{24,8},{28,12},{1,17},{... | collective-permute-start | bytes 983048 | tf_op jit(solution)/shard_map/ppermute | solution.py:37
  218.3 14.0 %collective-permute-start.16 = (bf16[128,1280]{1,0:T(8,128)(2,1)S(1)}, bf16[128,1280]{1,0:T(8,128)(2,1)S(1)}, u32[]{:S(2)}, u32[]{:S(2)}) collective-permute-start(bf16[128,1280]{1,0:T(8,128)(2,1)S(1)} %copy-done.28), channel_id=1, source_target_pairs={{0,20},{4,16},{8,28},{12,24},{16,4},{20,0},{24,12},{28,8},{1,21},{... | collective-permute-start | bytes 983048 | tf_op jit(solution)/shard_map/ppermute | solution.py:37
  226.1 26.7 %collective-permute-start.42 = (bf16[128,1280]{1,0:T(8,128)(2,1)}, bf16[128,1280]{1,0:T(8,128)(2,1)S(1)}, u32[]{:S(2)}, u32[]{:S(2)}) collective-permute-start(bf16[128,1280]{1,0:T(8,128)(2,1)} %get-tuple-element.78), channel_id=1, source_target_pairs={{0,3},{1,0},{2,1},{3,2},{4,7},{5,4},{6,5},{7,6},{8,11},{9,8},{10,9... | collective-permute-start | bytes 983048 | tf_op jit(solution)/shard_map/ppermute | solution.py:42
  229.1 30.0 %collective-permute-start.43 = (bf16[128,1280]{1,0:T(8,128)(2,1)}, bf16[128,1280]{1,0:T(8,128)(2,1)S(1)}, u32[]{:S(2)}, u32[]{:S(2)}) collective-permute-start(bf16[128,1280]{1,0:T(8,128)(2,1)} %get-tuple-element.79), channel_id=1, source_target_pairs={{0,2},{1,3},{2,0},{3,1},{4,6},{5,7},{6,4},{7,5},{8,10},{9,11},{10,... | collective-permute-start | bytes 983048 | tf_op jit(solution)/shard_map/ppermute | solution.py:42
  229.5 29.7 %collective-permute-start.44 = (bf16[128,1280]{1,0:T(8,128)(2,1)}, bf16[128,1280]{1,0:T(8,128)(2,1)S(1)}, u32[]{:S(2)}, u32[]{:S(2)}) collective-permute-start(bf16[128,1280]{1,0:T(8,128)(2,1)} %get-tuple-element.80), channel_id=1, source_target_pairs={{0,1},{1,2},{2,3},{3,0},{4,5},{5,6},{6,7},{7,4},{8,9},{9,10},{10,1... | collective-permute-start | bytes 983048 | tf_op jit(solution)/shard_map/ppermute | solution.py:42
  231.5 7.3 %collective-permute-start.24 = (bf16[64,1280]{1,0:T(8,128)(2,1)S(1)}, bf16[64,1280]{1,0:T(8,128)(2,1)S(1)}, u32[]{:S(2)}, u32[]{:S(2)}) collective-permute-start(bf16[64,1280]{1,0:T(8,128)(2,1)S(1)} %get-tuple-element.81), channel_id=1, source_target_pairs={{0,28},{4,24},{8,20},{12,16},{16,12},{20,8},{24,4},{28,0},{1,29},{... | collective-permute-start | bytes 491528 | tf_op jit(solution)/shard_map/ppermute | solution.py:37
  232.2 10.2 %collective-permute-start.23 = (bf16[64,1280]{1,0:T(8,128)(2,1)S(1)}, bf16[64,1280]{1,0:T(8,128)(2,1)S(1)}, u32[]{:S(2)}, u32[]{:S(2)}) collective-permute-start(bf16[64,1280]{1,0:T(8,128)(2,1)S(1)} %get-tuple-element.82), channel_id=1, source_target_pairs={{0,24},{4,28},{8,16},{12,20},{16,8},{20,12},{24,0},{28,4},{1,25},{... | collective-permute-start | bytes 491528 | tf_op jit(solution)/shard_map/ppermute | solution.py:37
  249.7 16.6 %collective-permute-start.31 = (bf16[128,1280]{1,0:T(8,128)(2,1)}, bf16[128,1280]{1,0:T(8,128)(2,1)S(1)}, u32[]{:S(2)}, u32[]{:S(2)}) collective-permute-start(bf16[128,1280]{1,0:T(8,128)(2,1)} %get-tuple-element.66), channel_id=1, source_target_pairs={{0,3},{1,0},{2,1},{3,2},{4,7},{5,4},{6,5},{7,6},{8,11},{9,8},{10,9... | collective-permute-start | bytes 983048 | tf_op jit(solution)/shard_map/ppermute | solution.py:42
  251.6 35.6 %collective-permute-start.32 = (bf16[128,1280]{1,0:T(8,128)(2,1)}, bf16[128,1280]{1,0:T(8,128)(2,1)S(1)}, u32[]{:S(2)}, u32[]{:S(2)}) collective-permute-start(bf16[128,1280]{1,0:T(8,128)(2,1)} %get-tuple-element.67), channel_id=1, source_target_pairs={{0,2},{1,3},{2,0},{3,1},{4,6},{5,7},{6,4},{7,5},{8,10},{9,11},{10,... | collective-permute-start | bytes 983048 | tf_op jit(solution)/shard_map/ppermute | solution.py:42
  252.8 34.4 %collective-permute-start.33 = (bf16[128,1280]{1,0:T(8,128)(2,1)}, bf16[128,1280]{1,0:T(8,128)(2,1)S(1)}, u32[]{:S(2)}, u32[]{:S(2)}) collective-permute-start(bf16[128,1280]{1,0:T(8,128)(2,1)} %get-tuple-element.68), channel_id=1, source_target_pairs={{0,1},{1,2},{2,3},{3,0},{4,5},{5,6},{6,7},{7,4},{8,9},{9,10},{10,1... | collective-permute-start | bytes 983048 | tf_op jit(solution)/shard_map/ppermute | solution.py:42
  (34 other events, 386.6 us)

commit v3 on v2

--- a/solution.py
+++ b/solution.py
@@ -12,6 +12,7 @@
 BF16 = jnp.bfloat16
 LANES = 128
 PARTS = 2
+FIRST_PART = 3, 5
 VMEM_BYTES = 56 * 1024 * 1024
 VMEM_SPEC = pl.BlockSpec(memory_space=pltpu.VMEM)
 ANY_SPEC = pl.BlockSpec(memory_space=pl.ANY)
@@ -70,6 +71,18 @@
     return add(part[0], *[ring(part[k], -k) for k in range(1, count)])
 
 
+def line_scatter_staged(part, place, count):
+    if count != 4:
+        return line_scatter(part, count)
+    odd = (place & 1) > 0
+    inward = jnp.where(odd, part[3], part[1])
+    ahead = lax.ppermute(inward, "tensor", [(0, 1), (3, 2)])
+    middle = lax.ppermute(inward, "tensor", [(1, 2), (2, 1)])
+    direct = ring(add(part[2], ahead), 2)
+    outer = swap(jnp.where(odd, part[1], part[3]), "tensor", 1)
+    return add(part[0], direct, outer, middle)
+
+
 def with_partner(held):
     return {**held, **{o + 1: swap(b, "expert", 1) for o, b in held.items()}}
 
@@ -163,6 +176,19 @@
     return begin, lambda: each(tiles, finish)
 
 
+def column_cuts(width):
+    above, below = FIRST_PART
+    first = max(LANES, width * above // below // LANES * LANES)
+    return [(0, first), (first, width - first)]
+
+
+def part_tile(width):
+    for tile in (512, 256, LANES):
+        if all(base % tile == 0 and wide % tile == 0 for base, wide in column_cuts(width)):
+            return tile
+    raise ValueError(width)
+
+
 def take(refs, *counts):
     out, at = [], 0
     for count in counts:
@@ -215,12 +241,11 @@
         refs, count, None, None, None, PARTS * count
     )
     inner, outer = down.shape
-    ins, os = tiles_of(inner // 2), tiles_of(outer // PARTS)
-    tile = outer // PARTS // os
+    ins, tiles = tiles_of(inner // 2), outer // part_tile(outer)
     wait_x = stack(blocks, x, sems[0])
     wait_gate = columns_in(gate_w.at[0], gate, ins, sems[1])
     wait_up = columns_in(up_w.at[0], upper, ins, sems[2])
-    wait_down = columns_in(down_w.at[0], down, PARTS * os, sems[3])
+    wait_down = columns_in(down_w.at[0], down, tiles, sems[3])
     wait_x()
 
     def one(n):
@@ -231,20 +256,20 @@
         hidden[:, at] = (jax.nn.silu(g) * dot(x[...], upper[:, at])).astype(BF16)
 
     each(ins, one)
-    finishes = []
-    for c in range(PARTS):
+    finishes, tile = [], outer // tiles
+    for c, (base, width) in enumerate(column_cuts(outer)):
         begin, finish = rows_out(
-            made, outs[c * count:(c + 1) * count], os, sems[4].at[c], c * outer // PARTS
+            made, outs[c * count:(c + 1) * count], width // tile, sems[4].at[c], base
         )
         finishes.append(finish)
 
         def two(n):
-            wait_down(c * os + n)
-            at = pl.ds(pl.multiple_of((c * os + n) * tile, LANES), tile)
+            wait_down(base // tile + n)
+            at = pl.ds(pl.multiple_of(base + n * tile, LANES), tile)
             made[:, at] = dot(hidden[...], down[:, at]).astype(BF16)
             begin(n)
 
-        each(os, two)
+        each(width // tile, two)
     for finish in finishes:
         finish()
 
@@ -406,12 +431,12 @@
 def expert_rows(blocks, w_gate, w_up, w_down):
     inner, width = w_down.shape[1:]
     rows, count = sum(b.shape[0] for b in blocks), len(blocks)
-    ins, outs = tiles_of(inner // 2), tiles_of(width // PARTS)
+    ins, outs = tiles_of(inner // 2), width // part_tile(width)
     made = call(
         functools.partial(expert_kernel, count),
         [*blocks, w_gate, w_up, w_down],
         (),
-        [((b.shape[0], width // PARTS), BF16) for b in blocks] * PARTS,
+        [((b.shape[0], wide), BF16) for _, wide in column_cuts(width) for b in blocks],
         [
             pltpu.VMEM((rows, width), BF16),
             pltpu.VMEM((width, inner), BF16),
@@ -422,7 +447,7 @@
             dma(count),
             dma(ins),
             dma(ins),
-            dma(PARTS * outs),
+            dma(outs),
             dma(PARTS, count, outs),
         ],
         6 * rows * inner * width,
@@ -590,9 +615,11 @@
 
     notes = jnp.stack([slot.astype(F32), scale], axis=1)
     outs = []
-    for c in range(PARTS):
-        parts = combine([home[c][o] for o in range(size)], notes, shared, count, c * width // PARTS)
-        outs.append(line_scatter(parts, count))
+    for c, (start, _) in enumerate(column_cuts(width)):
+        parts = combine(
+            [home[c][o] for o in range(size)], notes, shared, count, start
+        )
+        outs.append(line_scatter_staged(parts, place, count))
     return jnp.concatenate(outs, axis=1)
 
 

time: 290 us -> 295 us (1.017)
  starting transfers between devices: 49.6 us -> 58.5 us
  Pallas kernels: 75.7 us -> 71.9 us
    ppermute x0 -> x4, starting transfers between devices: none -> 6.84 us  [the longest x2 5.48 us: line_scatter_staged(): ahead = lax.ppermute(inward, 'tensor', [(0, 1), (3, 2)])]
    ppermute x10 -> x6, waiting for transfers between devices: 54.9 us -> 48.9 us  [ring(): lax.ppermute(block, 'tensor', [(i, (i + step) % count) for i in range(cou...]
    pallas_call x8, Pallas kernels: 75.7 us -> 71.9 us  [call(): pl.pallas_call(kernel, out_shape=[jax.ShapeDtypeStruct(shape, kind) for s...]
    ppermute x33 -> x35, starting transfers between devices: 30 us -> 32.4 us  [swap(): return lax.ppermute(block, axis, [(i, i ^ bits) for i in range(size)])]
    ppermute x33 -> x35, waiting for transfers between devices: 81 us -> 82.9 us  [swap(): return lax.ppermute(block, axis, [(i, i ^ bits) for i in range(size)])]
    ppermute x10 -> x6, starting transfers between devices: 17.6 us -> 17.2 us  [ring(): lax.ppermute(block, 'tensor', [(i, (i + step) % count) for i in range(cou...]
  transfers between devices with their start and end apart: 45 -> 47, of which waited for: 19 -> 18; matrix products, arithmetic and copies ran while one was open for 4% -> 5% of each run, Pallas kernels for 26% -> 24%
where the time goes in v3:
time: 295 us
  waiting for transfers between devices  146 us (49%)
  Pallas kernels  71.9 us (24%)
  starting transfers between devices  58.5 us (20%)
  local copies, waits for them, and re-layouts  10.6 us (4%)
  other arithmetic  6.58 us (2%)
    ppermute x35, waiting for transfers between devices, swap(): return lax.ppermute(block, axis, [(i, i ^ bits) for i in range(size)])  82.9 us
    pallas_call x8, Pallas kernels, call(): pl.pallas_call(kernel, out_shape=[jax.ShapeDtypeStruct(shape, kind) for s...  71.9 us
    ppermute x6, waiting for transfers between devices, ring(): lax.ppermute(block, 'tensor', [(i, (i + step) % count) for i in range(cou...  48.9 us
    ppermute x35, starting transfers between devices, swap(): return lax.ppermute(block, axis, [(i, i ^ bits) for i in range(size)])  32.4 us
    ppermute x6, starting transfers between devices, ring(): lax.ppermute(block, 'tensor', [(i, (i + step) % count) for i in range(cou...  17.2 us
    ppermute x1, waiting for transfers between devices, line_gather(): ahead = lax.ppermute(direct, 'tensor', [(2, 3), (1, 0)])  11.8 us
  transfers between devices with their start and end apart: 47, of which 18 were waited for; matrix products, arithmetic and copies ran while one was open for 5% of the time, Pallas kernels for 24%

profile of v3, /device:TPU:0, one launch (start us, length us, event | category | flops | bytes accessed | tf_op | source)
XLA Modules:
  0.0 294.7 jit_solution(12074616364697261518)
XLA Ops:
  0.0 4.1 %collective-permute-start = (bf16[128,2560]{1,0:T(8,128)(2,1)}, bf16[128,2560]{1,0:T(8,128)(2,1)}, u32[]{:S(2)}, u32[]{:S(2)}) collective-permute-start(bf16[128,2560]{1,0:T(8,128)(2,1)} %refs_0_.1), channel_id=1, source_target_pairs={{0,2},{1,3},{2,0},{3,1},{4,6},{5,7},{6,4},{7,5},{8,10},{9,11},{10,... | collective-permute-start | bytes 1966088 | tf_op jit(solution)/shard_map/ppermute | solution.py:43
  4.1 1.7 pad_maximum_fusion.refs_1_.refs_2_
  5.8 1.6 collective-permute-start.20
  8.8 1.7 collective-permute-start.5
  10.5 22.7 %collective-permute-done.refs_1_ = bf16[128,2560]{1,0:T(8,128)(2,1)} collective-permute-done((bf16[128,2560]{1,0:T(8,128)(2,1)}, bf16[128,2560]{1,0:T(8,128)(2,1)}, u32[]{:S(2)}, u32[]{:S(2)}) %collective-permute-start) | collective-permute-done | bytes 655392 | tf_op jit(solution)/shard_map/ppermute | solution.py:43
  33.2 1.5 collective-permute-start.19
  38.5 13.9 %collective-permute-done.1.refs_2_ = bf16[128,2560]{1,0:T(8,128)(2,1)S(1)} collective-permute-done((bf16[128,2560]{1,0:T(8,128)(2,1)S(1)}, bf16[128,2560]{1,0:T(8,128)(2,1)S(1)}, u32[]{:S(2)}, u32[]{:S(2)}) %collective-permute-start.1) | collective-permute-done | bytes 655392 | tf_op jit(solution)/shard_map/ppermute | solution.py:38
  52.5 11.8 %collective-permute-done.2.refs_3_ = bf16[128,2560]{1,0:T(8,128)(2,1)S(1)} collective-permute-done((bf16[128,2560]{1,0:T(8,128)(2,1)}, bf16[128,2560]{1,0:T(8,128)(2,1)S(1)}, u32[]{:S(2)}, u32[]{:S(2)}) %collective-permute-start.2) | collective-permute-done | bytes 655392 | tf_op jit(solution)/shard_map/ppermute | solution.py:60
  65.1 7.1 %shard_map.91 = (bf16[128,2560]{1,0:T(8,128)(2,1)}, bf16[128,2560]{1,0:T(8,128)(2,1)}, bf16[128,2560]{1,0:T(8,128)(2,1)}, bf16[128,2560]{1,0:T(8,128)(2,1)}, bf1...) custom-call(bf16[128,2560]{1,0:T(8,128)(2,1)} %refs_0_.1, ...), custom_call_target="tpu_custom_call" | custom-call | flops 2348810240 | bytes 9830400 | tf_op jit(solution)/shard_map/pallas_call | solution.py:391
  72.2 1.6 collective-permute-start.17
  73.8 1.5 collective-permute-start.9
  75.3 11.7 %collective-permute-done.17 = bf16[64,2560]{1,0:T(8,128)(2,1)S(1)} collective-permute-done((bf16[64,2560]{1,0:T(8,128)(2,1)}, bf16[64,2560]{1,0:T(8,128)(2,1)S(1)}, u32[]{:S(2)}, u32[]{:S(2)}) %collective-permute-start.17) | collective-permute-done | bytes 327712 | tf_op jit(solution)/shard_map/ppermute | solution.py:38
  86.9 5.2 %collective-permute-done.18 = bf16[64,2560]{1,0:T(8,128)(2,1)S(1)} collective-permute-done((bf16[64,2560]{1,0:T(8,128)(2,1)}, bf16[64,2560]{1,0:T(8,128)(2,1)S(1)}, u32[]{:S(2)}, u32[]{:S(2)}) %collective-permute-start.18) | collective-permute-done | bytes 327712 | tf_op jit(solution)/shard_map/ppermute | solution.py:38
  92.1 1.5 collective-permute-start.11
  93.6 1.5 collective-permute-start.12
  96.2 2.3 slice.28
  99.8 7.3 %collective-permute-done.9.refs_0_ = bf16[128,2560]{1,0:T(8,128)(2,1)} collective-permute-done((bf16[128,2560]{1,0:T(8,128)(2,1)}, bf16[128,2560]{1,0:T(8,128)(2,1)}, u32[]{:S(2)}, u32[]{:S(2)}) %collective-permute-start.9) | collective-permute-done | bytes 655392 | tf_op jit(solution)/shard_map/ppermute | solution.py:38
  107.1 11.1 %collective-permute-done.10.refs_1_ = bf16[128,2560]{1,0:T(8,128)(2,1)} collective-permute-done((bf16[128,2560]{1,0:T(8,128)(2,1)}, bf16[128,2560]{1,0:T(8,128)(2,1)}, u32[]{:S(2)}, u32[]{:S(2)}) %collective-permute-start.10) | collective-permute-done | bytes 655392 | tf_op jit(solution)/shard_map/ppermute | solution.py:38
  118.2 1.7 collective-permute-start.21
  119.9 1.5 collective-permute-start.29
  121.5 3.1 %collective-permute-done.12.refs_3_ = bf16[128,2560]{1,0:T(8,128)(2,1)} collective-permute-done((bf16[128,2560]{1,0:T(8,128)(2,1)}, bf16[128,2560]{1,0:T(8,128)(2,1)}, u32[]{:S(2)}, u32[]{:S(2)}) %collective-permute-start.12) | collective-permute-done | bytes 655392 | tf_op jit(solution)/shard_map/ppermute | solution.py:38
  124.6 14.0 %shard_map.93 = (bf16[128,1536]{1,0:T(8,128)(2,1)}, bf16[128,1536]{1,0:T(8,128)(2,1)}, bf16[128,1536]{1,0:T(8,128)(2,1)}, bf16[128,1536]{1,0:T(8,128)(2,1)}, bf1...) custom-call(bf16[128,2560]{1,0:T(8,128)(2,1)} %collective-permute-don, ...), custom_call_target="tpu_custom_call" | custom-call | flops 8053063680 | bytes 20971520 | tf_op jit(solution)/shard_map/pallas_call | solution.py:391
  138.7 9.1 %shard_map.94 = (bf16[128,1536]{1,0:T(8,128)(2,1)}, bf16[128,1536]{1,0:T(8,128)(2,1)}, bf16[128,1024]{1,0:T(8,128)(2,1)}, bf16[128,1024]{1,0:T(8,128)(2,1)}) custom-call(bf16[128,2560]{1,0:T(8,128)(2,1)} %copy-done.3, bf16[128,2560]{1,0:T(8,128)(2,1)} %collective-permute-done.21.refs_1_, bf16[1,2560,1024]{2,1,0:T(8,128)(2,1)} %refs_2_.3, ...), custom_call_target="tpu_custom_call" | custom-call | flops 4026531840 | bytes 18350080 | tf_op jit(solution)/shard_map/pallas_call | solution.py:391
  148.4 2.3 constant_dynamic-update-slice_fusion.1
  150.6 2.4 collective-permute-start.40
  153.0 2.2 constant_dynamic-update-slice_fusion.refs_8_
  155.3 9.2 %shard_map.92 = (bf16[128,1536]{1,0:T(8,128)(2,1)}, bf16[128,1536]{1,0:T(8,128)(2,1)}, bf16[128,1024]{1,0:T(8,128)(2,1)}, bf16[128,1024]{1,0:T(8,128)(2,1)}) custom-call(bf16[128,2560]{1,0:T(8,128)(2,1)} %get-tuple-element.45.refs_0_, bf16[128,2560]{1,0:T(8,128)(2,1)} %collective-permute-done.7.refs_1_, bf16[1,2560,1024]{2,1,0:T(8,128)(2,1)} %refs_2_.3, ...), custom_call_target="tpu_custom_call" | custom-call | flops 4026531840 | bytes 18350080 | tf_op jit(solution)/shard_map/pallas_call | solution.py:391
  164.7 11.4 %collective-permute-done.22 = bf16[128,1536]{1,0:T(8,128)(2,1)S(1)} collective-permute-done((bf16[128,1536]{1,0:T(8,128)(2,1)S(1)}, bf16[128,1536]{1,0:T(8,128)(2,1)S(1)}, u32[]{:S(2)}, u32[]{:S(2)}) %collective-permute-start.22) | collective-permute-done | bytes 393248 | tf_op jit(solution)/shard_map/ppermute | solution.py:38
  178.2 7.2 %collective-permute-done.36.refs_2_ = bf16[128,1024]{1,0:T(8,128)(2,1)S(1)} collective-permute-done((bf16[128,1024]{1,0:T(8,128)(2,1)S(1)}, bf16[128,1024]{1,0:T(8,128)(2,1)S(1)}, u32[]{:S(2)}, u32[]{:S(2)}) %collective-permute-start.36) | collective-permute-done | bytes 262176 | tf_op jit(solution)/shard_map/ppermute | solution.py:38
  185.5 4.7 %collective-permute-done.37.refs_3_ = bf16[128,1024]{1,0:T(8,128)(2,1)S(1)} collective-permute-done((bf16[128,1024]{1,0:T(8,128)(2,1)S(1)}, bf16[128,1024]{1,0:T(8,128)(2,1)S(1)}, u32[]{:S(2)}, u32[]{:S(2)}) %collective-permute-start.37) | collective-permute-done | bytes 262176 | tf_op jit(solution)/shard_map/ppermute | solution.py:38
  190.3 1.5 collective-permute-start.42
  191.9 1.5 collective-permute-start.41
  193.4 10.9 %shard_map.95.refs_0_ = f32[512,2048]{1,0:T(8,128)} custom-call(bf16[512,2560]{1,0:T(8,128)(2,1)} %get-tuple-element.62.refs_0_.refs_1_, bf16[320,3072]{1,0:T(8,128)(2,1)} %copy-done, bf16[320,3072]{1,0:T(8,128)(2,1)} %copy-done.1, bf16[320,3072]{1,0:T(8,128)(2,1)} %collective-permute-done.19.refs_3_.refs_4_, ...), custom_call_target="tpu_custom_call" | custom-call | flops 4026531840 | bytes 12058624 | tf_op jit(solution)/shard_map/pallas_call | solution.py:391
  206.4 1.6 collective-permute-start.15
  208.3 10.1 %shard_map.96.refs_9_ = f32[512,2560]{1,0:T(8,128)} custom-call(f32[512,2048]{1,0:T(8,128)} %shard_map.95.refs_0_, bf16[512,2560]{1,0:T(8,128)(2,1)} %get-tuple-element.62.refs_0_.refs_1_, bf16[320,3072]{1,0:T(8,128)(2,1)} %copy-done, bf16[320,3072]{1,0:T(8,128)(2,1)} %copy-done.1, bf16[320,3072]{1,0:T(8,128)(2,1)} %collective-permute-done.19.refs_3_.refs_4_, ...), custom_call_target="tpu_custom_call" | custom-call | flops 4026531840 | bytes 14680064 | tf_op jit(solution)/shard_map/pallas_call | solution.py:391
  218.4 5.1 %shard_map.98 = (bf16[128,1024]{1,0:T(8,128)(2,1)}, bf16[128,1024]{1,0:T(8,128)(2,1)}, bf16[128,1024]{1,0:T(8,128)(2,1)}, bf16[128,1024]{1,0:T(8,128)(2,1)}) custom-call(bf16[128,1024]{1,0:T(8,128)(2,1)} %get-tuple-element.69.refs_0_, bf16[128,1024]{1,0:T(8,128)(2,1)} %copy-done.13, bf16[128,1024]{1,0:T(8,128)(2,1)} %copy-done.15, ...), custom_call_target="tpu_custom_call" | custom-call | flops 939524096 | bytes 4980736 | tf_op jit(solution)/shard_map/pallas_call | solution.py:391
  223.5 1.4 collective-permute-start.24
  225.0 1.5 collective-permute-start.23
  227.6 2.6 collective-permute-start.43
  231.2 4.7 %collective-permute-done.23.refs_6_ = bf16[64,1536]{1,0:T(8,128)(2,1)S(1)} collective-permute-done((bf16[64,1536]{1,0:T(8,128)(2,1)S(1)}, bf16[64,1536]{1,0:T(8,128)(2,1)S(1)}, u32[]{:S(2)}, u32[]{:S(2)}) %collective-permute-start.23) | collective-permute-done | bytes 196640 | tf_op jit(solution)/shard_map/ppermute | solution.py:38
  236.6 6.4 %shard_map.97 = (bf16[128,1536]{1,0:T(8,128)(2,1)}, bf16[128,1536]{1,0:T(8,128)(2,1)}, bf16[128,1536]{1,0:T(8,128)(2,1)}, bf16[128,1536]{1,0:T(8,128)(2,1)}) custom-call(bf16[128,1536]{1,0:T(8,128)(2,1)} %get-tuple-element.47.refs_0_, bf16[128,1536]{1,0:T(8,128)(2,1)} %copy-done.4, bf16[128,1536]{1,0:T(8,128)(2,1)} %copy-done.5, ...), custom_call_target="tpu_custom_call" | custom-call | flops 1409286144 | bytes 7471104 | tf_op jit(solution)/shard_map/pallas_call | solution.py:391
  244.2 2.9 collective-permute-start.31
  248.5 5.0 %collective-permute-start.45 = (bf16[128,1024]{1,0:T(8,128)(2,1)S(1)}, bf16[128,1024]{1,0:T(8,128)(2,1)S(1)}, u32[]{:S(2)}, u32[]{:S(2)}) collective-permute-start(bf16[128,1024]{1,0:T(8,128)(2,1)S(1)} %get-tuple-element.83), channel_id=1, source_target_pairs={{0,1},{1,0},{2,3},{3,2},{4,5},{5,4},{6,7},{7,6},{8,9},{9,8},{10,11... | collective-permute-start | bytes 786440 | tf_op jit(solution)/shard_map/ppermute | solution.py:38
  253.7 2.9 collective-permute-done.31
  256.6 5.0 %collective-permute-start.44 = (bf16[128,1024]{1,0:T(8,128)(2,1)S(1)}, bf16[128,1024]{1,0:T(8,128)(2,1)S(1)}, u32[]{:S(2)}, u32[]{:S(2)}) collective-permute-start(bf16[128,1024]{1,0:T(8,128)(2,1)S(1)} %add_convert_fusion.4), channel_id=1, source_target_pairs={{0,2},{1,3},{2,0},{3,1},{4,6},{5,7},{6,4},{7,5},{8,10},{9,11},{10,... | collective-permute-start | bytes 786440 | tf_op jit(solution)/shard_map/ppermute | solution.py:43
  262.2 5.0 %collective-permute-start.32 = (bf16[128,1536]{1,0:T(8,128)(2,1)S(1)}, bf16[128,1536]{1,0:T(8,128)(2,1)S(1)}, u32[]{:S(2)}, u32[]{:S(2)}) collective-permute-start(bf16[128,1536]{1,0:T(8,128)(2,1)S(1)} %add_convert_fusion.1), channel_id=1, source_target_pairs={{0,2},{1,3},{2,0},{3,1},{4,6},{5,7},{6,4},{7,5},{8,10},{9,11},{10,... | collective-permute-start | bytes 1179656 | tf_op jit(solution)/shard_map/ppermute | solution.py:43
  267.2 9.0 %collective-permute-done.44 = bf16[128,1024]{1,0:T(8,128)(2,1)S(1)} collective-permute-done((bf16[128,1024]{1,0:T(8,128)(2,1)S(1)}, bf16[128,1024]{1,0:T(8,128)(2,1)S(1)}, u32[]{:S(2)}, u32[]{:S(2)}) %collective-permute-start.44) | collective-permute-done | bytes 262176 | tf_op jit(solution)/shard_map/ppermute | solution.py:43
  276.5 17.1 %collective-permute-done.32 = bf16[128,1536]{1,0:T(8,128)(2,1)S(1)} collective-permute-done((bf16[128,1536]{1,0:T(8,128)(2,1)S(1)}, bf16[128,1536]{1,0:T(8,128)(2,1)S(1)}, u32[]{:S(2)}, u32[]{:S(2)}) %collective-permute-start.32) | collective-permute-done | bytes 393248 | tf_op jit(solution)/shard_map/ppermute | solution.py:43
  (161 shorter events, 21.1 us)
Async XLA Ops:
  0.0 33.2 %collective-permute-start = (bf16[128,2560]{1,0:T(8,128)(2,1)}, bf16[128,2560]{1,0:T(8,128)(2,1)}, u32[]{:S(2)}, u32[]{:S(2)}) collective-permute-start(bf16[128,2560]{1,0:T(8,128)(2,1)} %refs_0_.1), channel_id=1, source_target_pairs={{0,2},{1,3},{2,0},{3,1},{4,6},{5,7},{6,4},{7,5},{8,10},{9,11},{10,... | collective-permute-start | bytes 1966088 | tf_op jit(solution)/shard_map/ppermute | solution.py:43
  5.8 90.3 %copy-start = (bf16[320,3072]{1,0:T(8,128)(2,1)}, bf16[320,3072]{1,0:T(8,128)(2,1)S(1)}, u32[]{:S(2)}) copy-start(bf16[320,3072]{1,0:T(8,128)(2,1)S(1)} %pad_maximum_fusion.refs_1_.refs_2_) | copy-start | bytes 5898244
  5.8 87.9 %collective-permute-start.20 = (bf16[320,3072]{1,0:T(8,128)(2,1)S(1)}, bf16[320,3072]{1,0:T(8,128)(2,1)}, u32[]{:S(2)}, u32[]{:S(2)}) collective-permute-start(bf16[320,3072]{1,0:T(8,128)(2,1)S(1)} %pad_maximum_fusion.refs_1_.refs_2_), channel_id=1, source_target_pairs={{0,16},{4,20},{8,24},{12,28},{16,0},{20,4},{24,8},{28,12},{1,17},{... | collective-permute-start | bytes 5898248 | tf_op jit(solution)/shard_map/ppermute | solution.py:38
  7.4 27.4 %collective-permute-start.6 = (f32[2,128]{1,0:T(2,128)S(1)}, f32[2,128]{1,0:T(2,128)S(1)}, u32[]{:S(2)}, u32[]{:S(2)}) collective-permute-start(f32[2,128]{1,0:T(2,128)S(1)} %pad_maximum_fusion.5), channel_id=1, source_target_pairs={{0,3},{1,0},{2,1},{3,2},{4,7},{5,4},{6,5},{7,6},{8,11},{9,8},{10,9... | collective-permute-start | bytes 3080 | tf_op jit(solution)/shard_map/ppermute | solution.py:43
  8.8 26.7 %collective-permute-start.5 = (f32[2,128]{1,0:T(2,128)S(1)}, f32[2,128]{1,0:T(2,128)S(1)}, u32[]{:S(2)}, u32[]{:S(2)}) collective-permute-start(f32[2,128]{1,0:T(2,128)S(1)} %pad_maximum_fusion.5), channel_id=1, source_target_pairs={{0,2},{1,3},{2,0},{3,1},{4,6},{5,7},{6,4},{7,5},{8,10},{9,11},{10,... | collective-permute-start | bytes 3080 | tf_op jit(solution)/shard_map/ppermute | solution.py:43
  10.5 25.8 %collective-permute-start.4 = (f32[2,128]{1,0:T(2,128)S(1)}, f32[2,128]{1,0:T(2,128)S(1)}, u32[]{:S(2)}, u32[]{:S(2)}) collective-permute-start(f32[2,128]{1,0:T(2,128)S(1)} %pad_maximum_fusion.5), channel_id=1, source_target_pairs={{0,1},{1,2},{2,3},{3,0},{4,5},{5,6},{6,7},{7,4},{8,9},{9,10},{10,1... | collective-permute-start | bytes 3080 | tf_op jit(solution)/shard_map/ppermute | solution.py:43
  33.2 62.9 %collective-permute-start.19 = (bf16[320,3072]{1,0:T(8,128)(2,1)S(1)}, bf16[320,3072]{1,0:T(8,128)(2,1)}, u32[]{:S(2)}, u32[]{:S(2)}) collective-permute-start(bf16[320,3072]{1,0:T(8,128)(2,1)S(1)} %pad_maximum_fusion.refs_1_.refs_2_), channel_id=1, source_target_pairs={{0,8},{4,12},{8,0},{12,4},{16,24},{20,28},{24,16},{28,20},{1,9},{5... | collective-permute-start | bytes 5898248 | tf_op jit(solution)/shard_map/ppermute | solution.py:38
  34.8 17.7 %collective-permute-start.1 = (bf16[128,2560]{1,0:T(8,128)(2,1)S(1)}, bf16[128,2560]{1,0:T(8,128)(2,1)S(1)}, u32[]{:S(2)}, u32[]{:S(2)}) collective-permute-start(bf16[128,2560]{1,0:T(8,128)(2,1)S(1)} %copy-done.26), channel_id=1, source_target_pairs={{0,1},{1,0},{2,3},{3,2},{4,5},{5,4},{6,7},{7,6},{8,9},{9,8},{10,11... | collective-permute-start | bytes 1966088 | tf_op jit(solution)/shard_map/ppermute | solution.py:38
  35.5 16.9 %collective-permute-start.3 = (bf16[128,2560]{1,0:T(8,128)(2,1)S(1)}, bf16[128,2560]{1,0:T(8,128)(2,1)S(1)}, u32[]{:S(2)}, u32[]{:S(2)}) collective-permute-start(bf16[128,2560]{1,0:T(8,128)(2,1)S(1)} %copy-done.26), channel_id=1, source_target_pairs={{1,2},{2,1},{5,6},{6,5},{9,10},{10,9},{13,14},{14,13},{17,18},{18,... | collective-permute-start | bytes 1966088 | tf_op jit(solution)/shard_map/ppermute | solution.py:61
  36.2 28.0 %collective-permute-start.2 = (bf16[128,2560]{1,0:T(8,128)(2,1)}, bf16[128,2560]{1,0:T(8,128)(2,1)S(1)}, u32[]{:S(2)}, u32[]{:S(2)}) collective-permute-start(bf16[128,2560]{1,0:T(8,128)(2,1)} %collective-permute-done.refs_1_), channel_id=1, source_target_pairs={{2,3},{1,0},{6,7},{5,4},{10,11},{9,8},{14,15},{13,12},{18,19},{17,... | collective-permute-start | bytes 1966088 | tf_op jit(solution)/shard_map/ppermute | solution.py:60
  72.2 14.7 %collective-permute-start.17 = (bf16[64,2560]{1,0:T(8,128)(2,1)}, bf16[64,2560]{1,0:T(8,128)(2,1)S(1)}, u32[]{:S(2)}, u32[]{:S(2)}) collective-permute-start(bf16[64,2560]{1,0:T(8,128)(2,1)} %get-tuple-element.57), channel_id=1, source_target_pairs={{0,24},{4,28},{8,16},{12,20},{16,8},{20,12},{24,0},{28,4},{1,25},{... | collective-permute-start | bytes 983048 | tf_op jit(solution)/shard_map/ppermute | solution.py:38
  73.8 18.3 %collective-permute-start.18 = (bf16[64,2560]{1,0:T(8,128)(2,1)}, bf16[64,2560]{1,0:T(8,128)(2,1)S(1)}, u32[]{:S(2)}, u32[]{:S(2)}) collective-permute-start(bf16[64,2560]{1,0:T(8,128)(2,1)} %get-tuple-element.58), channel_id=1, source_target_pairs={{0,28},{4,24},{8,20},{12,16},{16,12},{20,8},{24,4},{28,0},{1,29},{... | collective-permute-start | bytes 983048 | tf_op jit(solution)/shard_map/ppermute | solution.py:38
  73.8 33.3 %collective-permute-start.9 = (bf16[128,2560]{1,0:T(8,128)(2,1)}, bf16[128,2560]{1,0:T(8,128)(2,1)}, u32[]{:S(2)}, u32[]{:S(2)}) collective-permute-start(bf16[128,2560]{1,0:T(8,128)(2,1)} %get-tuple-element.49), channel_id=1, source_target_pairs={{0,8},{4,12},{8,0},{12,4},{16,24},{20,28},{24,16},{28,20},{1,9},{5... | collective-permute-start | bytes 1966088 | tf_op jit(solution)/shard_map/ppermute | solution.py:38
  86.9 31.3 %collective-permute-start.10 = (bf16[128,2560]{1,0:T(8,128)(2,1)}, bf16[128,2560]{1,0:T(8,128)(2,1)}, u32[]{:S(2)}, u32[]{:S(2)}) collective-permute-start(bf16[128,2560]{1,0:T(8,128)(2,1)} %get-tuple-element.50), channel_id=1, source_target_pairs={{0,12},{4,8},{8,4},{12,0},{16,28},{20,24},{24,20},{28,16},{1,13},{... | collective-permute-start | bytes 1966088 | tf_op jit(solution)/shard_map/ppermute | solution.py:38
  92.1 27.8 %collective-permute-start.11 = (bf16[128,2560]{1,0:T(8,128)(2,1)}, bf16[128,2560]{1,0:T(8,128)(2,1)}, u32[]{:S(2)}, u32[]{:S(2)}) collective-permute-start(bf16[128,2560]{1,0:T(8,128)(2,1)} %get-tuple-element.51), channel_id=1, source_target_pairs={{0,16},{4,20},{8,24},{12,28},{16,0},{20,4},{24,8},{28,12},{1,17},{... | collective-permute-start | bytes 1966088 | tf_op jit(solution)/shard_map/ppermute | solution.py:38
  93.6 30.9 %collective-permute-start.12 = (bf16[128,2560]{1,0:T(8,128)(2,1)}, bf16[128,2560]{1,0:T(8,128)(2,1)}, u32[]{:S(2)}, u32[]{:S(2)}) collective-permute-start(bf16[128,2560]{1,0:T(8,128)(2,1)} %get-tuple-element.52), channel_id=1, source_target_pairs={{0,20},{4,16},{8,28},{12,24},{16,4},{20,0},{24,12},{28,8},{1,21},{... | collective-permute-start | bytes 1966088 | tf_op jit(solution)/shard_map/ppermute | solution.py:38
  96.1 80.1 %collective-permute-start.25 = (bf16[320,3072]{1,0:T(8,128)(2,1)S(1)}, bf16[320,3072]{1,0:T(8,128)(2,1)S(1)}, u32[]{:S(2)}, u32[]{:S(2)}) collective-permute-start(bf16[320,3072]{1,0:T(8,128)(2,1)S(1)} %pad_maximum_fusion.refs_1_.refs_2_), channel_id=1, source_target_pairs={{0,4},{4,0},{8,12},{12,8},{16,20},{20,16},{24,28},{28,24},{1,5},{5... | collective-permute-start | bytes 5898248 | tf_op jit(solution)/shard_map/ppermute | solution.py:38
  107.1 48.1 %collective-permute-start.7 = (bf16[128,2560]{1,0:T(8,128)(2,1)}, bf16[128,2560]{1,0:T(8,128)(2,1)}, u32[]{:S(2)}, u32[]{:S(2)}) collective-permute-start(bf16[128,2560]{1,0:T(8,128)(2,1)} %get-tuple-element.46), channel_id=1, source_target_pairs={{0,4},{4,0},{8,12},{12,8},{16,20},{20,16},{24,28},{28,24},{1,5},{5... | collective-permute-start | bytes 1966088 | tf_op jit(solution)/shard_map/ppermute | solution.py:38
  118.2 20.4 %collective-permute-start.21 = (bf16[128,2560]{1,0:T(8,128)(2,1)S(1)}, bf16[128,2560]{1,0:T(8,128)(2,1)}, u32[]{:S(2)}, u32[]{:S(2)}) collective-permute-start(bf16[128,2560]{1,0:T(8,128)(2,1)S(1)} %pad_maximum_fusion.1.refs_0_), channel_id=1, source_target_pairs={{0,1},{1,0},{2,3},{3,2},{4,5},{5,4},{6,7},{7,6},{8,9},{9,8},{10,11... | collective-permute-start | bytes 1966088 | tf_op jit(solution)/shard_map/ppermute | solution.py:38
  119.9 30.7 %collective-permute-start.29 = (bf16[320,1536]{1,0:T(8,128)(2,1)S(1)}, bf16[320,1536]{1,0:T(8,128)(2,1)}, u32[]{:S(2)}, u32[]{:S(2)}) collective-permute-start(bf16[320,1536]{1,0:T(8,128)(2,1)S(1)} %slice.29), channel_id=1, source_target_pairs={{0,16},{4,20},{8,24},{12,28},{16,0},{20,4},{24,8},{28,12},{1,17},{... | collective-permute-start | bytes 2949128 | tf_op jit(solution)/shard_map/ppermute | solution.py:38
  124.6 23.2 %collective-permute-start.28 = (bf16[320,1536]{1,0:T(8,128)(2,1)}, bf16[320,1536]{1,0:T(8,128)(2,1)}, u32[]{:S(2)}, u32[]{:S(2)}) collective-permute-start(bf16[320,1536]{1,0:T(8,128)(2,1)} %slice.28), channel_id=1, source_target_pairs={{0,8},{4,12},{8,0},{12,4},{16,24},{20,28},{24,16},{28,20},{1,9},{5... | collective-permute-start | bytes 2949128 | tf_op jit(solution)/shard_map/ppermute | solution.py:38
  138.6 51.7 %collective-permute-start.27 = (bf16[320,3072]{1,0:T(8,128)(2,1)}, bf16[320,3072]{1,0:T(8,128)(2,1)S(1)}, u32[]{:S(2)}, u32[]{:S(2)}) collective-permute-start(bf16[320,3072]{1,0:T(8,128)(2,1)} %collective-permute-done.20.refs_5_.refs_6_), channel_id=1, source_target_pairs={{0,4},{4,0},{8,12},{12,8},{16,20},{20,16},{24,28},{28,24},{1,5},{5... | collective-permute-start | bytes 5898248 | tf_op jit(solution)/shard_map/ppermute | solution.py:38
  147.8 44.0 %collective-permute-start.26 = (bf16[320,3072]{1,0:T(8,128)(2,1)}, bf16[320,3072]{1,0:T(8,128)(2,1)}, u32[]{:S(2)}, u32[]{:S(2)}) collective-permute-start(bf16[320,3072]{1,0:T(8,128)(2,1)} %collective-permute-done.19.refs_3_.refs_4_), channel_id=1, source_target_pairs={{0,4},{4,0},{8,12},{12,8},{16,20},{20,16},{24,28},{28,24},{1,5},{5... | collective-permute-start | bytes 5898248 | tf_op jit(solution)/shard_map/ppermute | solution.py:38
  150.6 13.8 %collective-permute-start.40 = (bf16[128,1024]{1,0:T(8,128)(2,1)S(1)}, bf16[128,1024]{1,0:T(8,128)(2,1)S(1)}, u32[]{:S(2)}, u32[]{:S(2)}) collective-permute-start(bf16[128,1024]{1,0:T(8,128)(2,1)S(1)} %copy-done.38), channel_id=1, source_target_pairs={{0,1},{1,0},{2,3},{3,2},{4,5},{5,4},{6,7},{7,6},{8,9},{9,8},{10,11... | collective-permute-start | bytes 786440 | tf_op jit(solution)/shard_map/ppermute | solution.py:38
  155.2 52.7 %collective-permute-start.30 = (bf16[320,3072]{1,0:T(8,128)(2,1)}, bf16[320,3072]{1,0:T(8,128)(2,1)}, u32[]{:S(2)}, u32[]{:S(2)}) collective-permute-start(bf16[320,3072]{1,0:T(8,128)(2,1)} %constant_dynamic-update-slice_fusion.refs_8_), channel_id=1, source_target_pairs={{0,4},{4,0},{8,12},{12,8},{16,20},{20,16},{24,28},{28,24},{1,5},{5... | collective-permute-start | bytes 5898248 | tf_op jit(solution)/shard_map/ppermute | solution.py:38
  164.5 11.6 %collective-permute-start.22 = (bf16[128,1536]{1,0:T(8,128)(2,1)S(1)}, bf16[128,1536]{1,0:T(8,128)(2,1)S(1)}, u32[]{:S(2)}, u32[]{:S(2)}) collective-permute-start(bf16[128,1536]{1,0:T(8,128)(2,1)S(1)} %copy-done.35), channel_id=1, source_target_pairs={{0,1},{1,0},{2,3},{3,2},{4,5},{5,4},{6,7},{7,6},{8,9},{9,8},{10,11... | collective-permute-start | bytes 1179656 | tf_op jit(solution)/shard_map/ppermute | solution.py:38
  176.1 1.7 collective-permute-start.35
  176.2 9.2 %collective-permute-start.36 = (bf16[128,1024]{1,0:T(8,128)(2,1)S(1)}, bf16[128,1024]{1,0:T(8,128)(2,1)S(1)}, u32[]{:S(2)}, u32[]{:S(2)}) collective-permute-start(bf16[128,1024]{1,0:T(8,128)(2,1)S(1)} %copy-done.37), channel_id=1, source_target_pairs={{0,8},{4,12},{8,0},{12,4},{16,24},{20,28},{24,16},{28,20},{1,9},{5... | collective-permute-start | bytes 786440 | tf_op jit(solution)/shard_map/ppermute | solution.py:38
  177.8 12.3 %collective-permute-start.37 = (bf16[128,1024]{1,0:T(8,128)(2,1)S(1)}, bf16[128,1024]{1,0:T(8,128)(2,1)S(1)}, u32[]{:S(2)}, u32[]{:S(2)}) collective-permute-start(bf16[128,1024]{1,0:T(8,128)(2,1)S(1)} %copy-done.36), channel_id=1, source_target_pairs={{0,12},{4,8},{8,4},{12,0},{16,28},{20,24},{24,20},{28,16},{1,13},{... | collective-permute-start | bytes 786440 | tf_op jit(solution)/shard_map/ppermute | solution.py:38
  185.5 18.8 %collective-permute-start.38 = (bf16[128,1024]{1,0:T(8,128)(2,1)}, bf16[128,1024]{1,0:T(8,128)(2,1)S(1)}, u32[]{:S(2)}, u32[]{:S(2)}) collective-permute-start(bf16[128,1024]{1,0:T(8,128)(2,1)} %get-tuple-element.73), channel_id=1, source_target_pairs={{0,16},{4,20},{8,24},{12,28},{16,0},{20,4},{24,8},{28,12},{1,17},{... | collective-permute-start | bytes 786440 | tf_op jit(solution)/shard_map/ppermute | solution.py:38
  190.1 14.2 %collective-permute-start.39 = (bf16[128,1024]{1,0:T(8,128)(2,1)}, bf16[128,1024]{1,0:T(8,128)(2,1)S(1)}, u32[]{:S(2)}, u32[]{:S(2)}) collective-permute-start(bf16[128,1024]{1,0:T(8,128)(2,1)} %get-tuple-element.74), channel_id=1, source_target_pairs={{0,20},{4,16},{8,28},{12,24},{16,4},{20,0},{24,12},{28,8},{1,21},{... | collective-permute-start | bytes 786440 | tf_op jit(solution)/shard_map/ppermute | solution.py:38
  190.3 14.7 %collective-permute-start.42 = (bf16[64,1024]{1,0:T(8,128)(2,1)S(1)}, bf16[64,1024]{1,0:T(8,128)(2,1)S(1)}, u32[]{:S(2)}, u32[]{:S(2)}) collective-permute-start(bf16[64,1024]{1,0:T(8,128)(2,1)S(1)} %get-tuple-element.87), channel_id=1, source_target_pairs={{0,28},{4,24},{8,20},{12,16},{16,12},{20,8},{24,4},{28,0},{1,29},{... | collective-permute-start | bytes 393224 | tf_op jit(solution)/shard_map/ppermute | solution.py:38
  191.9 14.5 %collective-permute-start.41 = (bf16[64,1024]{1,0:T(8,128)(2,1)S(1)}, bf16[64,1024]{1,0:T(8,128)(2,1)S(1)}, u32[]{:S(2)}, u32[]{:S(2)}) collective-permute-start(bf16[64,1024]{1,0:T(8,128)(2,1)S(1)} %get-tuple-element.88), channel_id=1, source_target_pairs={{0,24},{4,28},{8,16},{12,20},{16,8},{20,12},{24,0},{28,4},{1,25},{... | collective-permute-start | bytes 393224 | tf_op jit(solution)/shard_map/ppermute | solution.py:38
  204.3 19.2 %collective-permute-start.8 = (bf16[128,1536]{1,0:T(8,128)(2,1)S(1)}, bf16[128,1536]{1,0:T(8,128)(2,1)S(1)}, u32[]{:S(2)}, u32[]{:S(2)}) collective-permute-start(bf16[128,1536]{1,0:T(8,128)(2,1)S(1)} %copy-done.34), channel_id=1, source_target_pairs={{0,4},{4,0},{8,12},{12,8},{16,20},{20,16},{24,28},{28,24},{1,5},{5... | collective-permute-start | bytes 1179656 | tf_op jit(solution)/shard_map/ppermute | solution.py:38
  204.4 20.6 %collective-permute-start.13 = (bf16[128,1536]{1,0:T(8,128)(2,1)S(1)}, bf16[128,1536]{1,0:T(8,128)(2,1)S(1)}, u32[]{:S(2)}, u32[]{:S(2)}) collective-permute-start(bf16[128,1536]{1,0:T(8,128)(2,1)S(1)} %copy-done.33), channel_id=1, source_target_pairs={{0,8},{4,12},{8,0},{12,4},{16,24},{20,28},{24,16},{28,20},{1,9},{5... | collective-permute-start | bytes 1179656 | tf_op jit(solution)/shard_map/ppermute | solution.py:38
  205.1 22.5 %collective-permute-start.14 = (bf16[128,1536]{1,0:T(8,128)(2,1)S(1)}, bf16[128,1536]{1,0:T(8,128)(2,1)S(1)}, u32[]{:S(2)}, u32[]{:S(2)}) collective-permute-start(bf16[128,1536]{1,0:T(8,128)(2,1)S(1)} %copy-done.32), channel_id=1, source_target_pairs={{0,12},{4,8},{8,4},{12,0},{16,28},{20,24},{24,20},{28,16},{1,13},{... | collective-permute-start | bytes 1179656 | tf_op jit(solution)/shard_map/ppermute | solution.py:38
  206.4 23.8 %collective-permute-start.15 = (bf16[128,1536]{1,0:T(8,128)(2,1)S(1)}, bf16[128,1536]{1,0:T(8,128)(2,1)S(1)}, u32[]{:S(2)}, u32[]{:S(2)}) collective-permute-start(bf16[128,1536]{1,0:T(8,128)(2,1)S(1)} %copy-done.31), channel_id=1, source_target_pairs={{0,16},{4,20},{8,24},{12,28},{16,0},{20,4},{24,8},{28,12},{1,17},{... | collective-permute-start | bytes 1179656 | tf_op jit(solution)/shard_map/ppermute | solution.py:38
  208.0 22.2 %collective-permute-start.16 = (bf16[128,1536]{1,0:T(8,128)(2,1)S(1)}, bf16[128,1536]{1,0:T(8,128)(2,1)S(1)}, u32[]{:S(2)}, u32[]{:S(2)}) collective-permute-start(bf16[128,1536]{1,0:T(8,128)(2,1)S(1)} %copy-done.30), channel_id=1, source_target_pairs={{0,20},{4,16},{8,28},{12,24},{16,4},{20,0},{24,12},{28,8},{1,21},{... | collective-permute-start | bytes 1179656 | tf_op jit(solution)/shard_map/ppermute | solution.py:38
  223.5 7.7 %collective-permute-start.24 = (bf16[64,1536]{1,0:T(8,128)(2,1)S(1)}, bf16[64,1536]{1,0:T(8,128)(2,1)S(1)}, u32[]{:S(2)}, u32[]{:S(2)}) collective-permute-start(bf16[64,1536]{1,0:T(8,128)(2,1)S(1)} %get-tuple-element.85), channel_id=1, source_target_pairs={{0,28},{4,24},{8,20},{12,16},{16,12},{20,8},{24,4},{28,0},{1,29},{... | collective-permute-start | bytes 589832 | tf_op jit(solution)/shard_map/ppermute | solution.py:38
  225.0 10.9 %collective-permute-start.23 = (bf16[64,1536]{1,0:T(8,128)(2,1)S(1)}, bf16[64,1536]{1,0:T(8,128)(2,1)S(1)}, u32[]{:S(2)}, u32[]{:S(2)}) collective-permute-start(bf16[64,1536]{1,0:T(8,128)(2,1)S(1)} %get-tuple-element.86), channel_id=1, source_target_pairs={{0,24},{4,28},{8,16},{12,20},{16,8},{20,12},{24,0},{28,4},{1,25},{... | collective-permute-start | bytes 589832 | tf_op jit(solution)/shard_map/ppermute | solution.py:38
  227.6 26.0 %collective-permute-start.43 = (bf16[128,1024]{1,0:T(8,128)(2,1)S(1)}, bf16[128,1024]{1,0:T(8,128)(2,1)S(1)}, u32[]{:S(2)}, u32[]{:S(2)}) collective-permute-start(bf16[128,1024]{1,0:T(8,128)(2,1)S(1)} %get-tuple-element.84), channel_id=1, source_target_pairs={{0,1},{3,2},{4,5},{7,6},{8,9},{11,10},{12,13},{15,14},{16,17},{19,... | collective-permute-start | bytes 786440 | tf_op jit(solution)/shard_map/ppermute | solution.py:79
  244.2 12.3 %collective-permute-start.31 = (bf16[128,1536]{1,0:T(8,128)(2,1)S(1)}, bf16[128,1536]{1,0:T(8,128)(2,1)S(1)}, u32[]{:S(2)}, u32[]{:S(2)}) collective-permute-start(bf16[128,1536]{1,0:T(8,128)(2,1)S(1)} %get-tuple-element.82), channel_id=1, source_target_pairs={{0,1},{3,2},{4,5},{7,6},{8,9},{11,10},{12,13},{15,14},{16,17},{19,... | collective-permute-start | bytes 1179656 | tf_op jit(solution)/shard_map/ppermute | solution.py:79
  247.1 20.1 %collective-permute-start.46 = (bf16[128,1024]{1,0:T(8,128)(2,1)S(1)}, bf16[128,1024]{1,0:T(8,128)(2,1)S(1)}, u32[]{:S(2)}, u32[]{:S(2)}) collective-permute-start(bf16[128,1024]{1,0:T(8,128)(2,1)S(1)} %get-tuple-element.84), channel_id=1, source_target_pairs={{1,2},{2,1},{5,6},{6,5},{9,10},{10,9},{13,14},{14,13},{17,18},{18,... | collective-permute-start | bytes 786440 | tf_op jit(solution)/shard_map/ppermute | solution.py:80
  247.8 28.7 %collective-permute-start.34 = (bf16[128,1536]{1,0:T(8,128)(2,1)S(1)}, bf16[128,1536]{1,0:T(8,128)(2,1)S(1)}, u32[]{:S(2)}, u32[]{:S(2)}) collective-permute-start(bf16[128,1536]{1,0:T(8,128)(2,1)S(1)} %get-tuple-element.82), channel_id=1, source_target_pairs={{1,2},{2,1},{5,6},{6,5},{9,10},{10,9},{13,14},{14,13},{17,18},{18,... | collective-permute-start | bytes 1179656 | tf_op jit(solution)/shard_map/ppermute | solution.py:80
  248.5 13.7 %collective-permute-start.45 = (bf16[128,1024]{1,0:T(8,128)(2,1)S(1)}, bf16[128,1024]{1,0:T(8,128)(2,1)S(1)}, u32[]{:S(2)}, u32[]{:S(2)}) collective-permute-start(bf16[128,1024]{1,0:T(8,128)(2,1)S(1)} %get-tuple-element.83), channel_id=1, source_target_pairs={{0,1},{1,0},{2,3},{3,2},{4,5},{5,4},{6,7},{7,6},{8,9},{9,8},{10,11... | collective-permute-start | bytes 786440 | tf_op jit(solution)/shard_map/ppermute | solution.py:38
  253.5 22.9 %collective-permute-start.33 = (bf16[128,1536]{1,0:T(8,128)(2,1)S(1)}, bf16[128,1536]{1,0:T(8,128)(2,1)S(1)}, u32[]{:S(2)}, u32[]{:S(2)}) collective-permute-start(bf16[128,1536]{1,0:T(8,128)(2,1)S(1)} %get-tuple-element.81), channel_id=1, source_target_pairs={{0,1},{1,0},{2,3},{3,2},{4,5},{5,4},{6,7},{7,6},{8,9},{9,8},{10,11... | collective-permute-start | bytes 1179656 | tf_op jit(solution)/shard_map/ppermute | solution.py:38
  256.6 19.7 %collective-permute-start.44 = (bf16[128,1024]{1,0:T(8,128)(2,1)S(1)}, bf16[128,1024]{1,0:T(8,128)(2,1)S(1)}, u32[]{:S(2)}, u32[]{:S(2)}) collective-permute-start(bf16[128,1024]{1,0:T(8,128)(2,1)S(1)} %add_convert_fusion.4), channel_id=1, source_target_pairs={{0,2},{1,3},{2,0},{3,1},{4,6},{5,7},{6,4},{7,5},{8,10},{9,11},{10,... | collective-permute-start | bytes 786440 | tf_op jit(solution)/shard_map/ppermute | solution.py:43
  262.2 31.4 %collective-permute-start.32 = (bf16[128,1536]{1,0:T(8,128)(2,1)S(1)}, bf16[128,1536]{1,0:T(8,128)(2,1)S(1)}, u32[]{:S(2)}, u32[]{:S(2)}) collective-permute-start(bf16[128,1536]{1,0:T(8,128)(2,1)S(1)} %add_convert_fusion.1), channel_id=1, source_target_pairs={{0,2},{1,3},{2,0},{3,1},{4,6},{5,7},{6,4},{7,5},{8,10},{9,11},{10,... | collective-permute-start | bytes 1179656 | tf_op jit(solution)/shard_map/ppermute | solution.py:43
  (39 other events, 542.5 us)
